TPU v7x, 256 devices: a whole 4x4x8 slice. The times are simulated.
256 devices in a mesh: dp: 16 (over z, y_lo), seq: 16 (over y_hi, x, core).
Axes of the slice: x: 4, y: 4 (y_hi: 2, y_lo: 2; y = y_hi * 2 + y_lo), z: 8, core: 2. Of those that a mesh axis runs over, the one named last changes fastest.
Arguments:
- trunk_acts: bfloat16 [16, 16384, 768], P('dp', 'seq'), may hold values from -6 to 6
- base_ids: int32 [16, 16384], P('dp', 'seq'), may hold values from 0 to 3
- base_table: float32 [4, 768], replicated, may hold values from -6 to 6
- norm_gain: float32 [768], replicated, may hold values from 0.1 to 1.9
- conv_weight: bfloat16 [768, 3, 768], replicated, may hold values from -0.125 to 0.125
- grad_out: bfloat16 [16, 16384, 768], P('dp', 'seq'), may hold values from -6 to 6
- donor_pos: int32 [16, 32768], P('dp', 'seq'), may hold values from 0 to 1023
- accept_pos: int32 [16, 32768], P('dp', 'seq'), may hold values from 0 to 1023
- pair_counts: int32 [16, 256], P('dp', 'seq'), may hold values from 1 to 128, as said below
- donor_weight: bfloat16 [768, 768], replicated, may hold values from -0.21875 to 0.21875
- accept_weight: bfloat16 [768, 768], replicated, may hold values from -0.21875 to 0.21875
Outputs:
- junction_pairs: bfloat16 [16, 32768, 768], P('dp', 'seq')
- weight_grad: float32 [768, 3, 768], P('seq', None, 'dp')
Inputs may be any that keep to these rules, and one draw needn't show every extreme that they name: `pair_counts`: for every interval one acceptor owner has all 128 slots valid from every sender; the other counts lie from 1 to 64.
All inputs are finite; a program needn't handle non-finite values.
Results may differ from a plain program's by a relative error of at most 0.0067.
Values may be sent and summed in bfloat16 or wider, within the bound.
No kernel may reach another device: no remote copies, remote signals or barrier semaphores. Data moves between devices by JAX's collectives and lax.ppermute only.
A program may use at most 128 MiB of HBM per device.

v0:
```python
import jax
import jax.numpy as jnp
from jax import lax
from jax.sharding import PartitionSpec as P

DILATION_STEP = 256


def with_halo(block, sides, width):
    for axis, dim in sides:
        count = lax.axis_size(axis)
        forward = [(i, i + 1) for i in range(count - 1)]
        backward = [(target, source) for source, target in forward]
        low = lax.ppermute(
            lax.slice_in_dim(block, block.shape[dim] - width, None, axis=dim), axis, forward
        )
        high = lax.ppermute(lax.slice_in_dim(block, 0, width, axis=dim), axis, backward)
        block = jnp.concatenate([low, block, high], axis=dim)
    return block


def rms_normed(inputs, norm_gain):
    scale = lax.rsqrt(jnp.mean(inputs * inputs, axis=-1, keepdims=True) + 1e-06)
    return (inputs * scale * norm_gain).astype(jnp.bfloat16)


def on_device(
    trunk_acts,
    base_ids,
    base_table,
    norm_gain,
    conv_weight,
    grad_out,
    donor_pos,
    accept_pos,
    pair_counts,
    donor_weight,
    accept_weight,
):
    seq_count = lax.axis_size("seq")
    trunk = trunk_acts[0]
    sequence_length = trunk.shape[0]
    width = trunk.shape[1]
    kernel_taps = conv_weight.shape[1]
    onehot = (base_ids[0][:, None] == jnp.arange(4)[None, :]).astype(jnp.float32)
    inputs = trunk.astype(jnp.float32) + jnp.dot(
        onehot, base_table, precision=lax.Precision.HIGHEST
    )
    normalized_rows = rms_normed(inputs, norm_gain)
    padded_input = with_halo(normalized_rows, (("seq", 0),), DILATION_STEP * (kernel_taps // 2))
    sliding_windows = [
        padded_input[kernel_tap * DILATION_STEP : kernel_tap * DILATION_STEP + sequence_length]
        for kernel_tap in range(kernel_taps)
    ]
    conv_out = jnp.zeros((sequence_length, width), jnp.float32)
    for kernel_tap in range(kernel_taps):
        conv_out = conv_out + jnp.dot(
            sliding_windows[kernel_tap],
            conv_weight[:, kernel_tap, :],
            preferred_element_type=jnp.float32,
        )
    hidden = (inputs + jax.nn.gelu(conv_out)).astype(jnp.bfloat16)
    _, pull_back = jax.vjp(jax.nn.gelu, conv_out)
    dconv = pull_back(grad_out[0].astype(jnp.float32))[0].astype(jnp.bfloat16)
    slot_table = accept_pos[0].reshape(seq_count, -1)
    accept_local = jnp.dot(hidden, accept_weight, preferred_element_type=jnp.float32).astype(
        jnp.bfloat16
    )
    slot_block = lax.all_to_all(slot_table, "seq", split_axis=0, concat_axis=0, tiled=True)
    senders, per_item = slot_block.shape
    picked = jnp.take(accept_local, slot_block.reshape(-1), axis=0).reshape(
        senders, per_item, width
    )
    accepted = lax.all_to_all(picked, "seq", split_axis=0, concat_axis=0, tiled=True).reshape(
        -1, width
    )
    donor_all = jnp.dot(hidden, donor_weight, preferred_element_type=jnp.float32)
    donor_emb = jnp.take(donor_all, donor_pos[0], axis=0)
    slot_cap = slot_table.shape[1]
    valid = (jnp.arange(slot_cap)[None, :] < pair_counts[0][:, None]).reshape(-1)
    junction_pairs = jnp.where(
        valid[:, None], donor_emb * accepted.astype(jnp.float32), 0.0
    ).astype(jnp.bfloat16)[None]
    local_grad = lax.psum_scatter(
        jnp.stack(
            [
                lax.dot_general(
                    win, dconv, (((0,), (0,)), ((), ())), preferred_element_type=jnp.float32
                )
                for win in sliding_windows
            ],
            axis=1,
        ),
        "seq",
        scatter_dimension=0,
        tiled=True,
    )
    weight_grad = lax.psum_scatter(local_grad, "dp", scatter_dimension=2, tiled=True)
    return (junction_pairs, weight_grad)


def solution(mesh):
    return jax.shard_map(
        on_device,
        mesh=mesh,
        in_specs=(
            P("dp", "seq", None),
            P("dp", "seq"),
            P(),
            P(),
            P(),
            P("dp", "seq", None),
            P("dp", "seq"),
            P("dp", "seq"),
            P("dp", "seq"),
            P(),
            P(),
        ),
        out_specs=(P("dp", "seq", None), P("seq", None, "dp")),
        check_vma=False,
    )
```

profile of v0, /device:TPU:2, one launch (start us, length us, event | category | flops | bytes accessed | tf_op | source)
XLA Modules:
  0.0 251.6 jit_solution(14156816245573865570)
XLA Ops:
  7.2 0.0 copy-start
  7.2 0.0 copy-start.3
  7.2 0.0 reduce-scatter.5.cloned.1.call-start
  7.2 3.3 %multiply_reduce_fusion = (f32[1024]{0:T(1024)S(1)}, f32[1024,768]{1,0:T(8,128)S(1)}) fusion(f32[4,768]{1,0:T(4,128)} %param.13, s32[1024]{0:T(1024)} %bitcast.68, bf16[1,1024,768]{2,1,0:T(8,128)(2,1)} %param.11), kind=kOutput, calls=%fused_computation.25 | convolution fusion | flops 40897536 | bytes 4739072 | tf_op jit(solution)/shard_map/dot_general | solution.py:46
  10.5 0.0 copy-done.3
  10.5 0.0 copy-start.5
  10.5 0.3 multiply_convert_fusion
  10.9 0.1 fusion.29
  10.9 2.1 collective-permute-start
  13.0 3.6 %collective-permute-start.1 = (bf16[256,768]{1,0:T(8,128)(2,1)S(1)}, bf16[256,768]{1,0:T(8,128)(2,1)S(1)}, u32[]{:S(2)}, u32[]{:S(2)}) collective-permute-start(bf16[256,768]{1,0:T(8,128)(2,1)S(1)} %get-tuple-element.4), channel_id=1, source_target_pairs={{1,0},{2,1},{3,2},{4,3},{5,4},{6,5},{7,6},{8,7},{9,8},{10,9},{11,1... | collective-permute-start | bytes 1179656 | tf_op jit(solution)/shard_map/ppermute | solution.py:17
  16.6 0.0 copy-done.5
  16.7 1.4 fusion.16
  18.1 0.0 copy-start.6
  18.1 2.1 collective-permute-done
  20.2 1.4 fusion.18
  21.6 0.4 collective-permute-done.1
  21.9 0.0 copy-done.6
  21.9 5.2 %fusion.4 = (bf16[1024,768]{1,0:T(8,128)(2,1)S(1)}, bf16[1024,768]{1,0:T(8,128)(2,1)}) fusion(bf16[1,1024,768]{2,1,0:T(8,128)(2,1)S(1)} %copy-done.6, f32[1024,768]{1,0:T(8,128)S(1)} %get-tuple-element.7, bf16[768,3,768]{2,0,1:T(8,128)(2,1)S(1)} %copy-done.5, bf16[256,768]{1,0:T(8,128)(2,1)S(1)} %collective-permute-done.1, ...), kind=kOutput, calls=%fused_computation.13 | convolution fusion | flops 1231552512 | bytes 17301504 | tf_op jit(solution)/shard_map/dot_general | solution.py:57
  27.1 1.5 convolution_bitcast_fusion.1
  28.6 1.5 convolution_bitcast_fusion
  30.0 1.5 convolution_bitcast_fusion.2
  31.5 3.4 %pad_maximum_fusion = f32[768,3,768]{2,0,1:T(8,128)} fusion(f32[768,1,768]{2,0,1:T(8,128)S(1)} %convolution_bitcast_fusion, f32[768,1,768]{2,0,1:T(8,128)S(1)} %convolution_bitcast_fusion.1, f32[768,1,768]{2,0,1:T(8,128)S(1)} %convolution_bitcast_fusion.2), kind=kLoop, calls=%fused_computation.2 | loop fusion | flops 3538944 | bytes 14155776 | tf_op jit(solution)/shard_map/stack | solution.py:85
  34.9 0.0 copy-start.2
  34.9 0.0 reduce-scatter.5.cloned.1.call-update
  34.9 0.7 copy-done.2
  35.6 17.2 %all_to_all.14 = s32[16,1,128]{2,1,0:T(1,128)S(1)} all-to-all(s32[16,1,128]{2,1,0:T(1,128)S(1)} %bitcast.67), channel_id=1, replica_groups=mesh['dp'=16,'seq'=16] {'seq'}, dimensions={0} | all-to-all | bytes 16384 | tf_op jit(solution)/shard_map/all_to_all | solution.py:69
  52.8 0.0 copy-done
  52.8 2.8 %convolution_convert_fusion = bf16[1024,768]{1,0:T(8,128)(2,1)S(1)} fusion(bf16[1024,768]{1,0:T(8,128)(2,1)} %get-tuple-element.3, bf16[768,768]{1,0:T(8,128)(2,1)S(1)} %copy-done), kind=kOutput, calls=%fused_computation.30 | convolution fusion | flops 1208745984 | bytes 4325376 | tf_op jit(solution)/shard_map/dot_general | solution.py:66
  55.6 9.4 %gather_fusion.1 = bf16[2048,768]{1,0:T(8,128)(2,1)} fusion(bf16[1024,768]{1,0:T(8,128)(2,1)S(1)} %convolution_convert_fusion, s32[2048]{0:T(1024)S(1)} %broadcast_clamp_fusion), kind=kCustom, calls=%fused_computation.1 | custom fusion | bytes 6299648 | tf_op jit(solution)/shard_map/jit(_take)/gather | solution.py:71
  65.0 3.6 %broadcast_select_fusion = bf16[16,128,768]{2,1,0:T(8,128)(2,1)} fusion(bf16[16,128,768]{2,1,0:T(8,128)(2,1)} %bitcast.60, pred[16,128]{1,0:T(8,128)(4,1)S(1)} %compare_and_fusion), kind=kLoop, calls=%fused_computation.26 | loop fusion | flops 1572864 | bytes 6293504 | tf_op jit(solution)/shard_map/jit(_take)/select_n | solution.py:71
  68.6 0.0 copy-start.4
  68.6 0.0 copy-start.1
  68.6 5.9 %all-to-all-start.1 = ((bf16[16,128,768]{2,1,0:T(8,128)(2,1)}), bf16[16,128,768]{2,1,0:T(8,128)(2,1)}, u32[]{:S(2)}, u32[]{:S(2)}) async-start(bf16[16,128,768]{2,1,0:T(8,128)(2,1)} %broadcast_select_fusion), calls=%async_computation.1 | async-start | bytes 6291456 | tf_op jit(solution)/shard_map/all_to_all | solution.py:74
  74.6 0.0 reduce-scatter.7.cloned.1.call-start
  74.6 0.0 copy-done.4
  74.6 0.1 fusion.24
  74.7 0.0 copy-done.1
  74.7 95.0 %reduce-scatter.5.cloned.1.call-done = f32[48,3,768]{2,0,1:T(8,128)} async-done(((f32[768,3,768]{2,0,1:T(8,128)}), f32[48,3,768]{2,0,1:T(8,128)}) %reduce-scatter.5.cloned.1.call-update) | async-done | bytes 442384 | tf_op jit(solution)/shard_map/reduce_scatter | solution.py:84
  169.8 1.6 copy.13
  171.4 1.5 reshape.203
  172.8 0.0 reduce-scatter.7.cloned.1.call-update
  172.9 4.8 %fusion.30 = f32[1024,768]{1,0:T(8,128)} fusion(bf16[1024,768]{1,0:T(8,128)(2,1)} %get-tuple-element.3, bf16[768,768]{1,0:T(8,128)(2,1)} %param.20), kind=kOutput, calls=%fused_computation.60 | convolution fusion | flops 1207959552 | bytes 5898240 | tf_op jit(solution)/shard_map/dot_general | solution.py:77
  177.7 12.5 %gather_fusion = f32[2048,768]{1,0:T(8,128)} fusion(f32[1024,768]{1,0:T(8,128)} %fusion.30, s32[2048]{0:T(1024)S(1)} %broadcast_clamp_fusion.1), kind=kCustom, calls=%fused_computation | custom fusion | bytes 12591104 | tf_op jit(solution)/shard_map/jit(_take)/gather | solution.py:78
  190.2 0.0 all-to-all-done.1
  190.2 5.5 %fusion.1 = bf16[1,2048,768]{2,1,0:T(8,128)(2,1)} fusion(f32[2048,768]{1,0:T(8,128)} %gather_fusion, pred[2048]{0:T(1024)(128)(4,1)S(1)} %compare_and_fusion.1, pred[2048]{0:T(1024)(128)(4,1)S(1)} %fusion.24, bf16[1,2048,768]{2,1,0:T(8,128)(2,1)} %bitcast.59), kind=kLoop, calls=%fused_computation.5 | loop fusion | flops 7864320 | bytes 12587008 | tf_op jit(solution)/shard_map/convert_element_type | solution.py:83
  195.7 47.5 %reduce-scatter.7.cloned.1.call-done = f32[48,144]{1,0:T(8,128)} async-done(((f32[768,144]{1,0:T(8,128)}), f32[48,144]{1,0:T(8,128)}) %reduce-scatter.7.cloned.1.call-update) | async-done | bytes 27664
  243.1 0.9 reshape.204
  244.0 0.7 copy.14
  (7 shorter events, 0.1 us)
Async XLA Ops:
  7.2 45.6 %copy-start = (bf16[768,768]{1,0:T(8,128)(2,1)S(1)}, bf16[768,768]{1,0:T(8,128)(2,1)}, u32[]{:S(2)}) copy-start(bf16[768,768]{1,0:T(8,128)(2,1)} %param.21) | copy-start | bytes 3538948
  7.2 3.3 %copy-start.3 = (f32[768]{0:T(1024)S(1)}, f32[768]{0:T(1024)}, u32[]{:S(2)}) copy-start(f32[768]{0:T(1024)} %param.14) | copy-start | bytes 9220
  7.2 162.6 %reduce-scatter.5.cloned.1.call-start = ((), (), s32[]{:S(2)}) async-start(), calls=%async_computation.4 | async-start | bytes 7520256 | tf_op jit(solution)/shard_map/reduce_scatter | solution.py:84
  10.5 6.1 %copy-start.5 = (bf16[768,3,768]{2,0,1:T(8,128)(2,1)S(1)}, bf16[768,3,768]{2,0,1:T(8,128)(2,1)}, u32[]{:S(2)}) copy-start(bf16[768,3,768]{2,0,1:T(8,128)(2,1)} %param.15) | copy-start | bytes 10616836
  10.9 9.2 %collective-permute-start = (bf16[256,768]{1,0:T(8,128)(2,1)S(1)}, bf16[256,768]{1,0:T(8,128)(2,1)S(1)}, u32[]{:S(2)}, u32[]{:S(2)}) collective-permute-start(bf16[256,768]{1,0:T(8,128)(2,1)S(1)} %get-tuple-element.5), channel_id=1, source_target_pairs={{0,1},{1,2},{2,3},{3,4},{4,5},{5,6},{6,7},{7,8},{8,9},{9,10},{10,1... | collective-permute-start | bytes 1179656 | tf_op jit(solution)/shard_map/ppermute | solution.py:14
  13.0 8.9 %collective-permute-start.1 = (bf16[256,768]{1,0:T(8,128)(2,1)S(1)}, bf16[256,768]{1,0:T(8,128)(2,1)S(1)}, u32[]{:S(2)}, u32[]{:S(2)}) collective-permute-start(bf16[256,768]{1,0:T(8,128)(2,1)S(1)} %get-tuple-element.4), channel_id=1, source_target_pairs={{1,0},{2,1},{3,2},{4,3},{5,4},{6,5},{7,6},{8,7},{9,8},{10,9},{11,1... | collective-permute-start | bytes 1179656 | tf_op jit(solution)/shard_map/ppermute | solution.py:17
  18.1 3.9 %copy-start.6 = (bf16[1,1024,768]{2,1,0:T(8,128)(2,1)S(1)}, bf16[1,1024,768]{2,1,0:T(8,128)(2,1)}, u32[]{:S(2)}) copy-start(bf16[1,1024,768]{2,1,0:T(8,128)(2,1)} %param.16) | copy-start | bytes 4718596
  34.9 0.7 copy-start.2
  68.6 6.0 %copy-start.4 = (s32[1,16]{1,0:T(1,128)S(1)}, s32[1,16]{1,0:T(1,128)}, u32[]{:S(2)}) copy-start(s32[1,16]{1,0:T(1,128)} %param.19) | copy-start | bytes 196
  68.6 6.1 %copy-start.1 = (s32[1,2048]{1,0:T(1,128)S(1)}, s32[1,2048]{1,0:T(1,128)}, u32[]{:S(2)}) copy-start(s32[1,2048]{1,0:T(1,128)} %param.17) | copy-start | bytes 24580
  68.6 121.5 %all-to-all-start.1 = ((bf16[16,128,768]{2,1,0:T(8,128)(2,1)}), bf16[16,128,768]{2,1,0:T(8,128)(2,1)}, u32[]{:S(2)}, u32[]{:S(2)}) async-start(bf16[16,128,768]{2,1,0:T(8,128)(2,1)} %broadcast_select_fusion), calls=%async_computation.1 | async-start | bytes 6291456 | tf_op jit(solution)/shard_map/all_to_all | solution.py:74
  74.6 168.6 %reduce-scatter.7.cloned.1.call-start = ((), (), s32[]{:S(2)}) async-start(), calls=%async_computation.5 | async-start | bytes 835584
Sparse Core Ops, SparseCore 0:
  35.0 134.6 reduce-scatter.4
  173.0 70.0 reduce-scatter.6
where the time goes:
time: 252 us
  waiting for transfers between devices  145 us (58%)
  local copies, waits for them, and re-layouts  27.4 us (11%)
  matrix products  23.2 us (9%)
  blocking collectives  17.2 us (7%)
  between operations  14.2 us (6%)
  other arithmetic  12.9 us (5%)
  starting transfers between devices  11.7 us (5%)
    reduce_scatter x1, waiting for transfers between devices, on_device(): lax.psum_scatter(jnp.stack([lax.dot_general(win, dconv, (((0,), (0,)), ((...  95 us
    unnamed x3, waiting for transfers between devices  47.5 us
    all_to_all x1, blocking collectives, on_device(): lax.all_to_all(slot_table, 'seq', split_axis=0, concat_axis=0, tiled=True)  17.2 us
    gather x1, local copies, waits for them, and re-layouts, on_device(): donor_emb = jnp.take(donor_all, donor_pos[0], axis=0)  12.5 us
    gather x1, local copies, waits for them, and re-layouts, on_device(): jnp.take(accept_local, slot_block.reshape(-1), axis=0)  9.4 us
    dot_general x3, matrix products, on_device(): jnp.dot(sliding_windows[kernel_tap], conv_weight[:, kernel_tap, :], prefe...  7.96 us
    all_to_all x1, starting transfers between devices, on_device(): lax.all_to_all(picked, 'seq', split_axis=0, concat_axis=0, tiled=True)  5.93 us
    convert_element_type x1, other arithmetic, on_device(): junction_pairs = jnp.where(valid[:, None], donor_emb * accepted.astype(jn...  5.49 us
  transfers between devices with their start and end apart: 5, of which 4 were waited for; matrix products, arithmetic and copies ran while one was open for 18% of the time, Pallas kernels for 0%

commit v1 on v0

v1 whole, which is shorter than its diff:
```python
import jax
import jax.numpy as jnp
from jax import lax
from jax.sharding import Mesh, PartitionSpec as P

DILATION_STEP = 256
AXES = ("z", "yl", "yh", "x", "core")
DP = ("z", "yl")
SEQ = ("yh", "x", "core")


def halos(block, width):
    count = lax.axis_size(SEQ)
    forward = [(i, i + 1) for i in range(count - 1)]
    backward = [(target, source) for source, target in forward]
    low = lax.ppermute(block[block.shape[0] - width :], SEQ, forward)
    high = lax.ppermute(block[:width], SEQ, backward)
    return low, high


def rms_normed(inputs, norm_gain):
    scale = lax.rsqrt(jnp.mean(inputs * inputs, axis=-1, keepdims=True) + 1e-06)
    return (inputs * scale * norm_gain).astype(jnp.bfloat16)


def picked_rows(table, index):
    onehot = (index[:, None] == jnp.arange(table.shape[0])[None, :]).astype(table.dtype)
    return jnp.dot(onehot, table, preferred_element_type=jnp.float32).astype(table.dtype)


def reduced_grad(windows, dconv):
    width = dconv.shape[1]
    core = lax.axis_index("core")
    seq_count = lax.axis_size(SEQ)
    dp_count = lax.axis_size(DP)
    chips = seq_count // 2
    rows, cols = width // seq_count, width // dp_count
    taps = len(windows)
    grad = jnp.stack(
        [
            lax.dot_general(win, dconv, (((0,), (0,)), ((), ())), preferred_element_type=jnp.float32)
            for win in windows
        ],
        axis=0,
    ).reshape(taps, chips, 2, rows, width)
    sent = lax.dynamic_index_in_dim(grad, 1 - core, 2, keepdims=False).astype(jnp.bfloat16)
    kept = lax.dynamic_index_in_dim(grad, core, 2, keepdims=False)
    other = lax.ppermute(sent, "core", [(0, 1), (1, 0)])
    chip_sum = (kept + other.astype(jnp.float32)).astype(jnp.bfloat16)
    pieces = jnp.transpose(chip_sum, (1, 0, 2, 3)).reshape(chips, taps * rows, width)
    pieces = lax.all_to_all(pieces, ("yh", "x"), 0, 0, tiled=True)
    own = jnp.sum(pieces.astype(jnp.float32), axis=0).astype(jnp.bfloat16)
    turned = own.T.reshape(dp_count, cols, taps * rows)
    turned = lax.all_to_all(turned, DP, 0, 0, tiled=True)
    total = jnp.sum(turned.astype(jnp.float32), axis=0)
    return jnp.transpose(total.reshape(cols, taps, rows), (2, 1, 0))


def on_device(
    trunk_acts,
    base_ids,
    base_table,
    norm_gain,
    conv_weight,
    grad_out,
    donor_pos,
    accept_pos,
    pair_counts,
    donor_weight,
    accept_weight,
):
    seq_count = lax.axis_size(SEQ)
    trunk = trunk_acts[0]
    length, width = trunk.shape
    slot_block = lax.all_to_all(accept_pos[0].reshape(seq_count, -1), SEQ, 0, 0, tiled=True)
    ids = base_ids[0][:, None]
    embedded = jnp.where(
        ids < 2,
        jnp.where(ids == 0, base_table[0:1], base_table[1:2]),
        jnp.where(ids == 2, base_table[2:3], base_table[3:4]),
    )
    inputs = trunk.astype(jnp.float32) + embedded
    rows = rms_normed(inputs, norm_gain)
    low, high = halos(rows, DILATION_STEP)
    windows = [
        jnp.concatenate([low, rows[: length - DILATION_STEP]], axis=0),
        rows,
        jnp.concatenate([rows[DILATION_STEP:], high], axis=0),
    ]
    conv_out = jnp.zeros((length, width), jnp.float32)
    for tap in (1, 0, 2):
        conv_out = conv_out + jnp.dot(
            windows[tap], conv_weight[:, tap, :], preferred_element_type=jnp.float32
        )
    hidden = (inputs + jax.nn.gelu(conv_out)).astype(jnp.bfloat16)
    _, pull_back = jax.vjp(jax.nn.gelu, conv_out)
    dconv = pull_back(grad_out[0].astype(jnp.float32))[0].astype(jnp.bfloat16)

    accept_local = jnp.dot(hidden, accept_weight, preferred_element_type=jnp.float32).astype(
        jnp.bfloat16
    )
    picked = picked_rows(accept_local, slot_block.reshape(-1)).reshape(seq_count, -1, width)
    accepted = lax.all_to_all(picked, SEQ, 0, 0, tiled=True).reshape(-1, width)

    weight_grad = reduced_grad(windows, dconv)

    donor_emb = jnp.dot(
        picked_rows(hidden, donor_pos[0]), donor_weight, preferred_element_type=jnp.float32
    )
    slots = donor_pos.shape[1] // seq_count
    valid = (jnp.arange(slots)[None, :] < pair_counts[0][:, None]).reshape(-1)
    junction_pairs = jnp.where(
        valid[:, None], donor_emb * accepted.astype(jnp.float32), 0.0
    ).astype(jnp.bfloat16)[None]
    return (junction_pairs, weight_grad)


def solution(mesh):
    grid = Mesh(mesh.devices.reshape(8, 2, 2, 4, 2), AXES)
    return jax.shard_map(
        on_device,
        mesh=grid,
        in_specs=(
            P(DP, SEQ, None),
            P(DP, SEQ),
            P(),
            P(),
            P(),
            P(DP, SEQ, None),
            P(DP, SEQ),
            P(DP, SEQ),
            P(DP, SEQ),
            P(),
            P(),
        ),
        out_specs=(P(DP, SEQ, None), P(SEQ, None, DP)),
        check_vma=False,
    )
```

time: 252 us -> 166 us (0.66)
  waiting for transfers between devices: 145 us -> 64.8 us
  starting transfers between devices: 11.7 us -> 34.3 us
  blocking collectives: 17.2 us -> 0 us
  matrix products: 23.2 us -> 39.5 us
  local copies, waits for them, and re-layouts: 27.4 us -> 12.7 us
  between operations: 14.2 us -> 0.93 us
    reduce_scatter x1 -> x0, waiting for transfers between devices: 95 us -> none  [on_device(): lax.psum_scatter(jnp.stack([lax.dot_general(win, dconv, (((0,), (0,)), ((...]
    all_to_all x1 -> x4, waiting for transfers between devices: 0.01 us -> 64.8 us  [the longest x1 41.6 us: on_device(): accepted = lax.all_to_all(picked, SEQ, 0, 0, tiled=True).reshape(-1, width)]
    unnamed x3 -> x0, waiting for transfers between devices: 47.5 us -> none
    all_to_all x1 -> x4, starting transfers between devices: 5.93 us -> 28.7 us  [the longest x1 8.75 us: on_device(): lax.all_to_all(accept_pos[0].reshape(seq_count, -1), SEQ, 0, 0, tiled=True)]
    gather x2 -> x0, local copies, waits for them, and re-layouts: 21.9 us -> none  [the longest x1 12.5 us: on_device(): donor_emb = jnp.take(donor_all, donor_pos[0], axis=0)]
    all_to_all x1 -> x0, blocking collectives: 17.2 us -> none  [on_device(): lax.all_to_all(slot_table, 'seq', split_axis=0, concat_axis=0, tiled=True)]
    dot_general x9 -> x8, matrix products: 23.2 us -> 39.5 us  [the longest x3 15.4 us: on_device(): jnp.dot(windows[tap], conv_weight[:, tap, :], preferred_element_type=jnp....]
    convert_element_type x1 -> x0, other arithmetic: 5.49 us -> none  [on_device(): junction_pairs = jnp.where(valid[:, None], donor_emb * accepted.astype(jn...]
  transfers between devices with their start and end apart: 5 -> 7, of which waited for: 4 -> 4; matrix products, arithmetic and copies ran while one was open for 18% -> 23% of each run, Pallas kernels for 0% -> 0%
where the time goes in v1:
time: 166 us; the launch traced here: 165 us
  waiting for transfers between devices  64.8 us (39%)
  matrix products  39.5 us (24%)
  starting transfers between devices  34.3 us (21%)
  other arithmetic  13.1 us (8%)
  local copies, waits for them, and re-layouts  12.7 us (8%)
    all_to_all x1, waiting for transfers between devices, on_device(): accepted = lax.all_to_all(picked, SEQ, 0, 0, tiled=True).reshape(-1, width)  41.6 us
    all_to_all x1, waiting for transfers between devices, reduced_grad(): pieces = lax.all_to_all(pieces, ('yh', 'x'), 0, 0, tiled=True)  16 us
    dot_general x3, matrix products, on_device(): jnp.dot(windows[tap], conv_weight[:, tap, :], preferred_element_type=jnp....  15.4 us
    dot_general x1, matrix products, on_device(): jnp.dot(picked_rows(hidden, donor_pos[0]), donor_weight, preferred_elemen...  9.73 us
    all_to_all x1, starting transfers between devices, on_device(): lax.all_to_all(accept_pos[0].reshape(seq_count, -1), SEQ, 0, 0, tiled=True)  8.75 us
    all_to_all x1, starting transfers between devices, reduced_grad(): turned = lax.all_to_all(turned, DP, 0, 0, tiled=True)  8.68 us
    dot_general x1, matrix products, picked_rows(): jnp.dot(onehot, table, preferred_element_type=jnp.float32)  8.05 us
    all_to_all x1, starting transfers between devices, on_device(): accepted = lax.all_to_all(picked, SEQ, 0, 0, tiled=True).reshape(-1, width)  6.36 us
  transfers between devices with their start and end apart: 7, of which 4 were waited for; matrix products, arithmetic and copies ran while one was open for 23% of the time, Pallas kernels for 0%

profile of v1, /device:TPU:2, one launch (start us, length us, event | category | flops | bytes accessed | tf_op | source)
XLA Modules:
  0.0 165.3 jit_solution(5307890917289202058)
XLA Ops:
  0.6 0.0 copy-start
  0.6 0.9 slice_reduce_fusion.3
  1.5 0.7 compare_reduce_fusion.2
  2.3 0.0 copy-start.8
  2.3 0.0 copy-start.10
  2.3 0.0 copy-start.2
  2.3 0.0 copy-start.12
  2.3 2.5 %multiply_reduce_fusion = f32[1024]{0:T(1024)S(1)} fusion(bf16[1,1024,768]{2,1,0:T(8,128)(2,1)} %param.11, f32[768]{0:T(1024)S(1)} %get-tuple-element.4, f32[768]{0:T(1024)S(1)} %get-tuple-element.5, f32[768]{0:T(1024)S(1)} %get-tuple-element.3, f32[768]{0:T(1024)S(1)} %get-tuple-element.2, pred[1024]{0:T(1024)(128)(4,1)S(1)} %get-tuple-element.7, ...), kind=kLoop, calls=%fused_computation.38 | loop fusion | flops 5504000 | bytes 1592320 | tf_op jit(solution)/shard_map/reduce_sum | solution.py:22
  4.9 3.2 %multiply_convert_fusion = bf16[1024,768]{1,0:T(8,128)(2,1)S(1)} fusion(bf16[1,1024,768]{2,1,0:T(8,128)(2,1)} %param.11, f32[768]{0:T(1024)} %param.14, f32[1024]{0:T(1024)S(1)} %add_rsqrt_fusion, f32[768]{0:T(1024)S(1)} %get-tuple-element.4, f32[768]{0:T(1024)S(1)} %get-tuple-element.5, f32[768]{0:T(1024)S(1)} %get-tuple-element.3, ...), kind=kLoop, calls=%fused_computation.37 | loop fusion | flops 6291456 | bytes 3168256 | tf_op jit(solution)/shard_map/convert_element_type | solution.py:23
  8.1 0.1 fusion.54
  8.2 1.9 %collective-permute-start = (bf16[256,768]{1,0:T(8,128)(2,1)S(1)}, bf16[256,768]{1,0:T(8,128)(2,1)}, u32[]{:S(2)}, u32[]{:S(2)}) collective-permute-start(bf16[256,768]{1,0:T(8,128)(2,1)S(1)} %get-tuple-element.14), channel_id=1, source_target_pairs={{0,1},{1,2},{2,3},{3,4},{4,5},{5,6},{6,7},{7,8},{8,9},{9,10},{10,1... | collective-permute-start | bytes 1179656 | tf_op jit(solution)/shard_map/ppermute | solution.py:16
  10.1 3.6 %collective-permute-start.1 = (bf16[256,768]{1,0:T(8,128)(2,1)S(1)}, bf16[256,768]{1,0:T(8,128)(2,1)}, u32[]{:S(2)}, u32[]{:S(2)}) collective-permute-start(bf16[256,768]{1,0:T(8,128)(2,1)S(1)} %get-tuple-element.13), channel_id=1, source_target_pairs={{1,0},{2,1},{3,2},{4,3},{5,4},{6,5},{7,6},{8,7},{9,8},{10,9},{11,1... | collective-permute-start | bytes 1179656 | tf_op jit(solution)/shard_map/ppermute | solution.py:17
  13.8 0.0 copy-done.2
  13.8 0.0 copy-done.12
  13.8 4.8 %fusion.27 = f32[1024,768]{1,0:T(8,128)} fusion(bf16[1,1024,768]{2,1,0:T(8,128)(2,1)S(1)} %copy-done.2, f32[768]{0:T(1024)S(1)} %copy-done.12, f32[1024]{0:T(1024)S(1)} %add_rsqrt_fusion, f32[768]{0:T(1024)S(1)} %get-tuple-element.4, f32[768]{0:T(1024)S(1)} %get-tuple-element.5, f32[768]{0:T(1024)S(1)} %get-tuple-element.3, f32[768]{0:T(1024)S(1)} %get-tuple-element.2, ...), kind=kOutput, calls=%fused_computation.45 | convolution fusion | flops 1214251008 | bytes 5920768 | tf_op jit(solution)/shard_map/dot_general | solution.py:92
  18.6 0.0 copy-done.6
  18.6 0.0 copy-done.8
  18.6 0.0 copy-done.10
  18.6 2.9 %fusion.62 = bf16[768,1024]{0,1:T(8,128)(2,1)} fusion(f32[768]{0:T(1024)S(1)} %copy-done.12, f32[1024]{0:T(1024)S(1)} %add_rsqrt_fusion, f32[768]{0:T(1024)S(1)} %get-tuple-element.4, f32[768]{0:T(1024)S(1)} %get-tuple-element.5, pred[1024]{0:T(1024)(128)(4,1)S(1)} %get-tuple-element.7, f32[768]{0:T(1024)S(1)} %get-tuple-element.3, ...), kind=kLoop, calls=%fused_computation.84 | loop fusion | flops 6291456 | bytes 3168256 | tf_op jit(solution)/shard_map/dot_general | solution.py:41
  21.5 1.6 fusion.53
  23.1 2.6 %copy.20 = bf16[768,1024]{1,0:T(8,128)(2,1)} copy(bf16[768,1024]{0,1:T(8,128)(2,1)} %fusion.62) | data formatting | bytes 3145728 | tf_op jit(solution)/shard_map/dot_general | solution.py:41
  25.7 0.0 collective-permute-done
  25.7 0.0 copy-start.9
  25.7 0.0 copy-start.11
  25.7 0.0 copy-start.14
  25.7 0.0 copy-start.16
  25.7 3.3 %fusion.40 = f32[1024,768]{1,0:T(8,128)S(1)} fusion(bf16[768,3,768]{2,0,1:T(8,128)(2,1)} %param.15, bf16[768,768]{1,0:T(8,128)(2,1)} %get-tuple-element.12, bf16[256,768]{1,0:T(8,128)(2,1)} %collective-permute-done), kind=kOutput, calls=%fused_computation.59 | convolution fusion | flops 1211105280 | bytes 5898240 | tf_op jit(solution)/shard_map/dot_general | solution.py:92
  29.0 0.0 collective-permute-done.1
  29.0 0.0 copy-done.4
  29.0 0.0 copy-done.7
  29.0 0.0 copy-done.9
  29.1 0.0 copy-done.11
  29.1 0.0 copy-done.14
  29.1 0.2 copy-done.16
  29.3 7.3 %fusion.15 = (bf16[1024,768]{1,0:T(8,128)(2,1)S(1)}, bf16[1024,768]{1,0:T(8,128)(2,1)}) fusion(bf16[1,1024,768]{2,1,0:T(8,128)(2,1)S(1)} %copy-done.14, f32[768]{0:T(1024)S(1)} %get-tuple-element.4, f32[768]{0:T(1024)S(1)} %get-tuple-element.5, pred[1024]{0:T(1024)(128)(4,1)S(1)} %copy-done.9, f32[768]{0:T(1024)S(1)} %get-tuple-element.3, ...), kind=kOutput, calls=%fused_computation.27 | convolution fusion | flops 1235484672 | bytes 15350784 | tf_op jit(solution)/shard_map/dot_general | solution.py:92
  36.6 0.0 copy-done.3
  36.6 1.4 convolution_bitcast_fusion
  38.0 0.0 copy-done.5
  38.0 2.5 %fusion.47 = f32[768,768]{1,0:T(8,128)S(1)} fusion(bf16[1024,768]{1,0:T(8,128)(2,1)S(1)} %get-tuple-element.9, bf16[768,768]{1,0:T(8,128)(2,1)S(1)} %copy-done.5, bf16[256,768]{1,0:T(8,128)(2,1)} %collective-permute-done), kind=kOutput, calls=%fused_computation.66 | convolution fusion | flops 1211105280 | bytes 5505024 | tf_op jit(solution)/shard_map/dot_general | solution.py:41
  40.5 2.5 %fusion.46 = f32[768,768]{1,0:T(8,128)S(1)} fusion(bf16[1024,768]{1,0:T(8,128)(2,1)S(1)} %get-tuple-element.9, bf16[256,768]{1,0:T(8,128)(2,1)} %collective-permute-done.1, bf16[768,768]{1,0:T(8,128)(2,1)S(1)} %copy-done.4), kind=kOutput, calls=%fused_computation.65 | convolution fusion | flops 1211105280 | bytes 5505024 | tf_op jit(solution)/shard_map/dot_general | solution.py:41
  43.0 0.8 pad_maximum_fusion
  43.7 0.0 copy-start.1
  43.7 2.9 %copy-done.1 = f32[3,8,2,48,768]{4,3,2,1,0:T(8,128)} copy-done((f32[3,8,2,48,768]{4,3,2,1,0:T(8,128)}, f32[3,8,2,48,768]{4,3,2,1,0:T(8,128)S(1)}, u32[]{:S(2)}) %copy-start.1) | copy-done | bytes 7077912
  46.6 1.4 fusion.24
  48.0 0.0 collective-permute-start.2
  48.0 8.7 %all-to-all-start = ((s32[16,1,128]{2,1,0:T(1,128)}), s32[16,1,128]{2,1,0:T(1,128)S(1)}, u32[]{:S(2)}, u32[]{:S(2)}) async-start(s32[16,1,128]{2,1,0:T(1,128)} %bitcast.8), calls=%async_computation | async-start | bytes 16384 | tf_op jit(solution)/shard_map/all_to_all | solution.py:75
  56.8 0.0 collective-permute-done.2
  56.8 2.5 %fusion.25 = bf16[8,3,48,768]{3,2,0,1:T(8,128)(2,1)S(1)} fusion(bf16[3,8,48,768]{3,2,1,0:T(8,128)(2,1)S(1)} %collective-permute-done.2, f32[3,8,2,48,768]{4,3,2,1,0:T(8,128)} %copy-done.1, s32[]{:T(128)S(6)} %select_n.56), kind=kLoop, calls=%fused_computation.41 | loop fusion | flops 2654208 | bytes 7077892 | tf_op jit(solution)/shard_map/transpose | solution.py:50
  59.3 1.4 copy.21
  60.6 2.3 %all-to-all-done = s32[16,1,128]{2,1,0:T(1,128)S(1)} async-done(((s32[16,1,128]{2,1,0:T(1,128)}), s32[16,1,128]{2,1,0:T(1,128)S(1)}, u32[]{:S(2)}, u32[]{:S(2)}) %all-to-all-start) | async-done | bytes 8224 | tf_op jit(solution)/shard_map/all_to_all | solution.py:75
  62.9 5.0 %all-to-all-start.2 = ((bf16[8,144,768]{2,1,0:T(8,128)(2,1)}), bf16[8,144,768]{2,1,0:T(8,128)(2,1)S(1)}, u32[]{:S(2)}, u32[]{:S(2)}) async-start(bf16[8,144,768]{2,1,0:T(8,128)(2,1)} %bitcast.75), calls=%async_computation.2 | async-start | bytes 3538944 | tf_op jit(solution)/shard_map/all_to_all | solution.py:51
  67.9 0.0 copy-done
  67.9 8.1 %fusion.7 = bf16[2048,768]{1,0:T(8,128)(2,1)} fusion(s32[2048]{0:T(1024)S(1)} %bitcast.82, bf16[1024,768]{1,0:T(8,128)(2,1)} %get-tuple-element.10, bf16[768,768]{1,0:T(8,128)(2,1)S(1)} %copy-done), kind=kOutput, calls=%fused_computation.19 | convolution fusion | flops 4433641472 | bytes 5906432 | tf_op jit(solution)/shard_map/dot_general | solution.py:28
  75.9 16.0 %all-to-all-done.2 = bf16[8,144,768]{2,1,0:T(8,128)(2,1)S(1)} async-done(((bf16[8,144,768]{2,1,0:T(8,128)(2,1)}), bf16[8,144,768]{2,1,0:T(8,128)(2,1)S(1)}, u32[]{:S(2)}, u32[]{:S(2)}) %all-to-all-start.2) | async-done | bytes 1769504 | tf_op jit(solution)/shard_map/all_to_all | solution.py:51
  91.9 6.4 %all-to-all-start.1 = ((bf16[16,128,768]{2,1,0:T(8,128)(2,1)}), bf16[16,128,768]{2,1,0:T(8,128)(2,1)}, u32[]{:S(2)}, u32[]{:S(2)}) async-start(bf16[16,128,768]{2,1,0:T(8,128)(2,1)} %bitcast.76), calls=%async_computation.1 | async-start | bytes 6291456 | tf_op jit(solution)/shard_map/all_to_all | solution.py:103
  98.3 0.1 fusion.48
  98.4 0.3 reduce_sum.31
  98.7 0.9 copy.22
  99.6 41.6 %all-to-all-done.1 = bf16[16,128,768]{2,1,0:T(8,128)(2,1)} async-done(((bf16[16,128,768]{2,1,0:T(8,128)(2,1)}), bf16[16,128,768]{2,1,0:T(8,128)(2,1)}, u32[]{:S(2)}, u32[]{:S(2)}) %all-to-all-start.1) | async-done | bytes 3145760 | tf_op jit(solution)/shard_map/all_to_all | solution.py:103
  141.3 8.7 %all-to-all-start.3 = ((bf16[16,48,144]{2,1,0:T(8,128)(2,1)}), bf16[16,48,144]{2,1,0:T(8,128)(2,1)S(1)}, u32[]{:S(2)}, u32[]{:S(2)}) async-start(bf16[16,48,144]{2,1,0:T(8,128)(2,1)} %bitcast.27), calls=%async_computation.3 | async-start | bytes 786432 | tf_op jit(solution)/shard_map/all_to_all | solution.py:54
  150.0 9.7 %fusion.23 = bf16[1,2048,768]{2,1,0:T(8,128)(2,1)} fusion(bf16[2048,768]{1,0:T(8,128)(2,1)} %bitcast.30, bf16[768,768]{1,0:T(8,128)(2,1)} %param.20, pred[2048]{0:T(1024)(128)(4,1)S(1)} %fusion.48, bf16[1024,768]{1,0:T(8,128)(2,1)} %get-tuple-element.10, s32[2048]{0:T(1024)S(1)} %bitcast.84), kind=kOutput, calls=%fused_computation.39 | convolution fusion | flops 5647106048 | bytes 9054208 | tf_op jit(solution)/shard_map/dot_general | solution.py:107
  159.7 4.8 %all-to-all-done.3 = bf16[16,48,144]{2,1,0:T(8,128)(2,1)S(1)} async-done(((bf16[16,48,144]{2,1,0:T(8,128)(2,1)}), bf16[16,48,144]{2,1,0:T(8,128)(2,1)S(1)}, u32[]{:S(2)}, u32[]{:S(2)}) %all-to-all-start.3) | async-done | bytes 221216 | tf_op jit(solution)/shard_map/all_to_all | solution.py:54
  164.5 0.1 convert_reduce_fusion
  164.6 0.7 copy.23
  (10 shorter events, 0.0 us)
Async XLA Ops:
  0.6 67.2 %copy-start = (bf16[768,768]{1,0:T(8,128)(2,1)S(1)}, bf16[768,768]{1,0:T(8,128)(2,1)}, u32[]{:S(2)}) copy-start(bf16[768,768]{1,0:T(8,128)(2,1)} %param.21) | copy-start | bytes 3538948
  2.3 16.3 %copy-start.6 = (pred[1024]{0:T(1024)(128)(4,1)}, pred[1024]{0:T(1024)(128)(4,1)S(1)}, u32[]{:S(2)}) copy-start(pred[1024]{0:T(1024)(128)(4,1)S(1)} %get-tuple-element.6) | copy-start | bytes 3076
  2.3 16.3 %copy-start.8 = (pred[1024]{0:T(1024)(128)(4,1)}, pred[1024]{0:T(1024)(128)(4,1)S(1)}, u32[]{:S(2)}) copy-start(pred[1024]{0:T(1024)(128)(4,1)S(1)} %get-tuple-element.7) | copy-start | bytes 3076
  2.3 16.3 %copy-start.10 = (pred[1024]{0:T(1024)(128)(4,1)}, pred[1024]{0:T(1024)(128)(4,1)S(1)}, u32[]{:S(2)}) copy-start(pred[1024]{0:T(1024)(128)(4,1)S(1)} %get-tuple-element.8) | copy-start | bytes 3076
  2.3 11.5 %copy-start.2 = (bf16[1,1024,768]{2,1,0:T(8,128)(2,1)S(1)}, bf16[1,1024,768]{2,1,0:T(8,128)(2,1)}, u32[]{:S(2)}) copy-start(bf16[1,1024,768]{2,1,0:T(8,128)(2,1)} %param.11) | copy-start | bytes 4718596
  2.3 11.5 %copy-start.12 = (f32[768]{0:T(1024)S(1)}, f32[768]{0:T(1024)}, u32[]{:S(2)}) copy-start(f32[768]{0:T(1024)} %param.14) | copy-start | bytes 9220
  8.2 17.5 %collective-permute-start = (bf16[256,768]{1,0:T(8,128)(2,1)S(1)}, bf16[256,768]{1,0:T(8,128)(2,1)}, u32[]{:S(2)}, u32[]{:S(2)}) collective-permute-start(bf16[256,768]{1,0:T(8,128)(2,1)S(1)} %get-tuple-element.14), channel_id=1, source_target_pairs={{0,1},{1,2},{2,3},{3,4},{4,5},{5,6},{6,7},{7,8},{8,9},{9,10},{10,1... | collective-permute-start | bytes 1179656 | tf_op jit(solution)/shard_map/ppermute | solution.py:16
  10.1 18.9 %collective-permute-start.1 = (bf16[256,768]{1,0:T(8,128)(2,1)S(1)}, bf16[256,768]{1,0:T(8,128)(2,1)}, u32[]{:S(2)}, u32[]{:S(2)}) collective-permute-start(bf16[256,768]{1,0:T(8,128)(2,1)S(1)} %get-tuple-element.13), channel_id=1, source_target_pairs={{1,0},{2,1},{3,2},{4,3},{5,4},{6,5},{7,6},{8,7},{9,8},{10,9},{11,1... | collective-permute-start | bytes 1179656 | tf_op jit(solution)/shard_map/ppermute | solution.py:17
  25.7 3.4 %copy-start.4 = (bf16[768,768]{1,0:T(8,128)(2,1)S(1)}, bf16[768,768]{1,0:T(8,128)(2,1)}, u32[]{:S(2)}) copy-start(bf16[768,768]{1,0:T(8,128)(2,1)} %get-tuple-element.11) | copy-start | bytes 3538948
  25.7 3.4 %copy-start.7 = (pred[1024]{0:T(1024)(128)(4,1)S(1)}, pred[1024]{0:T(1024)(128)(4,1)}, u32[]{:S(2)}) copy-start(pred[1024]{0:T(1024)(128)(4,1)} %copy-done.6) | copy-start | bytes 3076
  25.7 3.4 %copy-start.9 = (pred[1024]{0:T(1024)(128)(4,1)S(1)}, pred[1024]{0:T(1024)(128)(4,1)}, u32[]{:S(2)}) copy-start(pred[1024]{0:T(1024)(128)(4,1)} %copy-done.8) | copy-start | bytes 3076
  25.7 3.4 %copy-start.11 = (pred[1024]{0:T(1024)(128)(4,1)S(1)}, pred[1024]{0:T(1024)(128)(4,1)}, u32[]{:S(2)}) copy-start(pred[1024]{0:T(1024)(128)(4,1)} %copy-done.10) | copy-start | bytes 3076
  25.7 3.4 %copy-start.14 = (bf16[1,1024,768]{2,1,0:T(8,128)(2,1)S(1)}, bf16[1,1024,768]{2,1,0:T(8,128)(2,1)}, u32[]{:S(2)}) copy-start(bf16[1,1024,768]{2,1,0:T(8,128)(2,1)} %param.16) | copy-start | bytes 4718596
  25.7 3.6 %copy-start.16 = (f32[1024,768]{1,0:T(8,128)S(1)}, f32[1024,768]{1,0:T(8,128)}, u32[]{:S(2)}) copy-start(f32[1024,768]{1,0:T(8,128)} %fusion.27) | copy-start | bytes 9437188
  29.3 7.3 %copy-start.3 = (bf16[768,1024]{1,0:T(8,128)(2,1)S(1)}, bf16[768,1024]{1,0:T(8,128)(2,1)}, u32[]{:S(2)}) copy-start(bf16[768,1024]{1,0:T(8,128)(2,1)} %copy.20) | copy-start | bytes 4718596
  36.6 1.4 copy-start.5
  43.7 2.9 %copy-start.1 = (f32[3,8,2,48,768]{4,3,2,1,0:T(8,128)}, f32[3,8,2,48,768]{4,3,2,1,0:T(8,128)S(1)}, u32[]{:S(2)}) copy-start(f32[3,8,2,48,768]{4,3,2,1,0:T(8,128)S(1)} %pad_maximum_fusion) | copy-start | bytes 21233668
  48.0 8.8 %collective-permute-start.2 = (bf16[3,8,48,768]{3,2,1,0:T(8,128)(2,1)}, bf16[3,8,48,768]{3,2,1,0:T(8,128)(2,1)S(1)}, u32[]{:S(2)}, u32[]{:S(2)}) collective-permute-start(bf16[3,8,48,768]{3,2,1,0:T(8,128)(2,1)} %fusion.24), channel_id=1, source_target_pairs={{0,1},{1,0},{2,3},{3,2},{4,5},{5,4},{6,7},{7,6},{8,9},{9,8},{10,11... | collective-permute-start | bytes 5308424 | tf_op jit(solution)/shard_map/ppermute | solution.py:48
  48.0 14.9 %all-to-all-start = ((s32[16,1,128]{2,1,0:T(1,128)}), s32[16,1,128]{2,1,0:T(1,128)S(1)}, u32[]{:S(2)}, u32[]{:S(2)}) async-start(s32[16,1,128]{2,1,0:T(1,128)} %bitcast.8), calls=%async_computation | async-start | bytes 16384 | tf_op jit(solution)/shard_map/all_to_all | solution.py:75
  62.9 29.0 %all-to-all-start.2 = ((bf16[8,144,768]{2,1,0:T(8,128)(2,1)}), bf16[8,144,768]{2,1,0:T(8,128)(2,1)S(1)}, u32[]{:S(2)}, u32[]{:S(2)}) async-start(bf16[8,144,768]{2,1,0:T(8,128)(2,1)} %bitcast.75), calls=%async_computation.2 | async-start | bytes 3538944 | tf_op jit(solution)/shard_map/all_to_all | solution.py:51
  91.9 6.4 %copy-start.13 = (s32[1,16]{1,0:T(1,128)S(1)}, s32[1,16]{1,0:T(1,128)}, u32[]{:S(2)}) copy-start(s32[1,16]{1,0:T(1,128)} %param.19) | copy-start | bytes 196
  91.9 49.3 %all-to-all-start.1 = ((bf16[16,128,768]{2,1,0:T(8,128)(2,1)}), bf16[16,128,768]{2,1,0:T(8,128)(2,1)}, u32[]{:S(2)}, u32[]{:S(2)}) async-start(bf16[16,128,768]{2,1,0:T(8,128)(2,1)} %bitcast.76), calls=%async_computation.1 | async-start | bytes 6291456 | tf_op jit(solution)/shard_map/all_to_all | solution.py:103
  98.3 51.6 %copy-start.15 = (s32[1,2048]{1,0:T(1,128)S(1)}, s32[1,2048]{1,0:T(1,128)}, u32[]{:S(2)}) copy-start(s32[1,2048]{1,0:T(1,128)} %param.17) | copy-start | bytes 24580
  141.3 23.2 %all-to-all-start.3 = ((bf16[16,48,144]{2,1,0:T(8,128)(2,1)}), bf16[16,48,144]{2,1,0:T(8,128)(2,1)S(1)}, u32[]{:S(2)}, u32[]{:S(2)}) async-start(bf16[16,48,144]{2,1,0:T(8,128)(2,1)} %bitcast.27), calls=%async_computation.3 | async-start | bytes 786432 | tf_op jit(solution)/shard_map/all_to_all | solution.py:54

commit v2 on v1

v2 whole, which is shorter than its diff:
```python
import functools

import jax
import jax.numpy as jnp
from jax import lax
from jax.experimental import pallas as pl
from jax.experimental.pallas import tpu as pltpu
from jax.sharding import Mesh, PartitionSpec as P

DILATION_STEP = 256
AXES = ("z", "yl", "yh", "x", "core")
DP = ("z", "yl")
SEQ = ("yh", "x", "core")
CHIPS = ("yh", "x")
LANES = 128
VMEM_BYTES = 48 * 1024 * 1024
BF16 = jnp.bfloat16
F32 = jnp.float32
GELU_A = 0.7978845608028654
GELU_B = 0.044715


def params():
    return pltpu.CompilerParams(vmem_limit_bytes=VMEM_BYTES)


def cost(flops, nbytes):
    return pl.CostEstimate(flops=flops, bytes_accessed=nbytes, transcendentals=0)


def across_lanes(row):
    return jnp.transpose(jnp.broadcast_to(row, (LANES, LANES)))


def summed_inputs(trunk, ids_ref, first, table_ref):
    rows, width = trunk.shape
    parts = []
    for block in range(rows // LANES):
        ids = across_lanes(ids_ref[pl.ds(first + block, 1), :])
        ids = jnp.concatenate([ids] * (width // LANES), axis=1)
        embedded = jnp.where(
            ids < 2,
            jnp.where(ids == 0, table_ref[0:1, :], table_ref[1:2, :]),
            jnp.where(ids == 2, table_ref[2:3, :], table_ref[3:4, :]),
        )
        parts.append(trunk[block * LANES : (block + 1) * LANES].astype(F32) + embedded)
    return jnp.concatenate(parts, axis=0)


def norm_kernel(trunk_ref, ids_ref, table_ref, gain_ref, out_ref):
    per_chunk = trunk_ref.shape[0] // LANES
    inputs = summed_inputs(trunk_ref[...], ids_ref, pl.program_id(0) * per_chunk, table_ref)
    mean = jnp.mean(inputs * inputs, axis=-1, keepdims=True)
    out_ref[...] = (inputs * lax.rsqrt(mean + 1e-06) * gain_ref[...]).astype(BF16)


def norm_rows(trunk, ids, table, gain):
    length, width = trunk.shape
    chunk = DILATION_STEP
    whole = lambda i: (0, 0)
    return pl.pallas_call(
        norm_kernel,
        grid=(length // chunk,),
        in_specs=[
            pl.BlockSpec((chunk, width), lambda i: (i, 0)),
            pl.BlockSpec(ids.shape, whole),
            pl.BlockSpec(table.shape, whole),
            pl.BlockSpec(gain.shape, whole),
        ],
        out_specs=pl.BlockSpec((chunk, width), lambda i: (i, 0)),
        out_shape=jax.ShapeDtypeStruct((length, width), BF16),
        compiler_params=params(),
        cost_estimate=cost(10 * length * width, 4 * length * width),
    )(trunk, ids, table, gain)


def gelu_parts(x):
    square = x * x
    t = jnp.tanh(GELU_A * x * (1.0 + GELU_B * square))
    cdf = 0.5 + 0.5 * t
    slope = cdf + (0.5 * GELU_A) * x * (1.0 - t * t) * (1.0 + (3 * GELU_B) * square)
    return x * cdf, slope


def finish_chunk(conv, trunk, grad, ids_ref, first, table_ref, hidden_ref, dconv_ref):
    inputs = summed_inputs(trunk, ids_ref, first, table_ref)
    act, slope = gelu_parts(conv)
    hidden_ref[...] = (inputs + act).astype(BF16)
    dconv_ref[...] = (grad.astype(F32) * slope).astype(BF16)


def turned(block, rows):
    width = block.shape[1]
    return jnp.transpose(block).reshape(width // (2 * rows), 2, rows, block.shape[0])


def inner_kernel(left_ref, mid_ref, right_ref, w_ref, trunk_ref, grad_ref, ids_ref, table_ref, all_ref,
                 hidden_ref, dconv_ref, turned_ref, *, rows):
    i = pl.program_id(0)
    window = jnp.concatenate([left_ref[...], mid_ref[...], right_ref[...]], axis=1)
    conv = jnp.dot(window, w_ref[...], preferred_element_type=F32)
    finish_chunk(conv, trunk_ref[...], grad_ref[...], ids_ref, 2 * (i + 1), table_ref, hidden_ref, dconv_ref)
    chunk = left_ref.shape[0]
    turned_ref[:, :, :, :chunk] = turned(all_ref[:chunk], rows)
    turned_ref[:, :, :, chunk:] = turned(all_ref[chunk:], rows)


def edge_kernel(low_ref, high_ref, near_ref, mid_ref, w_ref, trunk_ref, grad_ref, ids_ref, table_ref, h_in, d_in,
                hidden_ref, dconv_ref, low_t_ref, high_t_ref, acc_ref, *, rows):
    del h_in, d_in
    i = pl.program_id(0)
    width = mid_ref.shape[1]

    @pl.when(i == 0)
    def _():
        window = jnp.concatenate([low_ref[...], mid_ref[...], near_ref[...]], axis=1)
        acc_ref[...] = jnp.dot(window, w_ref[...], preferred_element_type=F32)
        low_t_ref[...] = turned(low_ref[...], rows)

    @pl.when(i == 1)
    def _():
        window = jnp.concatenate([near_ref[...], mid_ref[...], high_ref[...]], axis=1)
        acc_ref[...] = jnp.dot(window, w_ref[...], preferred_element_type=F32)
        high_t_ref[...] = turned(high_ref[...], rows)

    finish_chunk(acc_ref[...], trunk_ref[...], grad_ref[...], ids_ref, 6 * i, table_ref, hidden_ref, dconv_ref)


def conv_inner(normed, weight, trunk, grad, ids, table, rows):
    length, width = trunk.shape
    chunk = DILATION_STEP
    whole = lambda i: (0, 0)
    block = lambda shift: pl.BlockSpec((chunk, width), lambda i: (i + shift, 0))
    groups = width // (2 * rows)
    return pl.pallas_call(
        functools.partial(inner_kernel, rows=rows),
        grid=(2,),
        in_specs=[
            block(0), block(1), block(2),
            pl.BlockSpec(weight.shape, whole),
            block(1), block(1),
            pl.BlockSpec(ids.shape, whole),
            pl.BlockSpec(table.shape, whole),
            pl.BlockSpec((2 * chunk, width), lambda i: (i, 0)),
        ],
        out_specs=[
            block(1), block(1),
            pl.BlockSpec((groups, 2, rows, 2 * chunk), lambda i: (0, 0, 0, i)),
        ],
        out_shape=[
            jax.ShapeDtypeStruct((length, width), BF16),
            jax.ShapeDtypeStruct((length, width), BF16),
            jax.ShapeDtypeStruct((groups, 2, rows, length), BF16),
        ],
        compiler_params=params(),
        cost_estimate=cost(3 * length * width * width, 8 * length * width),
    )(normed, normed, normed, weight, trunk, grad, ids, table, normed)


def conv_edges(low, high, normed, weight, trunk, grad, ids, table, hidden, dconv, rows):
    length, width = trunk.shape
    chunk = DILATION_STEP
    whole = lambda i: (0, 0)
    outer = pl.BlockSpec((chunk, width), lambda i: (3 * i, 0))
    groups = width // (2 * rows)
    t_spec = pl.BlockSpec((groups, 2, rows, chunk), lambda i: (0, 0, 0, 0))
    t_shape = jax.ShapeDtypeStruct((groups, 2, rows, chunk), BF16)
    return pl.pallas_call(
        functools.partial(edge_kernel, rows=rows),
        grid=(2,),
        in_specs=[
            pl.BlockSpec(low.shape, whole),
            pl.BlockSpec(high.shape, whole),
            pl.BlockSpec((chunk, width), lambda i: (i + 1, 0)),
            outer,
            pl.BlockSpec(weight.shape, whole),
            outer, outer,
            pl.BlockSpec(ids.shape, whole),
            pl.BlockSpec(table.shape, whole),
            pl.BlockSpec(memory_space=pl.ANY),
            pl.BlockSpec(memory_space=pl.ANY),
        ],
        out_specs=[outer, outer, t_spec, t_spec],
        out_shape=[
            jax.ShapeDtypeStruct((length, width), BF16),
            jax.ShapeDtypeStruct((length, width), BF16),
            t_shape, t_shape,
        ],
        scratch_shapes=[pltpu.VMEM((chunk, width), F32)],
        input_output_aliases={9: 0, 10: 1},
        compiler_params=params(),
        cost_estimate=cost(3 * length * width * width, 8 * length * width),
    )(low, high, normed, normed, weight, trunk, grad, ids, table, hidden, dconv)


def grad_kernel(half_ref, turned_ref, low_ref, high_ref, dconv_ref, *rest, add):
    del half_ref
    other_ref, out_ref = rest if add else (None, rest[0])
    groups, _, rows, length = turned_ref.shape
    edge = low_ref.shape[3]
    tap = pl.program_id(0)
    flat = lambda v: v.reshape(groups * rows, v.shape[-1])
    dot = lambda a, b: jnp.dot(a, b, preferred_element_type=F32)

    def put(value):
        if add:
            value = value + flat(other_ref[:, 0]).astype(F32)
        out_ref[:, 0] = value.reshape(groups, rows, value.shape[-1]).astype(BF16)

    @pl.when(tap == 0)
    def _():
        window = jnp.concatenate([flat(low_ref[:, 0]), flat(turned_ref[:, 0, :, : length - edge])], axis=1)
        put(dot(window, dconv_ref[...]))

    @pl.when(tap == 1)
    def _():
        put(dot(flat(turned_ref[:, 0]), dconv_ref[...]))

    @pl.when(tap == 2)
    def _():
        window = jnp.concatenate([flat(turned_ref[:, 0, :, edge:]), flat(high_ref[:, 0])], axis=1)
        put(dot(window, dconv_ref[...]))


def grad_half(half, turned_rows, low_t, high_t, dconv, other=None):
    groups, _, rows, length = turned_rows.shape
    width = dconv.shape[1]
    taps = 3
    pick = lambda t, h: (0, h[0], 0, 0)
    out_spec = pl.BlockSpec((groups, 1, rows, width), lambda t, h: (0, t, 0, 0))
    specs = [
        pl.BlockSpec((groups, 1, rows, length), pick),
        pl.BlockSpec((groups, 1, rows, low_t.shape[3]), pick),
        pl.BlockSpec((groups, 1, rows, high_t.shape[3]), pick),
        pl.BlockSpec(dconv.shape, lambda t, h: (0, 0)),
    ]
    args = [half, turned_rows, low_t, high_t, dconv]
    if other is not None:
        specs.append(out_spec)
        args.append(other)
    return pl.pallas_call(
        functools.partial(grad_kernel, add=other is not None),
        grid_spec=pltpu.PrefetchScalarGridSpec(
            num_scalar_prefetch=1, grid=(taps,), in_specs=specs, out_specs=out_spec
        ),
        out_shape=jax.ShapeDtypeStruct((groups, taps, rows, width), BF16),
        compiler_params=params(),
        cost_estimate=cost(taps * length * width * width, 6 * length * width),
    )(*args)


def selected(index_row, table_ref):
    index = across_lanes(index_row)
    lane = lax.broadcasted_iota(jnp.int32, (LANES, LANES), 1)
    blocks = [
        jnp.where(index == lane + b * LANES, 1.0, 0.0).astype(BF16)
        for b in range(table_ref.shape[0] // LANES)
    ]
    return jnp.dot(jnp.concatenate(blocks, axis=1), table_ref[...], preferred_element_type=F32)


def serve_kernel(hot_ref, place_ref, index_ref, own_ref, other_ref, out_ref):
    del place_ref
    half = LANES // 2
    own = selected(index_ref[0, 0:1, :], own_ref).astype(BF16)
    other = selected(index_ref[0, 1:2, :], other_ref).astype(BF16)
    out_ref[0, 0] = own[:half]
    out_ref[0, 1] = other[:half]

    @pl.when(hot_ref[0] == 0)
    def _():
        out_ref[0, 2] = own[half:]

    @pl.when(hot_ref[0] != 0)
    def _():
        out_ref[0, 2] = other[half:]


def serve(hot, place, index, own, other):
    groups = index.shape[0]
    width = own.shape[1]
    whole = lambda q, h, p: (0, 0)
    return pl.pallas_call(
        serve_kernel,
        grid_spec=pltpu.PrefetchScalarGridSpec(
            num_scalar_prefetch=2,
            grid=(groups,),
            in_specs=[
                pl.BlockSpec((1, 2, LANES), lambda q, h, p: (p[q], 0, 0)),
                pl.BlockSpec(own.shape, whole),
                pl.BlockSpec(other.shape, whole),
            ],
            out_specs=pl.BlockSpec((1, 3, LANES // 2, width), lambda q, h, p: (q, 0, 0, 0)),
        ),
        out_shape=jax.ShapeDtypeStruct((groups, 3, LANES // 2, width), BF16),
        compiler_params=params(),
        cost_estimate=cost(4 * groups * LANES * own.shape[0] * width, 8 * own.size),
    )(hot, place, index, own, other)


def donor_kernel(index_ref, hidden_ref, w_ref, out_ref):
    for b in range(2):
        rows = selected(index_ref[0, b : b + 1, :], hidden_ref).astype(BF16)
        out_ref[b * LANES : (b + 1) * LANES] = jnp.dot(rows, w_ref[...], preferred_element_type=F32)


def donor_rows(index, hidden, weight):
    groups = index.shape[0]
    width = hidden.shape[1]
    whole = lambda q: (0, 0)
    return pl.pallas_call(
        donor_kernel,
        grid=(groups,),
        in_specs=[
            pl.BlockSpec((1, 2, LANES), lambda q: (q, 0, 0)),
            pl.BlockSpec(hidden.shape, whole),
            pl.BlockSpec(weight.shape, whole),
        ],
        out_specs=pl.BlockSpec((2 * LANES, width), lambda q: (q, 0)),
        out_shape=jax.ShapeDtypeStruct((groups * 2 * LANES, width), F32),
        compiler_params=params(),
        cost_estimate=cost(4 * groups * LANES * (hidden.shape[0] + width) * width, 10 * hidden.size),
    )(index, hidden, weight)


def pair_kernel(core_ref, counts_ref, donor_ref, accepted_ref, out_ref):
    half = LANES // 2
    group = pl.program_id(0)
    slot = lax.broadcasted_iota(jnp.int32, (half, out_ref.shape[1]), 0)
    for owner_core in range(2):
        count = counts_ref[2 * group + owner_core]
        place = lax.rem(core_ref[0] + owner_core, 2)
        first = owner_core * LANES
        lower = accepted_ref[0, place].astype(F32) * donor_ref[first : first + half]
        out_ref[first : first + half] = jnp.where(slot < count, lower, 0.0).astype(BF16)
        upper = accepted_ref[0, 2].astype(F32) * donor_ref[first + half : first + LANES]
        out_ref[first + half : first + LANES] = jnp.where(slot + half < count, upper, 0.0).astype(BF16)


def pairs(core, counts, donor, accepted):
    groups = accepted.shape[0]
    width = donor.shape[1]
    return pl.pallas_call(
        pair_kernel,
        grid_spec=pltpu.PrefetchScalarGridSpec(
            num_scalar_prefetch=2,
            grid=(groups,),
            in_specs=[
                pl.BlockSpec((2 * LANES, width), lambda q, c, n: (q, 0)),
                pl.BlockSpec((1,) + accepted.shape[1:], lambda q, c, n: (q, 0, 0, 0)),
            ],
            out_specs=pl.BlockSpec((2 * LANES, width), lambda q, c, n: (q, 0)),
        ),
        out_shape=jax.ShapeDtypeStruct(donor.shape, BF16),
        compiler_params=params(),
        cost_estimate=cost(2 * donor.size, 8 * donor.size),
    )(core, counts, donor, accepted)


def halos(block, width):
    count = lax.axis_size(SEQ)
    forward = [(i, i + 1) for i in range(count - 1)]
    backward = [(target, source) for source, target in forward]
    low = lax.ppermute(block[block.shape[0] - width :], SEQ, forward)
    high = lax.ppermute(block[:width], SEQ, backward)
    return low, high


def chip_exchange(blocks):
    ny, nx = lax.axis_size("yh"), lax.axis_size("x")
    y, x = lax.axis_index("yh"), lax.axis_index("x")
    got = []
    for step in range(ny * nx):
        dy, dx = step // nx, step % nx
        target = lax.rem(y + dy, ny) * nx + lax.rem(x + dx, nx)
        block = lax.dynamic_index_in_dim(blocks, target, 0, keepdims=False)
        if step:
            perm = [
                (i * nx + j, (i + dy) % ny * nx + (j + dx) % nx) for i in range(ny) for j in range(nx)
            ]
            block = lax.ppermute(block, CHIPS, perm)
        got.append(block)
    sources = jnp.arange(ny * nx)
    steps = lax.rem(y - sources // nx + ny, ny) * nx + lax.rem(x - sources % nx + nx, nx)
    return jnp.stack(got), steps


def dp_sum(own):
    nz = lax.axis_size("z")
    z, yl = lax.axis_index("z"), lax.axis_index("yl")
    blocks = own.reshape(nz, -1, own.shape[1])
    narrow = blocks.astype(BF16)
    total = lax.dynamic_index_in_dim(blocks, z, 0, keepdims=False)
    for step in range(1, nz):
        sent = lax.dynamic_index_in_dim(narrow, lax.rem(z + step, nz), 0, keepdims=False)
        got = lax.ppermute(sent, "z", [(i, (i + step) % nz) for i in range(nz)])
        total = total + got.astype(F32)
    total = total.reshape(2, -1, own.shape[1])
    sent = lax.dynamic_index_in_dim(total, 1 - yl, 0, keepdims=False).astype(BF16)
    kept = lax.dynamic_index_in_dim(total, yl, 0, keepdims=False)
    return kept + lax.ppermute(sent, "yl", [(0, 1), (1, 0)]).astype(F32)


def on_device(
    trunk_acts,
    base_ids,
    base_table,
    norm_gain,
    conv_weight,
    grad_out,
    donor_pos,
    accept_pos,
    pair_counts,
    donor_weight,
    accept_weight,
):
    seq_count = lax.axis_size(SEQ)
    core = lax.axis_index("core")
    chip = lax.axis_index(CHIPS)
    trunk, grad = trunk_acts[0], grad_out[0]
    length, width = trunk.shape
    taps = conv_weight.shape[1]
    rows = width // seq_count
    chips = seq_count // 2
    ids = base_ids.reshape(length // LANES, LANES)
    weight = jnp.transpose(conv_weight, (1, 0, 2)).reshape(taps * width, width)

    normed = norm_rows(trunk, ids, base_table, norm_gain[None])
    low, high = halos(normed, DILATION_STEP)
    hidden, dconv, turned_rows = conv_inner(normed, weight, trunk, grad, ids, base_table, rows)
    hidden, dconv, low_t, high_t = conv_edges(
        low, high, normed, weight, trunk, grad, ids, base_table, hidden, dconv, rows
    )

    swap = [(0, 1), (1, 0)]
    sent = grad_half((1 - core)[None], turned_rows, low_t, high_t, dconv)
    other_half = lax.ppermute(sent, "core", swap)
    accept_local = jnp.dot(hidden, accept_weight, preferred_element_type=F32).astype(BF16)
    accept_local, other_half = lax.optimization_barrier((accept_local, other_half))
    chip_half = grad_half(core[None], turned_rows, low_t, high_t, dconv, other_half)
    accept_local, accept_pos, donor_pos, chip_half = lax.optimization_barrier(
        (accept_local, accept_pos, donor_pos, chip_half)
    )
    pieces = lax.all_to_all(chip_half, CHIPS, 0, 0, tiled=True)

    accept_other = lax.ppermute(accept_local, "core", swap)
    slots = accept_pos.reshape(chips, 2, -1)
    mine, theirs = slots[:, :1], slots[:, 1:]
    slots = jnp.concatenate(
        [jnp.where(core == 0, mine, theirs), jnp.where(core == 0, theirs, mine)], axis=1
    )
    slots, place = chip_exchange(slots)
    counts = pair_counts[0]
    hot = (lax.dynamic_index_in_dim(counts, 2 * chip + 1 - core, 0) > slots.shape[2] // 2).astype(jnp.int32)
    served = serve(hot, place, slots, accept_local, accept_other)
    donor_emb = donor_rows(donor_pos.reshape(chips, 2, -1), hidden, donor_weight)

    pieces, served = lax.optimization_barrier((pieces, served))
    accepted = lax.all_to_all(served, CHIPS, 0, 0, tiled=True)

    own = jnp.sum(pieces.astype(F32), axis=0).reshape(taps * rows, width)
    total = dp_sum(own.T)
    weight_grad = jnp.transpose(total.reshape(-1, taps, rows), (2, 1, 0))
    junction_pairs = pairs(core[None], counts, donor_emb, accepted)[None]
    return (junction_pairs, weight_grad)


def solution(mesh):
    grid = Mesh(mesh.devices.reshape(8, 2, 2, 4, 2), AXES)
    return jax.shard_map(
        on_device,
        mesh=grid,
        in_specs=(
            P(DP, SEQ, None),
            P(DP, SEQ),
            P(),
            P(),
            P(),
            P(DP, SEQ, None),
            P(DP, SEQ),
            P(DP, SEQ),
            P(DP, SEQ),
            P(),
            P(),
        ),
        out_specs=(P(DP, SEQ, None), P(SEQ, None, DP)),
        check_vma=False,
    )
```

time: 166 us -> 164 us (0.988)
  Pallas kernels: 0 us -> 48.3 us
  waiting for transfers between devices: 64.8 us -> 21.2 us
  matrix products: 39.5 us -> 2.57 us
  starting transfers between devices: 34.3 us -> 55 us
  local copies, waits for them, and re-layouts: 12.7 us -> 27.5 us
  other arithmetic: 13.1 us -> 6.36 us
    all_to_all x4 -> x2, waiting for transfers between devices: 64.8 us -> 0.01 us  [the longest x1 0.01 us: on_device(): pieces = lax.all_to_all(chip_half, CHIPS, 0, 0, tiled=True)]
    pallas_call x0 -> x8, Pallas kernels: none -> 48.3 us  [the longest x1 10.9 us: donor_rows(): pl.pallas_call(donor_kernel, grid=(groups,), in_specs=[pl.BlockSpec((1, 2...]
    ppermute x1 -> x17, starting transfers between devices: 0.01 us -> 37.5 us  [the longest x7 18.4 us: dp_sum(): got = lax.ppermute(sent, 'z', [(i, (i + step) % nz) for i in range(nz)])]
    dot_general x8 -> x1, matrix products: 39.5 us -> 2.57 us  [on_device(): jnp.dot(hidden, accept_weight, preferred_element_type=F32).astype(BF16)]
    ppermute x1 -> x17, waiting for transfers between devices: 0.01 us -> 21.1 us  [the longest x7 19 us: chip_exchange(): block = lax.ppermute(block, CHIPS, perm)]
    all_to_all x4 -> x2, starting transfers between devices: 28.7 us -> 13.2 us  [the longest x1 9.23 us: on_device(): pieces = lax.all_to_all(chip_half, CHIPS, 0, 0, tiled=True)]
    unnamed x34 -> x63, local copies, waits for them, and re-layouts: 3.18 us -> 17.4 us
    add x0 -> x2, local copies, waits for them, and re-layouts: none -> 3.14 us  [the longest x1 1.61 us: dp_sum(): total = total + got.astype(F32)]
  transfers between devices with their start and end apart: 7 -> 21, of which waited for: 4 -> 5; matrix products, arithmetic and copies ran while one was open for 23% -> 14% of each run, Pallas kernels for 0% -> 14%
where the time goes in v2:
time: 164 us; the launch traced here: 163 us
  starting transfers between devices  55 us (34%)
  Pallas kernels  48.3 us (29%)
  local copies, waits for them, and re-layouts  27.5 us (17%)
  waiting for transfers between devices  21.2 us (13%)
  other arithmetic  6.36 us (4%)
  matrix products  2.57 us (2%)
    ppermute x7, waiting for transfers between devices, chip_exchange(): block = lax.ppermute(block, CHIPS, perm)  19 us
    ppermute x7, starting transfers between devices, dp_sum(): got = lax.ppermute(sent, 'z', [(i, (i + step) % nz) for i in range(nz)])  18.4 us
    unnamed x63, local copies, waits for them, and re-layouts  17.4 us
    ppermute x7, starting transfers between devices, chip_exchange(): block = lax.ppermute(block, CHIPS, perm)  16.6 us
    pallas_call x1, Pallas kernels, donor_rows(): pl.pallas_call(donor_kernel, grid=(groups,), in_specs=[pl.BlockSpec((1, 2...  10.9 us
    all_to_all x1, starting transfers between devices, on_device(): pieces = lax.all_to_all(chip_half, CHIPS, 0, 0, tiled=True)  9.23 us
    pallas_call x2, Pallas kernels, grad_half(): pl.pallas_call(functools.partial(grad_kernel, add=other is not None), gri...  8.19 us
    pallas_call x1, Pallas kernels, conv_edges(): pl.pallas_call(functools.partial(edge_kernel, rows=rows), grid=(2,), in_s...  7.72 us
  transfers between devices with their start and end apart: 21, of which 5 were waited for; matrix products, arithmetic and copies ran while one was open for 14% of the time, Pallas kernels for 14%

profile of v2, /device:TPU:2, one launch (start us, length us, event | category | flops | bytes accessed | tf_op | source)
XLA Modules:
  0.0 162.5 jit_solution(12828128114348193947)
XLA Ops:
  0.6 0.8 broadcast_in_dim.14.gain_ref
  1.4 1.4 copy-done.2
  2.8 0.7 copy-done.15
  3.5 0.7 copy-done.17
  4.2 1.5 shard_map.122.left_ref.mid_ref.right_ref.all_ref.near_ref
  5.7 0.9 fusion.24
  6.7 1.9 %collective-permute-start.1 = (bf16[256,768]{1,0:T(8,128)(2,1)}, bf16[256,768]{1,0:T(8,128)(2,1)S(1)}, u32[]{:S(2)}, u32[]{:S(2)}) collective-permute-start(bf16[256,768]{1,0:T(8,128)(2,1)} %get-tuple-element.32), channel_id=1, source_target_pairs={{1,0},{2,1},{3,2},{4,3},{5,4},{6,5},{7,6},{8,7},{9,8},{10,9},{11,1... | collective-permute-start | bytes 1179656 | tf_op jit(solution)/shard_map/ppermute | solution.py:365
  8.6 2.4 %collective-permute-start = (bf16[256,768]{1,0:T(8,128)(2,1)}, bf16[256,768]{1,0:T(8,128)(2,1)S(1)}, u32[]{:S(2)}, u32[]{:S(2)}) collective-permute-start(bf16[256,768]{1,0:T(8,128)(2,1)} %get-tuple-element.33), channel_id=1, source_target_pairs={{0,1},{1,2},{2,3},{3,4},{4,5},{5,6},{6,7},{7,8},{8,9},{9,10},{10,1... | collective-permute-start | bytes 1179656 | tf_op jit(solution)/shard_map/ppermute | solution.py:364
  11.0 6.5 %shard_map.123 = (bf16[1024,768]{1,0:T(8,128)(2,1)S(1)}, bf16[1024,768]{1,0:T(8,128)(2,1)S(1)}, bf16[8,2,48,1024]{3,2,1,0:T(8,128)(2,1)S(1)}) custom-call(bf16[1024,768]{1,0:T(8,128)(2,1)} %copy-done.1, bf16[1024,768]{1,0:T(8,128)(2,1)} %copy-done.1, bf16[1024,768]{1,0:T(8,128)(2,1)} %copy-done.1, bf16[2304,768]{1,0:T(8,128)(2,1)} %bitcast.86, ...), custom_call_target="tpu_custom_call" | custom-call | flops 1811939328 | bytes 6291456 | tf_op jit(solution)/shard_map/pallas_call | solution.py:135
  17.6 0.8 copy-done.11
  18.4 0.2 collective-permute-done.low_ref
  18.5 0.8 copy-done.13
  19.3 1.0 copy-done.12
  20.3 1.0 copy-done.14
  21.3 7.7 %shard_map.124 = (bf16[1024,768]{1,0:T(8,128)(2,1)S(1)}, bf16[1024,768]{1,0:T(8,128)(2,1)S(1)}, bf16[8,2,48,256]{3,2,1,0:T(8,128)(2,1)S(1)}, bf16[8,2,48,256]{3,2,1,0:T(8,128)(2,1)S(1)}) custom-call(bf16[256,768]{1,0:T(8,128)(2,1)S(1)} %copy-done.14, bf16[256,768]{1,0:T(8,128)(2,1)S(1)} %copy-done.12, ...), custom_call_target="tpu_custom_call", output_to_operand_aliasing={{0}: (9, {}), {1}: (10, {})} | custom-call | flops 1811939328 | bytes 6291456 | tf_op jit(solution)/shard_map/pallas_call | solution.py:168
  29.0 1.2 copy-done.8
  30.2 3.4 %shard_map.125 = bf16[8,3,48,768]{3,2,1,0:T(8,128)(2,1)} custom-call(s32[1]{0:T(128)} %bitcast.8.half_ref, bf16[8,2,48,1024]{3,2,1,0:T(8,128)(2,1)S(1)} %get-tuple-element.20.turned_ref, bf16[8,2,48,256]{3,2,1,0:T(8,128)(2,1)S(1)} %get-tuple-element.21.low_ref, bf16[8,2,48,256]{3,2,1,0:T(8,128)(2,1)S(1)} %get-tuple-element.22.high_ref, ...), custom_call_target="tpu_custom_call" | custom-call | flops 1811939328 | bytes 4718592 | tf_op jit(solution)/shard_map/pallas_call | solution.py:241
  33.6 0.9 collective-permute-start.2
  34.6 0.6 fusion.25
  35.9 2.6 %convolution_convert_fusion.own_ref = bf16[1024,768]{1,0:T(8,128)(2,1)} fusion(bf16[1024,768]{1,0:T(8,128)(2,1)S(1)} %copy-done.9, bf16[768,768]{1,0:T(8,128)(2,1)S(1)} %copy-done), kind=kOutput, calls=%fused_computation.1 | convolution fusion | flops 1208745984 | bytes 4325376 | tf_op jit(solution)/shard_map/dot_general | solution.py:438
  38.5 4.8 %shard_map.126 = bf16[8,3,48,768]{3,2,1,0:T(8,128)(2,1)} custom-call(s32[1]{0:T(128)} %bitcast.half_ref.core_ref, bf16[8,2,48,1024]{3,2,1,0:T(8,128)(2,1)S(1)} %copy-done.7, bf16[8,2,48,256]{3,2,1,0:T(8,128)(2,1)S(1)} %get-tuple-element.21.low_ref, bf16[8,2,48,256]{3,2,1,0:T(8,128)(2,1)S(1)} %get-tuple-element.22.high_ref, bf16[1024,768]{1,0:T(8,128)(2,1)S(1)} %copy-done.4, ...), custom_call_target="tpu_custom_call" | custom-call | flops 1811939328 | bytes 4718592 | tf_op jit(solution)/shard_map/pallas_call | solution.py:241
  43.3 9.2 %all-to-all-start = ((bf16[8,3,48,768]{3,2,1,0:T(8,128)(2,1)}), bf16[8,3,48,768]{3,2,1,0:T(8,128)(2,1)}, u32[]{:S(2)}, u32[]{:S(2)}) async-start(bf16[8,3,48,768]{3,2,1,0:T(8,128)(2,1)} %shard_map.126), calls=%async_computation | async-start | bytes 3538944 | tf_op jit(solution)/shard_map/all_to_all | solution.py:444
  52.5 3.0 %collective-permute-start.9 = (s32[2,128]{1,0:T(2,128)S(1)}, s32[2,128]{1,0:T(2,128)S(1)}, u32[]{:S(2)}, u32[]{:S(2)}) collective-permute-start(s32[2,128]{1,0:T(2,128)S(1)} %get-tuple-element.41), channel_id=1, source_target_pairs={{0,14},{2,8},{4,10},{6,12},{8,6},{10,0},{12,2},{14,4},{1,15},{3,9}... | collective-permute-start | bytes 3080 | tf_op jit(solution)/shard_map/ppermute | solution.py:381
  55.6 1.5 collective-permute-start.3
  57.1 3.3 %collective-permute-start.4 = (s32[2,128]{1,0:T(2,128)S(1)}, s32[2,128]{1,0:T(2,128)S(1)}, u32[]{:S(2)}, u32[]{:S(2)}) collective-permute-start(s32[2,128]{1,0:T(2,128)S(1)} %get-tuple-element.44), channel_id=1, source_target_pairs={{0,4},{2,6},{4,0},{6,2},{8,12},{10,14},{12,8},{14,10},{1,5},{3,7},... | collective-permute-start | bytes 3080 | tf_op jit(solution)/shard_map/ppermute | solution.py:381
  60.3 0.3 collective-permute-start.5
  60.6 13.3 %collective-permute-done.3 = s32[2,128]{1,0:T(2,128)S(1)} collective-permute-done((s32[2,128]{1,0:T(2,128)S(1)}, s32[2,128]{1,0:T(2,128)S(1)}, u32[]{:S(2)}, u32[]{:S(2)}) %collective-permute-start.3) | collective-permute-done | bytes 1056 | tf_op jit(solution)/shard_map/ppermute | solution.py:381
  73.9 3.0 %collective-permute-start.6 = (s32[2,128]{1,0:T(2,128)S(1)}, s32[2,128]{1,0:T(2,128)S(1)}, u32[]{:S(2)}, u32[]{:S(2)}) collective-permute-start(s32[2,128]{1,0:T(2,128)S(1)} %get-tuple-element.46), channel_id=1, source_target_pairs={{0,8},{2,10},{4,12},{6,14},{8,0},{10,2},{12,4},{14,6},{1,9},{3,11}... | collective-permute-start | bytes 3080 | tf_op jit(solution)/shard_map/ppermute | solution.py:381
  76.9 5.2 %collective-permute-start.8 = (s32[2,128]{1,0:T(2,128)S(1)}, s32[2,128]{1,0:T(2,128)S(1)}, u32[]{:S(2)}, u32[]{:S(2)}) collective-permute-start(s32[2,128]{1,0:T(2,128)S(1)} %get-tuple-element.47), channel_id=1, source_target_pairs={{0,12},{2,14},{4,8},{6,10},{8,4},{10,6},{12,0},{14,2},{1,13},{3,15... | collective-permute-start | bytes 3080 | tf_op jit(solution)/shard_map/ppermute | solution.py:381
  82.2 0.3 collective-permute-start.7
  82.5 5.6 %collective-permute-done.7 = s32[2,128]{1,0:T(2,128)S(1)} collective-permute-done((s32[2,128]{1,0:T(2,128)S(1)}, s32[2,128]{1,0:T(2,128)S(1)}, u32[]{:S(2)}, u32[]{:S(2)}) %collective-permute-start.7) | collective-permute-done | bytes 1056 | tf_op jit(solution)/shard_map/ppermute | solution.py:381
  88.2 5.9 %shard_map.128 = bf16[8,3,64,768]{3,2,1,0:T(8,128)(2,1)S(1)} custom-call(s32[1]{0:T(128)} %bitcast.10.hot_ref, s32[8]{0:T(128)S(1)} %fusion.22.place_ref, s32[8,2,128]{2,1,0:T(2,128)S(1)} %constant_dynamic-update-slice_fusion.index_ref, bf16[1024,768]{1,0:T(8,128)(2,1)S(1)} %copy-done.20, bf16[1024,768]{1,0:T(8,128)(2,1)S(1)} %collective-permute-done.10.other_ref), custom_call_target="tpu_custom_call" | custom-call | flops 3221225472 | bytes 6291456 | tf_op jit(solution)/shard_map/pallas_call | solution.py:283
  94.1 1.4 copy-done.5
  95.5 3.9 %all-to-all-start.1 = ((bf16[8,3,64,768]{3,2,1,0:T(8,128)(2,1)}), bf16[8,3,64,768]{3,2,1,0:T(8,128)(2,1)S(1)}, u32[]{:S(2)}, u32[]{:S(2)}) async-start(bf16[8,3,64,768]{3,2,1,0:T(8,128)(2,1)} %copy-done.5), calls=%async_computation.1 | async-start | bytes 4718592 | tf_op jit(solution)/shard_map/all_to_all | solution.py:459
  99.4 2.5 %convert_reduce_fusion = f32[3,48,768]{2,1,0:T(8,128)} fusion(bf16[8,3,48,768]{3,2,1,0:T(8,128)(2,1)} %all-to-all-done), kind=kLoop, calls=%fused_computation | loop fusion | flops 1658880 | bytes 2211840 | tf_op jit(solution)/shard_map/reduce_sum | solution.py:461
  102.0 2.1 %reshape.39 = f32[8,96,144]{1,0,2:T(8,128)} reshape(f32[768,144]{0,1:T(8,128)} %bitcast.91) | data formatting | bytes 884736 | tf_op jit(solution)/shard_map/reshape | solution.py:391
  104.1 1.1 convert_element_type.48
  105.2 1.2 constant_dynamic-slice_fusion.6
  106.4 0.6 copy.38
  107.0 3.3 %collective-permute-start.12 = (bf16[96,144]{0,1:T(8,128)(2,1)}, bf16[96,144]{0,1:T(8,128)(2,1)}, u32[]{:S(2)}, u32[]{:S(2)}) collective-permute-start(bf16[96,144]{0,1:T(8,128)(2,1)} %bitcast.76), channel_id=1, source_target_pairs={{0,64},{32,96},{64,128},{96,160},{128,192},{160,224},{192,0},{224,... | collective-permute-start | bytes 82952 | tf_op jit(solution)/shard_map/ppermute | solution.py:396
  110.3 0.6 copy.37
  111.0 4.9 %collective-permute-start.13 = (bf16[96,144]{0,1:T(8,128)(2,1)}, bf16[96,144]{0,1:T(8,128)(2,1)}, u32[]{:S(2)}, u32[]{:S(2)}) collective-permute-start(bf16[96,144]{0,1:T(8,128)(2,1)} %bitcast.75), channel_id=1, source_target_pairs={{0,96},{32,128},{64,160},{96,192},{128,224},{160,0},{192,32},{224,... | collective-permute-start | bytes 82952 | tf_op jit(solution)/shard_map/ppermute | solution.py:396
  115.9 0.9 copy.39
  116.8 0.9 copy.33
  117.7 0.9 copy.34
  118.5 0.9 copy.35
  119.4 0.9 copy.36
  120.3 0.9 collective-permute-start.14
  121.2 4.6 %collective-permute-start.15 = (bf16[96,144]{0,1:T(8,128)(2,1)S(1)}, bf16[96,144]{0,1:T(8,128)(2,1)S(1)}, u32[]{:S(2)}, u32[]{:S(2)}) collective-permute-start(bf16[96,144]{0,1:T(8,128)(2,1)S(1)} %bitcast.99), channel_id=1, source_target_pairs={{0,160},{32,192},{64,224},{96,0},{128,32},{160,64},{192,96},{224,1... | collective-permute-start | bytes 82952 | tf_op jit(solution)/shard_map/ppermute | solution.py:396
  125.8 2.6 %collective-permute-start.16 = (bf16[96,144]{0,1:T(8,128)(2,1)S(1)}, bf16[96,144]{0,1:T(8,128)(2,1)S(1)}, u32[]{:S(2)}, u32[]{:S(2)}) collective-permute-start(bf16[96,144]{0,1:T(8,128)(2,1)S(1)} %bitcast.98), channel_id=1, source_target_pairs={{0,192},{32,224},{64,0},{96,32},{128,64},{160,96},{192,128},{224,1... | collective-permute-start | bytes 82952 | tf_op jit(solution)/shard_map/ppermute | solution.py:396
  128.5 2.0 %collective-permute-start.11 = (bf16[96,144]{0,1:T(8,128)(2,1)S(1)}, bf16[96,144]{0,1:T(8,128)(2,1)S(1)}, u32[]{:S(2)}, u32[]{:S(2)}) collective-permute-start(bf16[96,144]{0,1:T(8,128)(2,1)S(1)} %bitcast.96), channel_id=1, source_target_pairs={{0,32},{32,64},{64,96},{96,128},{128,160},{160,192},{192,224},{224... | collective-permute-start | bytes 82952 | tf_op jit(solution)/shard_map/ppermute | solution.py:396
  130.5 1.1 constant_dynamic-slice_fusion.7
  131.7 0.8 collective-permute-done.17
  132.4 1.3 collective-permute-done.11
  133.7 1.5 convert_add_fusion
  135.2 1.6 copy.17
  136.8 0.8 fusion
  137.6 1.6 collective-permute-start.18
  139.2 1.4 copy-done.10
  140.6 1.3 copy-done.21
  141.9 10.9 %shard_map.127.donor_ref = f32[2048,768]{1,0:T(8,128)} custom-call(s32[8,2,128]{2,1,0:T(2,128)S(1)} %bitcast.85, bf16[1024,768]{1,0:T(8,128)(2,1)S(1)} %copy-done.10, bf16[768,768]{1,0:T(8,128)(2,1)S(1)} %copy-done.21), custom_call_target="tpu_custom_call" | custom-call | flops 5637144576 | bytes 7864320 | tf_op jit(solution)/shard_map/pallas_call | solution.py:311
  152.8 0.6 bitcast_add_fusion
  153.4 1.5 copy.18
  155.0 7.6 %shard_map.129 = bf16[2048,768]{1,0:T(8,128)(2,1)} custom-call(s32[1]{0:T(128)} %bitcast.half_ref.core_ref, s32[16]{0:T(128)S(1)} %bitcast.84, f32[2048,768]{1,0:T(8,128)} %shard_map.127.donor_ref, bf16[8,3,64,768]{3,2,1,0:T(8,128)(2,1)S(1)} %all-to-all-done.1.accepted_ref), custom_call_target="tpu_custom_call" | custom-call | flops 3145728 | bytes 12582912 | tf_op jit(solution)/shard_map/pallas_call | solution.py:343
  (68 shorter events, 0.2 us)
Async XLA Ops:
  0.6 35.2 %copy-start = (bf16[768,768]{1,0:T(8,128)(2,1)S(1)}, bf16[768,768]{1,0:T(8,128)(2,1)}, u32[]{:S(2)}) copy-start(bf16[768,768]{1,0:T(8,128)(2,1)} %param.21) | copy-start | bytes 3538948
  1.4 1.4 copy-start.2
  2.8 0.7 copy-start.15
  3.5 0.7 copy-start.17
  5.7 5.3 %copy-start.1 = (bf16[1024,768]{1,0:T(8,128)(2,1)}, bf16[1024,768]{1,0:T(8,128)(2,1)S(1)}, u32[]{:S(2)}) copy-start(bf16[1024,768]{1,0:T(8,128)(2,1)S(1)} %shard_map.122.left_ref.mid_ref.right_ref.all_ref.near_ref) | copy-start | bytes 4718596
  5.7 5.3 %copy-start.16 = (f32[4,768]{1,0:T(4,128)S(1)}, f32[4,768]{1,0:T(4,128)}, u32[]{:S(2)}) copy-start(f32[4,768]{1,0:T(4,128)} %table_ref.5) | copy-start | bytes 36868
  5.7 5.3 %copy-start.18 = (s32[1,1024]{1,0:T(1,128)S(1)}, s32[1,1024]{1,0:T(1,128)}, u32[]{:S(2)}) copy-start(s32[1,1024]{1,0:T(1,128)} %param.12) | copy-start | bytes 12292
  6.7 10.9 %collective-permute-start.1 = (bf16[256,768]{1,0:T(8,128)(2,1)}, bf16[256,768]{1,0:T(8,128)(2,1)S(1)}, u32[]{:S(2)}, u32[]{:S(2)}) collective-permute-start(bf16[256,768]{1,0:T(8,128)(2,1)} %get-tuple-element.32), channel_id=1, source_target_pairs={{1,0},{2,1},{3,2},{4,3},{5,4},{6,5},{7,6},{8,7},{9,8},{10,9},{11,1... | collective-permute-start | bytes 1179656 | tf_op jit(solution)/shard_map/ppermute | solution.py:365
  8.6 9.9 %collective-permute-start = (bf16[256,768]{1,0:T(8,128)(2,1)}, bf16[256,768]{1,0:T(8,128)(2,1)S(1)}, u32[]{:S(2)}, u32[]{:S(2)}) collective-permute-start(bf16[256,768]{1,0:T(8,128)(2,1)} %get-tuple-element.33), channel_id=1, source_target_pairs={{0,1},{1,2},{2,3},{3,4},{4,5},{5,6},{6,7},{7,8},{8,9},{9,10},{10,1... | collective-permute-start | bytes 1179656 | tf_op jit(solution)/shard_map/ppermute | solution.py:364
  17.6 12.6 %copy-start.6 = (bf16[8,2,48,1024]{3,2,1,0:T(8,128)(2,1)}, bf16[8,2,48,1024]{3,2,1,0:T(8,128)(2,1)S(1)}, u32[]{:S(2)}) copy-start(bf16[8,2,48,1024]{3,2,1,0:T(8,128)(2,1)S(1)} %get-tuple-element.20.turned_ref) | copy-start | bytes 4718596
  17.6 0.8 copy-start.11
  18.5 0.8 copy-start.13
  19.3 1.0 copy-start.12
  20.3 1.0 copy-start.14
  29.0 1.2 copy-start.8
  30.2 3.4 %copy-start.3 = (bf16[1024,768]{1,0:T(8,128)(2,1)}, bf16[1024,768]{1,0:T(8,128)(2,1)S(1)}, u32[]{:S(2)}) copy-start(bf16[1024,768]{1,0:T(8,128)(2,1)S(1)} %get-tuple-element.23.dconv_ref) | copy-start | bytes 4718596
  30.2 4.4 %copy-start.19 = (s32[1,16]{1,0:T(1,128)S(1)}, s32[1,16]{1,0:T(1,128)}, u32[]{:S(2)}) copy-start(s32[1,16]{1,0:T(1,128)} %param.19) | copy-start | bytes 196
  30.2 5.7 %copy-start.9 = (bf16[1024,768]{1,0:T(8,128)(2,1)S(1)}, bf16[1024,768]{1,0:T(8,128)(2,1)}, u32[]{:S(2)}) copy-start(bf16[1024,768]{1,0:T(8,128)(2,1)} %copy-done.8) | copy-start | bytes 4718596
  33.6 4.9 %collective-permute-start.2 = (bf16[8,3,48,768]{3,2,1,0:T(8,128)(2,1)}, bf16[8,3,48,768]{3,2,1,0:T(8,128)(2,1)}, u32[]{:S(2)}, u32[]{:S(2)}) collective-permute-start(bf16[8,3,48,768]{3,2,1,0:T(8,128)(2,1)} %shard_map.125), channel_id=1, source_target_pairs={{0,1},{1,0},{2,3},{3,2},{4,5},{5,4},{6,7},{7,6},{8,9},{9,8},{10,11... | collective-permute-start | bytes 5308424 | tf_op jit(solution)/shard_map/ppermute | solution.py:437
  35.9 2.6 %copy-start.4 = (bf16[1024,768]{1,0:T(8,128)(2,1)S(1)}, bf16[1024,768]{1,0:T(8,128)(2,1)}, u32[]{:S(2)}) copy-start(bf16[1024,768]{1,0:T(8,128)(2,1)} %copy-done.3) | copy-start | bytes 4718596
  35.9 2.6 %copy-start.7 = (bf16[8,2,48,1024]{3,2,1,0:T(8,128)(2,1)S(1)}, bf16[8,2,48,1024]{3,2,1,0:T(8,128)(2,1)}, u32[]{:S(2)}) copy-start(bf16[8,2,48,1024]{3,2,1,0:T(8,128)(2,1)} %copy-done.6) | copy-start | bytes 4718596
  43.3 9.2 %copy-start.24 = (s32[1,2048]{1,0:T(1,128)S(1)}, s32[1,2048]{1,0:T(1,128)}, u32[]{:S(2)}) copy-start(s32[1,2048]{1,0:T(1,128)} %param.18) | copy-start | bytes 24580
  43.3 17.3 %copy-start.20 = (bf16[1024,768]{1,0:T(8,128)(2,1)S(1)}, bf16[1024,768]{1,0:T(8,128)(2,1)}, u32[]{:S(2)}) copy-start(bf16[1024,768]{1,0:T(8,128)(2,1)} %convolution_convert_fusion.own_ref) | copy-start | bytes 4718596
  43.3 52.2 %all-to-all-start = ((bf16[8,3,48,768]{3,2,1,0:T(8,128)(2,1)}), bf16[8,3,48,768]{3,2,1,0:T(8,128)(2,1)}, u32[]{:S(2)}, u32[]{:S(2)}) async-start(bf16[8,3,48,768]{3,2,1,0:T(8,128)(2,1)} %shard_map.126), calls=%async_computation | async-start | bytes 3538944 | tf_op jit(solution)/shard_map/all_to_all | solution.py:444
  52.5 35.6 %collective-permute-start.9 = (s32[2,128]{1,0:T(2,128)S(1)}, s32[2,128]{1,0:T(2,128)S(1)}, u32[]{:S(2)}, u32[]{:S(2)}) collective-permute-start(s32[2,128]{1,0:T(2,128)S(1)} %get-tuple-element.41), channel_id=1, source_target_pairs={{0,14},{2,8},{4,10},{6,12},{8,6},{10,0},{12,2},{14,4},{1,15},{3,9}... | collective-permute-start | bytes 3080 | tf_op jit(solution)/shard_map/ppermute | solution.py:381
  55.6 18.3 %collective-permute-start.3 = (s32[2,128]{1,0:T(2,128)S(1)}, s32[2,128]{1,0:T(2,128)S(1)}, u32[]{:S(2)}, u32[]{:S(2)}) collective-permute-start(s32[2,128]{1,0:T(2,128)S(1)} %get-tuple-element.43), channel_id=1, source_target_pairs={{0,2},{2,4},{4,6},{6,0},{8,10},{10,12},{12,14},{14,8},{1,3},{3,5},... | collective-permute-start | bytes 3080 | tf_op jit(solution)/shard_map/ppermute | solution.py:381
  57.1 19.9 %collective-permute-start.4 = (s32[2,128]{1,0:T(2,128)S(1)}, s32[2,128]{1,0:T(2,128)S(1)}, u32[]{:S(2)}, u32[]{:S(2)}) collective-permute-start(s32[2,128]{1,0:T(2,128)S(1)} %get-tuple-element.44), channel_id=1, source_target_pairs={{0,4},{2,6},{4,0},{6,2},{8,12},{10,14},{12,8},{14,10},{1,5},{3,7},... | collective-permute-start | bytes 3080 | tf_op jit(solution)/shard_map/ppermute | solution.py:381
  60.3 21.8 %collective-permute-start.5 = (s32[2,128]{1,0:T(2,128)S(1)}, s32[2,128]{1,0:T(2,128)S(1)}, u32[]{:S(2)}, u32[]{:S(2)}) collective-permute-start(s32[2,128]{1,0:T(2,128)S(1)} %get-tuple-element.45), channel_id=1, source_target_pairs={{0,6},{2,0},{4,2},{6,4},{8,14},{10,8},{12,10},{14,12},{1,7},{3,1},... | collective-permute-start | bytes 3080 | tf_op jit(solution)/shard_map/ppermute | solution.py:381
  60.6 27.6 %collective-permute-start.10 = (bf16[1024,768]{1,0:T(8,128)(2,1)S(1)}, bf16[1024,768]{1,0:T(8,128)(2,1)S(1)}, u32[]{:S(2)}, u32[]{:S(2)}) collective-permute-start(bf16[1024,768]{1,0:T(8,128)(2,1)S(1)} %copy-done.20), channel_id=1, source_target_pairs={{0,1},{1,0},{2,3},{3,2},{4,5},{5,4},{6,7},{7,6},{8,9},{9,8},{10,11... | collective-permute-start | bytes 4718600 | tf_op jit(solution)/shard_map/ppermute | solution.py:446
  73.9 8.6 %collective-permute-start.6 = (s32[2,128]{1,0:T(2,128)S(1)}, s32[2,128]{1,0:T(2,128)S(1)}, u32[]{:S(2)}, u32[]{:S(2)}) collective-permute-start(s32[2,128]{1,0:T(2,128)S(1)} %get-tuple-element.46), channel_id=1, source_target_pairs={{0,8},{2,10},{4,12},{6,14},{8,0},{10,2},{12,4},{14,6},{1,9},{3,11}... | collective-permute-start | bytes 3080 | tf_op jit(solution)/shard_map/ppermute | solution.py:381
  76.9 11.2 %collective-permute-start.8 = (s32[2,128]{1,0:T(2,128)S(1)}, s32[2,128]{1,0:T(2,128)S(1)}, u32[]{:S(2)}, u32[]{:S(2)}) collective-permute-start(s32[2,128]{1,0:T(2,128)S(1)} %get-tuple-element.47), channel_id=1, source_target_pairs={{0,12},{2,14},{4,8},{6,10},{8,4},{10,6},{12,0},{14,2},{1,13},{3,15... | collective-permute-start | bytes 3080 | tf_op jit(solution)/shard_map/ppermute | solution.py:381
  82.2 6.0 %collective-permute-start.7 = (s32[2,128]{1,0:T(2,128)S(1)}, s32[2,128]{1,0:T(2,128)S(1)}, u32[]{:S(2)}, u32[]{:S(2)}) collective-permute-start(s32[2,128]{1,0:T(2,128)S(1)} %get-tuple-element.48), channel_id=1, source_target_pairs={{0,10},{2,12},{4,14},{6,8},{8,2},{10,4},{12,6},{14,0},{1,11},{3,13... | collective-permute-start | bytes 3080 | tf_op jit(solution)/shard_map/ppermute | solution.py:381
  94.1 1.4 copy-start.5
  95.5 59.5 %all-to-all-start.1 = ((bf16[8,3,64,768]{3,2,1,0:T(8,128)(2,1)}), bf16[8,3,64,768]{3,2,1,0:T(8,128)(2,1)S(1)}, u32[]{:S(2)}, u32[]{:S(2)}) async-start(bf16[8,3,64,768]{3,2,1,0:T(8,128)(2,1)} %copy-done.5), calls=%async_computation.1 | async-start | bytes 4718592 | tf_op jit(solution)/shard_map/all_to_all | solution.py:459
  104.1 35.1 %copy-start.22 = (s32[1,2048]{1,0:T(1,128)S(1)}, s32[1,2048]{1,0:T(1,128)}, u32[]{:S(2)}) copy-start(s32[1,2048]{1,0:T(1,128)} %param.17) | copy-start | bytes 24580
  107.0 21.4 %collective-permute-start.12 = (bf16[96,144]{0,1:T(8,128)(2,1)}, bf16[96,144]{0,1:T(8,128)(2,1)}, u32[]{:S(2)}, u32[]{:S(2)}) collective-permute-start(bf16[96,144]{0,1:T(8,128)(2,1)} %bitcast.76), channel_id=1, source_target_pairs={{0,64},{32,96},{64,128},{96,160},{128,192},{160,224},{192,0},{224,... | collective-permute-start | bytes 82952 | tf_op jit(solution)/shard_map/ppermute | solution.py:396
  111.0 17.5 %collective-permute-start.13 = (bf16[96,144]{0,1:T(8,128)(2,1)}, bf16[96,144]{0,1:T(8,128)(2,1)}, u32[]{:S(2)}, u32[]{:S(2)}) collective-permute-start(bf16[96,144]{0,1:T(8,128)(2,1)} %bitcast.75), channel_id=1, source_target_pairs={{0,96},{32,128},{64,160},{96,192},{128,224},{160,0},{192,32},{224,... | collective-permute-start | bytes 82952 | tf_op jit(solution)/shard_map/ppermute | solution.py:396
  120.3 11.3 %collective-permute-start.14 = (bf16[96,144]{0,1:T(8,128)(2,1)S(1)}, bf16[96,144]{0,1:T(8,128)(2,1)S(1)}, u32[]{:S(2)}, u32[]{:S(2)}) collective-permute-start(bf16[96,144]{0,1:T(8,128)(2,1)S(1)} %bitcast.100), channel_id=1, source_target_pairs={{0,128},{32,160},{64,192},{96,224},{128,0},{160,32},{192,64},{224,... | collective-permute-start | bytes 82952 | tf_op jit(solution)/shard_map/ppermute | solution.py:396
  121.2 10.4 %collective-permute-start.15 = (bf16[96,144]{0,1:T(8,128)(2,1)S(1)}, bf16[96,144]{0,1:T(8,128)(2,1)S(1)}, u32[]{:S(2)}, u32[]{:S(2)}) collective-permute-start(bf16[96,144]{0,1:T(8,128)(2,1)S(1)} %bitcast.99), channel_id=1, source_target_pairs={{0,160},{32,192},{64,224},{96,0},{128,32},{160,64},{192,96},{224,1... | collective-permute-start | bytes 82952 | tf_op jit(solution)/shard_map/ppermute | solution.py:396
  125.8 5.8 %collective-permute-start.16 = (bf16[96,144]{0,1:T(8,128)(2,1)S(1)}, bf16[96,144]{0,1:T(8,128)(2,1)S(1)}, u32[]{:S(2)}, u32[]{:S(2)}) collective-permute-start(bf16[96,144]{0,1:T(8,128)(2,1)S(1)} %bitcast.98), channel_id=1, source_target_pairs={{0,192},{32,224},{64,0},{96,32},{128,64},{160,96},{192,128},{224,1... | collective-permute-start | bytes 82952 | tf_op jit(solution)/shard_map/ppermute | solution.py:396
  128.5 4.0 %collective-permute-start.17 = (bf16[96,144]{0,1:T(8,128)(2,1)S(1)}, bf16[96,144]{0,1:T(8,128)(2,1)S(1)}, u32[]{:S(2)}, u32[]{:S(2)}) collective-permute-start(bf16[96,144]{0,1:T(8,128)(2,1)S(1)} %bitcast.97), channel_id=1, source_target_pairs={{0,224},{32,0},{64,32},{96,64},{128,96},{160,128},{192,160},{224,1... | collective-permute-start | bytes 82952 | tf_op jit(solution)/shard_map/ppermute | solution.py:396
  128.5 5.2 %collective-permute-start.11 = (bf16[96,144]{0,1:T(8,128)(2,1)S(1)}, bf16[96,144]{0,1:T(8,128)(2,1)S(1)}, u32[]{:S(2)}, u32[]{:S(2)}) collective-permute-start(bf16[96,144]{0,1:T(8,128)(2,1)S(1)} %bitcast.96), channel_id=1, source_target_pairs={{0,32},{32,64},{64,96},{96,128},{128,160},{160,192},{192,224},{224... | collective-permute-start | bytes 82952 | tf_op jit(solution)/shard_map/ppermute | solution.py:396
  137.6 15.2 %collective-permute-start.18 = (bf16[48,144]{1,0:T(8,128)(2,1)S(1)}, bf16[48,144]{1,0:T(8,128)(2,1)S(1)}, u32[]{:S(2)}, u32[]{:S(2)}) collective-permute-start(bf16[48,144]{1,0:T(8,128)(2,1)S(1)} %fusion), channel_id=1, source_target_pairs={{0,16},{16,0},{1,17},{17,1},{2,18},{18,2},{3,19},{19,3},{4,20},{20... | collective-permute-start | bytes 41480 | tf_op jit(solution)/shard_map/ppermute | solution.py:401
  139.2 1.4 copy-start.10
  140.6 1.3 copy-start.21
  141.9 10.9 %copy-start.23 = (f32[96,144]{1,0:T(8,128)S(1)}, f32[96,144]{1,0:T(8,128)}, u32[]{:S(2)}) copy-start(f32[96,144]{1,0:T(8,128)} %copy.17) | copy-start | bytes 165892

commit v3 on v1

v3 whole, which is shorter than its diff:
```python
import functools

import jax
import jax.numpy as jnp
from jax import lax
from jax.experimental import pallas as pl
from jax.experimental.pallas import tpu as pltpu
from jax.sharding import Mesh, PartitionSpec as P

DILATION_STEP = 256
AXES = ("z", "yl", "yh", "x", "core")
DP = ("z", "yl")
SEQ = ("yh", "x", "core")
CHIPS = ("yh", "x")
LANES = 128
MIB = 1024 * 1024
TILE = 256
BF16 = jnp.bfloat16
F32 = jnp.float32
GELU_A = 0.7978845608028654
GELU_B = 0.044715


def params(mib):
    return pltpu.CompilerParams(vmem_limit_bytes=mib * MIB)


def cost(flops, nbytes):
    return pl.CostEstimate(flops=flops, bytes_accessed=nbytes, transcendentals=0)


def in_hbm(x):
    return pltpu.with_memory_space_constraint(x, pltpu.HBM)


def dot(a, b):
    return jnp.dot(a, b, preferred_element_type=F32)


def across_lanes(row):
    return jnp.transpose(jnp.broadcast_to(row, (LANES, LANES)))


def summed_inputs(trunk, ids_ref, first, table_ref):
    rows, width = trunk.shape
    parts = []
    for block in range(rows // LANES):
        ids = across_lanes(ids_ref[pl.ds(first + block, 1), :])
        ids = jnp.concatenate([ids] * (width // LANES), axis=1)
        embedded = jnp.where(
            ids < 2,
            jnp.where(ids == 0, table_ref[0:1, :], table_ref[1:2, :]),
            jnp.where(ids == 2, table_ref[2:3, :], table_ref[3:4, :]),
        )
        parts.append(trunk[block * LANES : (block + 1) * LANES].astype(F32) + embedded)
    return jnp.concatenate(parts, axis=0)


def norm_kernel(core_ref, trunk_ref, ids_ref, table_ref, gain_ref, out_ref, near_ref, far_ref):
    i = pl.program_id(0)
    last = pl.num_programs(0) - 1
    per_chunk = trunk_ref.shape[0] // LANES
    inputs = summed_inputs(trunk_ref[...], ids_ref, i * per_chunk, table_ref)
    mean = jnp.mean(inputs * inputs, axis=-1, keepdims=True)
    normed = (inputs * lax.rsqrt(mean + 1e-06) * gain_ref[...][None, :]).astype(BF16)
    out_ref[...] = normed

    @pl.when(i == jnp.where(core_ref[0] == 0, last, 0))
    def _():
        near_ref[...] = normed

    @pl.when(i == jnp.where(core_ref[0] == 0, 0, last))
    def _():
        far_ref[...] = normed


def norm_rows(core, trunk, ids, table, gain):
    length, width = trunk.shape
    chunk = DILATION_STEP
    whole = lambda i, c: (0, 0)
    edge = jax.ShapeDtypeStruct((chunk, width), BF16)
    return pl.pallas_call(
        norm_kernel,
        grid_spec=pltpu.PrefetchScalarGridSpec(
            num_scalar_prefetch=1,
            grid=(length // chunk,),
            in_specs=[
                pl.BlockSpec((chunk, width), lambda i, c: (i, 0)),
                pl.BlockSpec(ids.shape, whole),
                pl.BlockSpec(table.shape, whole),
                pl.BlockSpec(gain.shape, lambda i, c: (0,)),
            ],
            out_specs=[
                pl.BlockSpec((chunk, width), lambda i, c: (i, 0)),
                pl.BlockSpec((chunk, width), whole),
                pl.BlockSpec((chunk, width), whole),
            ],
        ),
        out_shape=[jax.ShapeDtypeStruct((length, width), BF16), edge, edge],
        compiler_params=params(60),
        cost_estimate=cost(10 * length * width, 4 * length * width),
    )(core, trunk, ids, table, gain)


def gelu_parts(x):
    square = x * x
    t = jnp.tanh(GELU_A * x * (1.0 + GELU_B * square))
    cdf = 0.5 + 0.5 * t
    slope = cdf + (0.5 * GELU_A) * x * (1.0 - t * t) * (1.0 + (3 * GELU_B) * square)
    return x * cdf, slope


def turned(block, rows):
    width = block.shape[1]
    return jnp.transpose(block).reshape(width // (2 * rows), 2, rows, block.shape[0])


def conv_tile(left, mid, right, chunks, w_ref, trunk_refs, grad_refs, ids_ref, table_ref):
    out = dot(left, w_ref[0]) + dot(mid, w_ref[1]) + dot(right, w_ref[2])
    act, slope = gelu_parts(out)
    chunk = out.shape[0] // 2
    hidden, dconv = [], []
    for part in range(2):
        span = slice(part * chunk, (part + 1) * chunk)
        inputs = summed_inputs(trunk_refs[part][0], ids_ref, 2 * chunks[part], table_ref)
        hidden.append((inputs + act[span]).astype(BF16))
        dconv.append((grad_refs[part][0].astype(F32) * slope[span]).astype(BF16))
    return hidden, dconv


def inner_kernel(n_ref, w_ref, ta_ref, tb_ref, ga_ref, gb_ref, ids_ref, table_ref,
                 hidden_ref, dconv_ref, turned_ref, *, rows):
    chunk = DILATION_STEP
    two = 2 * chunk

    def tile():
        hidden, dconv = conv_tile(
            n_ref[:two], n_ref[chunk : chunk + two], n_ref[two:], (1, 2), w_ref,
            (ta_ref, tb_ref), (ga_ref, gb_ref), ids_ref, table_ref,
        )
        hidden_ref[...] = jnp.concatenate(hidden, axis=0)
        dconv_ref[...] = jnp.concatenate(dconv, axis=0)

    for step in range(2):

        @pl.when(pl.program_id(0) == step)
        def _():
            span = slice(step * two, (step + 1) * two)
            turned_ref[:, :, :, span] = turned(n_ref[span], rows)
            tile()

    pl.when(pl.program_id(0) == 2)(tile)


def conv_inner(normed, weight, trunk, grad, ids, table, rows):
    length, width = normed.shape
    chunk = DILATION_STEP
    groups = width // (2 * rows)
    whole = lambda n: (0, 0)
    part = lambda c: pl.BlockSpec((1, chunk, TILE), lambda n: (c, 0, n))
    out = pl.BlockSpec((2 * chunk, TILE), lambda n: (0, n))
    half = jax.ShapeDtypeStruct((2 * chunk, width), BF16)
    turned_shape = (groups, 2, rows, length)
    return pl.pallas_call(
        functools.partial(inner_kernel, rows=rows),
        grid=(width // TILE,),
        in_specs=[
            pl.BlockSpec(normed.shape, whole),
            pl.BlockSpec((3, width, TILE), lambda n: (0, 0, n)),
            part(1), part(2), part(1), part(2),
            pl.BlockSpec(ids.shape, whole),
            pl.BlockSpec((table.shape[0], TILE), lambda n: (0, n)),
        ],
        out_specs=[out, out, pl.BlockSpec(turned_shape, lambda n: (0, 0, 0, 0))],
        out_shape=[half, half, jax.ShapeDtypeStruct(turned_shape, BF16)],
        compiler_params=params(60),
        cost_estimate=cost(3 * length * width * width, 8 * length * width),
    )(normed, weight, trunk, trunk, grad, grad, ids, table)


def edge_kernel(core_ref, near_ref, far_ref, n_ref, w_ref, ta_ref, tb_ref, ga_ref, gb_ref, ids_ref, table_ref,
                inner_ref, turned_ref, hidden_ref, sent_ref, kept_ref, dconv_ref, low_t_ref, high_t_ref, *, rows):
    step = pl.program_id(0)
    chunk = near_ref.shape[0]
    length, width = n_ref.shape
    tiles = width // TILE
    first = core_ref[0] == 0
    part = lambda i: n_ref[i * chunk : (i + 1) * chunk]

    def conv(tile):
        low = jnp.where(first, far_ref[...], near_ref[...])
        high = jnp.where(first, near_ref[...], far_ref[...])
        left = jnp.concatenate([low, part(2)], axis=0)
        mid = jnp.concatenate([part(0), part(3)], axis=0)
        right = jnp.concatenate([part(1), high], axis=0)
        hidden, dconv = conv_tile(left, mid, right, (0, 3), w_ref, (ta_ref, tb_ref), (ga_ref, gb_ref),
                                  ids_ref, table_ref)
        hidden_ref[...] = jnp.concatenate(hidden, axis=0)
        span = slice(tile * TILE, (tile + 1) * TILE)
        dconv_ref[:chunk, span] = dconv[0]
        dconv_ref[3 * chunk :, span] = dconv[1]
        if tile == 0:
            low_t_ref[...] = turned(low, rows)
            dconv_ref[chunk : 3 * chunk] = inner_ref[...]
        if tile == 1:
            high_t_ref[...] = turned(high, rows)

    for tile in range(tiles):
        pl.when(step == tile)(functools.partial(conv, tile))

    for tap in range(3):

        @pl.when(step == tiles + tap)
        def _():
            if tap == 0:
                window = jnp.concatenate([low_t_ref[...], turned_ref[:, :, :, : length - chunk]], axis=3)
            elif tap == 1:
                window = turned_ref[...]
            else:
                window = jnp.concatenate([turned_ref[:, :, :, chunk:], high_t_ref[...]], axis=3)
            value = dot(window.reshape(width, length), dconv_ref[...])
            value = value.reshape(width // (2 * rows), 2, rows, width)
            kept_ref[:, 0] = jnp.where(first, value[:, 0], value[:, 1]).astype(BF16)
            sent_ref[:, 0] = jnp.where(first, value[:, 1], value[:, 0]).astype(BF16)


def edges_and_grad(core, near, far, normed, weight, trunk, grad, ids, table, inner, turned_rows):
    length, width = normed.shape
    chunk = near.shape[0]
    groups, _, rows, _ = turned_rows.shape
    tiles, taps = width // TILE, weight.shape[0]
    whole = lambda n, c: (0, 0)
    tile = lambda n: jnp.minimum(n, tiles - 1)
    part = lambda k: pl.BlockSpec((1, chunk, TILE), lambda n, c: (k, 0, tile(n)))
    block = pl.BlockSpec((groups, 1, rows, width), lambda n, c: (0, jnp.maximum(n - tiles, 0), 0, 0))
    piece = jax.ShapeDtypeStruct((groups, taps, rows, width), BF16)
    edge_t = pltpu.VMEM((groups, 2, rows, chunk), BF16)
    return pl.pallas_call(
        functools.partial(edge_kernel, rows=rows),
        grid_spec=pltpu.PrefetchScalarGridSpec(
            num_scalar_prefetch=1,
            grid=(tiles + taps,),
            in_specs=[
                pl.BlockSpec(near.shape, whole),
                pl.BlockSpec(far.shape, whole),
                pl.BlockSpec(normed.shape, whole),
                pl.BlockSpec((taps, width, TILE), lambda n, c: (0, 0, tile(n))),
                part(0), part(3), part(0), part(3),
                pl.BlockSpec(ids.shape, whole),
                pl.BlockSpec((table.shape[0], TILE), lambda n, c: (0, tile(n))),
                pl.BlockSpec(inner.shape, whole),
                pl.BlockSpec(turned_rows.shape, lambda n, c: (0, 0, 0, 0)),
            ],
            out_specs=[pl.BlockSpec((2 * chunk, TILE), lambda n, c: (0, tile(n))), block, block],
            scratch_shapes=[pltpu.VMEM((length, width), BF16), edge_t, edge_t],
        ),
        out_shape=[jax.ShapeDtypeStruct((2 * chunk, width), BF16), piece, piece],
        compiler_params=params(60),
        cost_estimate=cost(9 * length * width * width, 20 * length * width),
    )(core, near, far, normed, weight, trunk, trunk, grad, grad, ids, table, inner, turned_rows)


def table_kernel(inner_ref, outer_ref, weight_ref, after_ref, out_ref):
    del after_ref
    half = inner_ref.shape[0]
    out_ref[:half] = dot(inner_ref[...], weight_ref[...]).astype(BF16)
    out_ref[half:] = dot(outer_ref[...], weight_ref[...]).astype(BF16)


def projected(inner, outer, weight, after):
    half, width = inner.shape
    whole = lambda n: (0, 0)
    tile = lambda count: pl.BlockSpec((count, TILE), lambda n: (0, n))
    return pl.pallas_call(
        table_kernel,
        grid=(width // TILE,),
        in_specs=[
            pl.BlockSpec(inner.shape, whole),
            pl.BlockSpec(outer.shape, whole),
            tile(width),
            pl.BlockSpec(memory_space=pl.ANY),
        ],
        out_specs=tile(2 * half),
        out_shape=jax.ShapeDtypeStruct((2 * half, width), BF16),
        compiler_params=params(60),
        cost_estimate=cost(4 * half * width * width, 8 * half * width),
    )(inner, outer, weight, in_hbm(after))


def table_place(position):
    chunk = DILATION_STEP
    moved = jnp.where(position < 3 * chunk, position - chunk, position)
    return jnp.where(position < chunk, position + 2 * chunk, moved)


def join_kernel(kept_ref, got_ref, after_ref, out_ref):
    del after_ref
    out_ref[...] = (kept_ref[...].astype(F32) + got_ref[...].astype(F32)).astype(BF16)


def join(kept, got, after):
    groups, taps, rows, width = kept.shape
    block = pl.BlockSpec((groups // 4, taps, rows, width), lambda i: (i, 0, 0, 0))
    return pl.pallas_call(
        join_kernel,
        grid=(4,),
        in_specs=[block, block, pl.BlockSpec(memory_space=pl.ANY)],
        out_specs=block,
        out_shape=jax.ShapeDtypeStruct(kept.shape, BF16),
        compiler_params=params(8),
        cost_estimate=cost(kept.size, 6 * kept.size),
    )(in_hbm(kept), got, in_hbm(after))


def selected(index_rows, table_ref):
    lane = lax.broadcasted_iota(jnp.int32, (LANES, LANES), 1)
    picks = []
    for row in index_rows:
        index = across_lanes(table_place(row))
        picks.append(
            jnp.concatenate(
                [
                    jnp.where(index == lane + b * LANES, 1.0, 0.0).astype(BF16)
                    for b in range(table_ref.shape[0] // LANES)
                ],
                axis=1,
            )
        )
    return dot(jnp.concatenate(picks, axis=0), table_ref[...]).astype(BF16)


def serve_kernel(chip_ref, hot_ref, index_ref, own_ref, other_ref, after_ref, out_ref):
    del after_ref
    half = LANES // 2
    per = out_ref.shape[0]
    chip, core = chip_ref[0], chip_ref[1]
    sources = []
    for q in range(per):
        apart = jnp.bitwise_xor(chip, pl.program_id(0) * per + q)
        sources.append(apart // 4 + apart % 4 // 2 * 2 + apart % 2 * 4)
    asked = lambda k: [index_ref[source, pl.ds(2 * chip + k, 1), :] for source in sources]
    own = selected(asked(core), own_ref)
    other = selected(asked(1 - core), other_ref)
    hot = hot_ref[0] != 0
    for q in range(per):
        low, high = q * LANES, q * LANES + half
        out_ref[q, 0] = own[low:high]
        out_ref[q, 1] = other[low:high]

    @pl.when(jnp.logical_not(hot))
    def _():
        for q in range(per):
            out_ref[q, 2] = own[q * LANES + half : (q + 1) * LANES]

    @pl.when(hot)
    def _():
        for q in range(per):
            out_ref[q, 2] = other[q * LANES + half : (q + 1) * LANES]


def serve(chip, hot, index, own, other, after):
    groups = index.shape[0]
    width = own.shape[1]
    per = 4
    whole = lambda q, c, h: (0, 0)
    return pl.pallas_call(
        serve_kernel,
        grid_spec=pltpu.PrefetchScalarGridSpec(
            num_scalar_prefetch=2,
            grid=(groups // per,),
            in_specs=[
                pl.BlockSpec(index.shape, lambda q, c, h: (0, 0, 0)),
                pl.BlockSpec(own.shape, whole),
                pl.BlockSpec(other.shape, whole),
                pl.BlockSpec(memory_space=pl.ANY),
            ],
            out_specs=pl.BlockSpec((per, 3, LANES // 2, width), lambda q, c, h: (q, 0, 0, 0)),
        ),
        out_shape=jax.ShapeDtypeStruct((groups, 3, LANES // 2, width), BF16),
        compiler_params=params(60),
        cost_estimate=cost(4 * groups * LANES * own.shape[0] * width, 8 * own.size),
    )(chip, hot, index, own, other, in_hbm(after))


def donor_kernel(index_ref, table_ref, after_ref, out_ref):
    del after_ref
    per = out_ref.shape[0] // LANES
    first = pl.program_id(0) * per
    out_ref[...] = selected([index_ref[pl.ds(first + r, 1), :] for r in range(per)], table_ref)


def donor_rows(index, table, after):
    count = index.shape[0]
    width = table.shape[1]
    per = 4
    whole = lambda q: (0, 0)
    return pl.pallas_call(
        donor_kernel,
        grid=(count // per,),
        in_specs=[
            pl.BlockSpec(index.shape, whole),
            pl.BlockSpec(table.shape, whole),
            pl.BlockSpec(memory_space=pl.ANY),
        ],
        out_specs=pl.BlockSpec((per * LANES, width), lambda q: (q, 0)),
        out_shape=jax.ShapeDtypeStruct((count * LANES, width), BF16),
        compiler_params=params(60),
        cost_estimate=cost(2 * count * LANES * table.shape[0] * width, 10 * table.size),
    )(index, table, in_hbm(after))


def pair_kernel(core_ref, counts_ref, donor_ref, accepted_ref, out_ref):
    half = LANES // 2
    per = accepted_ref.shape[0]
    slot = lax.broadcasted_iota(jnp.int32, (half, LANES), 0)
    copies = out_ref.shape[1] // LANES
    for q in range(per):
        group = pl.program_id(0) * per + q
        for owner_core in range(2):
            count = counts_ref[2 * group + owner_core]
            place = lax.rem(core_ref[0] + owner_core, 2)
            for part, source in enumerate((place, 2)):
                at = (2 * q + owner_core) * LANES + part * half
                mask = jnp.where(slot + part * half < count, 1.0, 0.0).astype(BF16)
                mask = jnp.concatenate([mask] * copies, axis=1)
                out_ref[at : at + half] = accepted_ref[q, source] * donor_ref[at : at + half] * mask


def pairs(core, counts, donor, accepted):
    groups = accepted.shape[0]
    width = donor.shape[1]
    per = 2
    rows = pl.BlockSpec((2 * per * LANES, width), lambda q, c, n: (q, 0))
    return pl.pallas_call(
        pair_kernel,
        grid_spec=pltpu.PrefetchScalarGridSpec(
            num_scalar_prefetch=2,
            grid=(groups // per,),
            in_specs=[rows, pl.BlockSpec((per,) + accepted.shape[1:], lambda q, c, n: (q, 0, 0, 0))],
            out_specs=rows,
        ),
        out_shape=jax.ShapeDtypeStruct(donor.shape, BF16),
        compiler_params=params(12),
        cost_estimate=cost(2 * donor.size, 6 * donor.size),
    )(core, counts, in_hbm(donor), accepted)


def spread_kernel(z_ref, pieces_ref, *refs):
    outs, scratch = refs[:-1], refs[-1]
    chips, taps, rows, width = pieces_ref.shape
    total = pieces_ref[0].astype(F32)
    for i in range(1, chips):
        total = total + pieces_ref[i].astype(F32)
    scratch[...] = jnp.transpose(total.reshape(taps * rows, width))
    count = len(outs)
    size = width // count
    for step, out in enumerate(outs):
        start = pl.multiple_of(lax.rem(z_ref[0] + step, count) * size, size)
        out[...] = scratch[pl.ds(start, size), :].astype(out.dtype)


def spread(z, pieces, count):
    chips, taps, rows, width = pieces.shape
    shape = (width // count, taps * rows)
    return pl.pallas_call(
        spread_kernel,
        grid_spec=pltpu.PrefetchScalarGridSpec(
            num_scalar_prefetch=1,
            grid=(1,),
            in_specs=[pl.BlockSpec(pieces.shape, lambda i, z: (0, 0, 0, 0))],
            out_specs=[pl.BlockSpec(shape, lambda i, z: (0, 0))] * count,
            scratch_shapes=[pltpu.VMEM((width, taps * rows), F32)],
        ),
        out_shape=[jax.ShapeDtypeStruct(shape, BF16 if k else F32) for k in range(count)],
        compiler_params=params(12),
        cost_estimate=cost(2 * pieces.size, 3 * pieces.size),
    )(z, pieces)


def gather_kernel(yl_ref, own_ref, *refs):
    got, (kept_ref, sent_ref) = refs[:-2], refs[-2:]
    half = kept_ref.shape[0]

    def total(start):
        value = own_ref[start : start + half]
        for ref in got:
            value = value + ref[start : start + half].astype(F32)
        return value

    for yl in range(2):

        @pl.when(yl_ref[0] == yl)
        def _():
            kept_ref[...] = total(yl * half)
            sent_ref[...] = total((1 - yl) * half).astype(BF16)


def gathered(yl, own, got):
    rows, width = own.shape
    whole = lambda i, y: (0, 0)
    full = pl.BlockSpec(own.shape, whole)
    half = pl.BlockSpec((rows // 2, width), whole)
    return pl.pallas_call(
        gather_kernel,
        grid_spec=pltpu.PrefetchScalarGridSpec(
            num_scalar_prefetch=1, grid=(1,), in_specs=[full] * (1 + len(got)), out_specs=[half, half]
        ),
        out_shape=[
            jax.ShapeDtypeStruct((rows // 2, width), F32),
            jax.ShapeDtypeStruct((rows // 2, width), BF16),
        ],
        compiler_params=params(8),
        cost_estimate=cost(8 * own.size, 20 * own.size),
    )(yl, own, *got)


def final_kernel(kept_ref, got_ref, out_ref):
    total = kept_ref[...] + got_ref[...].astype(F32)
    out_ref[...] = jnp.transpose(total).reshape(out_ref.shape)


def final_grad(kept, got, taps):
    cols, width = kept.shape
    return pl.pallas_call(
        final_kernel,
        out_shape=jax.ShapeDtypeStruct((taps, width // taps, cols), F32),
        compiler_params=params(8),
    )(kept, got)


def dp_sum(outs, taps):
    nz = len(outs)
    got = [
        lax.ppermute(outs[step], "z", [(i, (i + step) % nz) for i in range(nz)])
        for step in range(1, nz)
    ]
    kept, sent = gathered(lax.axis_index("yl")[None], outs[0], got)
    return final_grad(kept, lax.ppermute(sent, "yl", [(0, 1), (1, 0)]), taps)


def on_device(
    trunk_acts,
    base_ids,
    base_table,
    norm_gain,
    conv_weight,
    grad_out,
    donor_pos,
    accept_pos,
    pair_counts,
    donor_weight,
    accept_weight,
):
    core = lax.axis_index("core")
    chip = lax.axis_index(CHIPS)
    trunk = trunk_acts[0]
    length, width = trunk.shape
    seq_count = lax.axis_size(SEQ)
    rows = width // seq_count
    chips = seq_count // 2
    ids = base_ids.reshape(length // LANES, LANES)
    weight = jnp.transpose(conv_weight, (1, 0, 2))
    swap = [(0, 1), (1, 0)]
    split = lambda v: v.reshape(length // DILATION_STEP, DILATION_STEP, width)
    core_id = core[None]

    def widened(slots, bit):
        other = lax.ppermute(slots, CHIPS, [(i, i ^ bit) for i in range(chips)])
        return jnp.concatenate([slots, other], axis=0)

    slots = widened(accept_pos.reshape(1, seq_count, -1), 4)
    normed, near, far = norm_rows(core_id, trunk, ids, base_table, norm_gain)
    slots = widened(slots, 2)
    borders = [(i, i + 1) for i in range(1, seq_count - 1, 2)]
    far = lax.ppermute(far, SEQ, borders + [(target, source) for source, target in borders])
    near = lax.ppermute(near, "core", swap)
    common = (normed, weight, split(trunk_acts), split(grad_out), ids, base_table)
    hidden_in, dconv_in, turned_rows = conv_inner(*common, rows)
    slots, dconv_in = lax.optimization_barrier((slots, dconv_in))
    slots = widened(slots, 1)
    near, far, slots = lax.optimization_barrier((near, far, slots))
    hidden_out, sent, kept = edges_and_grad(core_id, near, far, *common, dconv_in, turned_rows)
    got = lax.ppermute(sent, "core", swap)
    accept_local = projected(hidden_in, hidden_out, accept_weight, kept)
    chip_half = join(kept, got, accept_local)
    pieces = lax.all_to_all(chip_half, CHIPS, 0, 0, tiled=True)

    accept_other = lax.ppermute(accept_local, "core", swap)
    counts = pair_counts[0]
    hot = (lax.dynamic_index_in_dim(counts, 2 * chip + 1 - core, 0) > slots.shape[2] // 2).astype(jnp.int32)
    donor_table = projected(hidden_in, hidden_out, donor_weight, chip_half)
    donor_emb = donor_rows(donor_pos.reshape(2 * chips, -1), donor_table, chip_half)
    served = serve(jnp.stack([chip, core]), hot, slots, accept_local, accept_other, donor_emb)
    blocks = list(spread(lax.axis_index("z")[None], pieces, lax.axis_size("z")))
    served, blocks[0] = lax.optimization_barrier((served, blocks[0]))
    accepted = lax.all_to_all(served, CHIPS, 0, 0, tiled=True)
    weight_grad = jnp.transpose(dp_sum(blocks, conv_weight.shape[1]), (1, 0, 2))
    junction_pairs = pairs(core[None], counts, donor_emb, accepted)[None]
    return (junction_pairs, weight_grad)


def solution(mesh):
    grid = Mesh(mesh.devices.reshape(8, 2, 2, 4, 2), AXES)
    return jax.shard_map(
        on_device,
        mesh=grid,
        in_specs=(
            P(DP, SEQ, None),
            P(DP, SEQ),
            P(),
            P(),
            P(),
            P(DP, SEQ, None),
            P(DP, SEQ),
            P(DP, SEQ),
            P(DP, SEQ),
            P(),
            P(),
        ),
        out_specs=(P(DP, SEQ, None), P(SEQ, None, DP)),
        check_vma=False,
    )
```

time: 166 us -> 123 us (0.74)
  Pallas kernels: 0 us -> 57.9 us
  waiting for transfers between devices: 64.8 us -> 14.5 us
  matrix products: 39.5 us -> 0 us
  local copies, waits for them, and re-layouts: 12.7 us -> 2.05 us
  other arithmetic: 13.1 us -> 2.59 us
  starting transfers between devices: 34.3 us -> 42.6 us
    all_to_all x4 -> x2, waiting for transfers between devices: 64.8 us -> 3.6 us  [the longest x1 2.23 us: on_device(): pieces = lax.all_to_all(chip_half, CHIPS, 0, 0, tiled=True)]
    pallas_call x0 -> x12, Pallas kernels: none -> 57.9 us  [the longest x1 12.6 us: edges_and_grad(): pl.pallas_call(functools.partial(edge_kernel, rows=rows), grid_spec=pltpu...]
    dot_general x8 -> x0, matrix products: 39.5 us -> none  [the longest x3 15.4 us: on_device(): jnp.dot(windows[tap], conv_weight[:, tap, :], preferred_element_type=jnp....]
    ppermute x3 -> x15, starting transfers between devices: 5.57 us -> 29.4 us  [the longest x7 18.4 us: dp_sum(): lax.ppermute(outs[step], 'z', [(i, (i + step) % nz) for i in range(nz)])]
    all_to_all x4 -> x2, starting transfers between devices: 28.7 us -> 13.2 us  [the longest x1 7.4 us: on_device(): pieces = lax.all_to_all(chip_half, CHIPS, 0, 0, tiled=True)]
    ppermute x3 -> x15, waiting for transfers between devices: 0.01 us -> 10.9 us  [the longest x1 4.78 us: dp_sum(): return final_grad(kept, lax.ppermute(sent, 'yl', [(0, 1), (1, 0)]), taps)]
    convert_element_type x1 -> x0, other arithmetic: 3.24 us -> none  [rms_normed(): return (inputs * scale * norm_gain).astype(jnp.bfloat16)]
    reduce_sum x3 -> x0, other arithmetic: 2.9 us -> none  [the longest x1 2.54 us: rms_normed(): scale = lax.rsqrt(jnp.mean(inputs * inputs, axis=-1, keepdims=True) + 1e-06)]
  transfers between devices with their start and end apart: 7 -> 17, of which waited for: 4 -> 7; matrix products, arithmetic and copies ran while one was open for 23% -> 2% of each run, Pallas kernels for 0% -> 33%
where the time goes in v3:
time: 123 us; the launch traced here: 121 us
  Pallas kernels  57.9 us (47%)
  starting transfers between devices  42.6 us (35%)
  waiting for transfers between devices  14.5 us (12%)
  other arithmetic  2.59 us (2%)
  local copies, waits for them, and re-layouts  2.05 us (2%)
  between operations  1.42 us (1%)
    ppermute x7, starting transfers between devices, dp_sum(): lax.ppermute(outs[step], 'z', [(i, (i + step) % nz) for i in range(nz)])  18.4 us
    pallas_call x1, Pallas kernels, edges_and_grad(): pl.pallas_call(functools.partial(edge_kernel, rows=rows), grid_spec=pltpu...  12.6 us
    pallas_call x2, Pallas kernels, projected(): pl.pallas_call(table_kernel, grid=(width // TILE,), in_specs=[pl.BlockSpe...  9.4 us
    pallas_call x1, Pallas kernels, serve(): pl.pallas_call(serve_kernel, grid_spec=pltpu.PrefetchScalarGridSpec(num_s...  7.43 us
    pallas_call x1, Pallas kernels, conv_inner(): pl.pallas_call(functools.partial(inner_kernel, rows=rows), grid=(width //...  7.41 us
    all_to_all x1, starting transfers between devices, on_device(): pieces = lax.all_to_all(chip_half, CHIPS, 0, 0, tiled=True)  7.4 us
    ppermute x3, starting transfers between devices, widened(): other = lax.ppermute(slots, CHIPS, [(i, i ^ bit) for i in range(chips)])  6.93 us
    pallas_call x1, Pallas kernels, donor_rows(): pl.pallas_call(donor_kernel, grid=(count // per,), in_specs=[pl.BlockSpec...  6.54 us
  transfers between devices with their start and end apart: 17, of which 7 were waited for; matrix products, arithmetic and copies ran while one was open for 2% of the time, Pallas kernels for 33%

profile of v3, /device:TPU:2, one launch (start us, length us, event | category | flops | bytes accessed | tf_op | source)
XLA Modules:
  0.0 121.1 jit_solution(10551975276536041110)
XLA Ops:
  0.6 3.3 %collective-permute-start.2 = (s32[1,16,128]{2,1,0:T(8,128)}, s32[1,16,128]{2,1,0:T(8,128)S(1)}, u32[]{:S(2)}, u32[]{:S(2)}) collective-permute-start(s32[1,16,128]{2,1,0:T(8,128)} %bitcast.29), channel_id=1, source_target_pairs={{0,8},{2,10},{4,12},{6,14},{8,0},{10,2},{12,4},{14,6},{1,9},{3,11}... | collective-permute-start | bytes 24584 | tf_op jit(solution)/shard_map/ppermute | solution.py:568
  3.9 4.6 %shard_map.122 = (bf16[1024,768]{1,0:T(8,128)(2,1)}, bf16[256,768]{1,0:T(8,128)(2,1)}, bf16[256,768]{1,0:T(8,128)(2,1)}) custom-call(s32[1]{0:T(128)} %bitcast.core_ref, bf16[1024,768]{1,0:T(8,128)(2,1)} %bitcast.16, s32[8,128]{1,0:T(8,128)} %bitcast.32, f32[4,768]{1,0:T(4,128)} %table_ref.5, f32[768]{0:T(1024)} %gain_ref.1), custom_call_target="tpu_custom_call" | custom-call | flops 7864320 | bytes 3145728 | tf_op jit(solution)/shard_map/pallas_call | solution.py:82
  8.5 0.0 collective-permute-start
  8.5 2.5 %collective-permute-start.1 = (bf16[256,768]{1,0:T(8,128)(2,1)}, bf16[256,768]{1,0:T(8,128)(2,1)S(1)}, u32[]{:S(2)}, u32[]{:S(2)}) collective-permute-start(bf16[256,768]{1,0:T(8,128)(2,1)} %get-tuple-element.31), channel_id=1, source_target_pairs={{1,2},{3,4},{5,6},{7,8},{9,10},{11,12},{13,14},{2,1},{4,3},{6,5},{... | collective-permute-start | bytes 1179656 | tf_op jit(solution)/shard_map/ppermute | solution.py:575
  11.0 0.0 collective-permute-done.2
  11.1 0.7 pad_add_fusion.2
  11.8 2.4 %collective-permute-start.3 = (s32[2,16,128]{2,1,0:T(8,128)S(1)}, s32[2,16,128]{2,1,0:T(8,128)S(1)}, u32[]{:S(2)}, u32[]{:S(2)}) collective-permute-start(s32[2,16,128]{2,1,0:T(8,128)S(1)} %pad_add_fusion.2), channel_id=1, source_target_pairs={{0,4},{2,6},{4,0},{6,2},{8,12},{10,14},{12,8},{14,10},{1,5},{3,7},... | collective-permute-start | bytes 49160 | tf_op jit(solution)/shard_map/ppermute | solution.py:568
  14.2 0.0 copy-start.1
  14.2 7.4 %shard_map.123 = (bf16[512,768]{1,0:T(8,128)(2,1)}, bf16[512,768]{1,0:T(8,128)(2,1)}, bf16[8,2,48,1024]{3,2,1,0:T(8,128)(2,1)}) custom-call(bf16[1024,768]{1,0:T(8,128)(2,1)} %get-tuple-element.28.n_ref, bf16[3,768,768]{2,1,0:T(8,128)(2,1)} %bitcast.25, bf16[4,256,768]{2,1,0:T(8,128)(2,1)} %bitcast.17, bf16[4,256,768]{2,1,0:T(8,128)(2,1)} %bitcast.18, ...), custom_call_target="tpu_custom_call" | custom-call | flops 1811939328 | bytes 6291456 | tf_op jit(solution)/shard_map/pallas_call | solution.py:164
  21.6 0.0 collective-permute-done.3
  21.6 0.0 copy-done.1
  21.6 1.2 %collective-permute-start.4 = (s32[4,16,128]{2,1,0:T(8,128)S(1)}, s32[4,16,128]{2,1,0:T(8,128)S(1)}, u32[]{:S(2)}, u32[]{:S(2)}) collective-permute-start(s32[4,16,128]{2,1,0:T(8,128)S(1)} %pad_add_fusion.1), channel_id=1, source_target_pairs={{0,2},{2,0},{4,6},{6,4},{8,10},{10,8},{12,14},{14,12},{1,3},{3,1},... | collective-permute-start | bytes 98312 | tf_op jit(solution)/shard_map/ppermute | solution.py:568
  22.9 3.1 %collective-permute-done.4 = s32[4,16,128]{2,1,0:T(8,128)S(1)} collective-permute-done((s32[4,16,128]{2,1,0:T(8,128)S(1)}, s32[4,16,128]{2,1,0:T(8,128)S(1)}, u32[]{:S(2)}, u32[]{:S(2)}) %collective-permute-start.4) | collective-permute-done | bytes 32800 | tf_op jit(solution)/shard_map/ppermute | solution.py:568
  25.9 0.6 pad_add_fusion.index_ref
  26.5 0.0 collective-permute-done.near_ref
  26.5 0.0 copy-start.3
  26.5 0.0 collective-permute-done.1.far_ref
  26.5 0.0 copy-start.4
  26.6 0.7 copy-done.3
  27.3 0.1 copy-done.4
  27.4 12.6 %shard_map.124 = (bf16[512,768]{1,0:T(8,128)(2,1)}, bf16[8,3,48,768]{3,2,1,0:T(8,128)(2,1)}, bf16[8,3,48,768]{3,2,1,0:T(8,128)(2,1)}) custom-call(s32[1]{0:T(128)} %bitcast.core_ref, bf16[256,768]{1,0:T(8,128)(2,1)} %copy-done.3, bf16[256,768]{1,0:T(8,128)(2,1)} %copy-done.4, bf16[1024,768]{1,0:T(8,128)(2,1)} %get-tuple-element.28.n_ref, ...), custom_call_target="tpu_custom_call" | custom-call | flops 5435817984 | bytes 15728640 | tf_op jit(solution)/shard_map/pallas_call | solution.py:238
  40.0 0.3 collective-permute-start.5
  40.3 4.8 %shard_map.125.after_ref.own_ref = bf16[1024,768]{1,0:T(8,128)(2,1)} custom-call(bf16[512,768]{1,0:T(8,128)(2,1)} %get-tuple-element.29.inner_ref, bf16[512,768]{1,0:T(8,128)(2,1)} %get-tuple-element.38.outer_ref, bf16[768,768]{1,0:T(8,128)(2,1)} %weight_ref.2, bf16[8,3,48,768]{3,2,1,0:T(8,128)(2,1)} %get-tuple-element.39.after_ref.kept_ref), custom_call_target="tpu_custom_call" | custom-call | flops 1207959552 | bytes 3145728 | tf_op jit(solution)/shard_map/pallas_call | solution.py:274
  45.1 0.5 collective-permute-start.6
  45.5 0.0 collective-permute-done.5.got_ref
  45.5 3.9 %shard_map.126.after_ref = bf16[8,3,48,768]{3,2,1,0:T(8,128)(2,1)} custom-call(bf16[8,3,48,768]{3,2,1,0:T(8,128)(2,1)} %get-tuple-element.39.after_ref.kept_ref, bf16[8,3,48,768]{3,2,1,0:T(8,128)(2,1)S(1)} %collective-permute-done.5.got_ref, bf16[1024,768]{1,0:T(8,128)(2,1)} %shard_map.125.after_ref.own_ref), custom_call_target="tpu_custom_call" | custom-call | flops 884736 | bytes 5308416 | tf_op jit(solution)/shard_map/pallas_call | solution.py:304
  49.4 0.0 copy-start
  49.4 7.4 %all-to-all-start = ((bf16[8,3,48,768]{3,2,1,0:T(8,128)(2,1)}), bf16[8,3,48,768]{3,2,1,0:T(8,128)(2,1)S(1)}, u32[]{:S(2)}, u32[]{:S(2)}) async-start(bf16[8,3,48,768]{3,2,1,0:T(8,128)(2,1)} %shard_map.126.after_ref), calls=%async_computation | async-start | bytes 3538944 | tf_op jit(solution)/shard_map/all_to_all | solution.py:586
  56.8 0.0 copy-done
  56.8 0.7 fusion
  58.2 0.6 pad_add_fusion.3.chip_ref
  58.8 4.6 %shard_map.127.table_ref = bf16[1024,768]{1,0:T(8,128)(2,1)} custom-call(bf16[512,768]{1,0:T(8,128)(2,1)} %get-tuple-element.29.inner_ref, bf16[512,768]{1,0:T(8,128)(2,1)} %get-tuple-element.38.outer_ref, bf16[768,768]{1,0:T(8,128)(2,1)} %weight_ref.3, bf16[8,3,48,768]{3,2,1,0:T(8,128)(2,1)} %shard_map.126.after_ref), custom_call_target="tpu_custom_call" | custom-call | flops 1207959552 | bytes 3145728 | tf_op jit(solution)/shard_map/pallas_call | solution.py:274
  63.4 6.5 %shard_map.128.after_ref.donor_ref = bf16[2048,768]{1,0:T(8,128)(2,1)} custom-call(s32[16,128]{1,0:T(8,128)} %bitcast.35, bf16[1024,768]{1,0:T(8,128)(2,1)} %shard_map.127.table_ref, bf16[8,3,48,768]{3,2,1,0:T(8,128)(2,1)} %shard_map.126.after_ref), custom_call_target="tpu_custom_call" | custom-call | flops 3221225472 | bytes 7864320 | tf_op jit(solution)/shard_map/pallas_call | solution.py:397
  69.9 0.0 collective-permute-done.6.other_ref
  69.9 0.0 copy-start.2
  69.9 1.2 copy-done.2
  71.1 7.4 %shard_map.129 = bf16[8,3,64,768]{3,2,1,0:T(8,128)(2,1)} custom-call(s32[2]{0:T(128)} %pad_add_fusion.3.chip_ref, s32[1]{0:T(128)} %bitcast.10.hot_ref, s32[8,16,128]{2,1,0:T(8,128)} %pad_add_fusion.index_ref, bf16[1024,768]{1,0:T(8,128)(2,1)} %shard_map.125.after_ref.own_ref, bf16[1024,768]{1,0:T(8,128)(2,1)} %copy-done.2, ...), custom_call_target="tpu_custom_call" | custom-call | flops 3221225472 | bytes 6291456 | tf_op jit(solution)/shard_map/pallas_call | solution.py:366
  78.5 2.2 %all-to-all-done.pieces_ref = bf16[8,3,48,768]{3,2,1,0:T(8,128)(2,1)S(1)} async-done(((bf16[8,3,48,768]{3,2,1,0:T(8,128)(2,1)}), bf16[8,3,48,768]{3,2,1,0:T(8,128)(2,1)S(1)}, u32[]{:S(2)}, u32[]{:S(2)}) %all-to-all-start) | async-done | bytes 1769504 | tf_op jit(solution)/shard_map/all_to_all | solution.py:586
  80.8 0.4 shard_map.130
  81.2 5.8 %all-to-all-start.1 = ((bf16[8,3,64,768]{3,2,1,0:T(8,128)(2,1)}), bf16[8,3,64,768]{3,2,1,0:T(8,128)(2,1)S(1)}, u32[]{:S(2)}, u32[]{:S(2)}) async-start(bf16[8,3,64,768]{3,2,1,0:T(8,128)(2,1)} %shard_map.129), calls=%async_computation.1 | async-start | bytes 4718592 | tf_op jit(solution)/shard_map/all_to_all | solution.py:596
  87.0 1.9 %collective-permute-start.7 = (bf16[96,144]{1,0:T(8,128)(2,1)S(1)}, bf16[96,144]{1,0:T(8,128)(2,1)S(1)}, u32[]{:S(2)}, u32[]{:S(2)}) collective-permute-start(bf16[96,144]{1,0:T(8,128)(2,1)S(1)} %get-tuple-element.45), channel_id=1, source_target_pairs={{0,32},{32,64},{64,96},{96,128},{128,160},{160,192},{192,224},{224... | collective-permute-start | bytes 82952 | tf_op jit(solution)/shard_map/ppermute | solution.py:534
  88.9 3.3 %collective-permute-start.8 = (bf16[96,144]{1,0:T(8,128)(2,1)S(1)}, bf16[96,144]{1,0:T(8,128)(2,1)S(1)}, u32[]{:S(2)}, u32[]{:S(2)}) collective-permute-start(bf16[96,144]{1,0:T(8,128)(2,1)S(1)} %get-tuple-element.46), channel_id=1, source_target_pairs={{0,64},{32,96},{64,128},{96,160},{128,192},{160,224},{192,0},{224,... | collective-permute-start | bytes 82952 | tf_op jit(solution)/shard_map/ppermute | solution.py:534
  92.2 4.0 %collective-permute-start.9 = (bf16[96,144]{1,0:T(8,128)(2,1)S(1)}, bf16[96,144]{1,0:T(8,128)(2,1)S(1)}, u32[]{:S(2)}, u32[]{:S(2)}) collective-permute-start(bf16[96,144]{1,0:T(8,128)(2,1)S(1)} %get-tuple-element.47), channel_id=1, source_target_pairs={{0,96},{32,128},{64,160},{96,192},{128,224},{160,0},{192,32},{224,... | collective-permute-start | bytes 82952 | tf_op jit(solution)/shard_map/ppermute | solution.py:534
  96.2 0.5 collective-permute-start.10
  96.8 4.9 %collective-permute-start.11 = (bf16[96,144]{1,0:T(8,128)(2,1)S(1)}, bf16[96,144]{1,0:T(8,128)(2,1)S(1)}, u32[]{:S(2)}, u32[]{:S(2)}) collective-permute-start(bf16[96,144]{1,0:T(8,128)(2,1)S(1)} %get-tuple-element.49), channel_id=1, source_target_pairs={{0,160},{32,192},{64,224},{96,0},{128,32},{160,64},{192,96},{224,1... | collective-permute-start | bytes 82952 | tf_op jit(solution)/shard_map/ppermute | solution.py:534
  101.7 0.0 collective-permute-done.7.refs_0_
  101.7 2.7 %collective-permute-start.12 = (bf16[96,144]{1,0:T(8,128)(2,1)S(1)}, bf16[96,144]{1,0:T(8,128)(2,1)S(1)}, u32[]{:S(2)}, u32[]{:S(2)}) collective-permute-start(bf16[96,144]{1,0:T(8,128)(2,1)S(1)} %get-tuple-element.50), channel_id=1, source_target_pairs={{0,192},{32,224},{64,0},{96,32},{128,64},{160,96},{192,128},{224,1... | collective-permute-start | bytes 82952 | tf_op jit(solution)/shard_map/ppermute | solution.py:534
  104.4 0.0 collective-permute-done.8.refs_1_
  104.4 1.0 collective-permute-start.13
  105.4 0.0 collective-permute-done.9.refs_2_
  105.4 0.0 collective-permute-done.10.refs_3_
  105.4 1.0 collective-permute-done.11.refs_4_
  106.4 1.3 %collective-permute-done.12.refs_5_ = bf16[96,144]{1,0:T(8,128)(2,1)S(1)} collective-permute-done((bf16[96,144]{1,0:T(8,128)(2,1)S(1)}, bf16[96,144]{1,0:T(8,128)(2,1)S(1)}, u32[]{:S(2)}, u32[]{:S(2)}) %collective-permute-start.12) | collective-permute-done | bytes 27680 | tf_op jit(solution)/shard_map/ppermute | solution.py:534
  107.7 0.8 collective-permute-done.13.refs_6_
  108.5 0.1 shard_map.132
  108.6 0.8 collective-permute-start.14
  109.3 4.8 %collective-permute-done.14.got_ref = bf16[48,144]{1,0:T(8,128)(2,1)S(1)} collective-permute-done((bf16[48,144]{1,0:T(8,128)(2,1)S(1)}, bf16[48,144]{1,0:T(8,128)(2,1)S(1)}, u32[]{:S(2)}, u32[]{:S(2)}) %collective-permute-start.14) | collective-permute-done | bytes 13856 | tf_op jit(solution)/shard_map/ppermute | solution.py:538
  114.1 0.7 shard_map.133
  114.8 1.4 %all-to-all-done.1.accepted_ref = bf16[8,3,64,768]{3,2,1,0:T(8,128)(2,1)S(1)} async-done(((bf16[8,3,64,768]{3,2,1,0:T(8,128)(2,1)}), bf16[8,3,64,768]{3,2,1,0:T(8,128)(2,1)S(1)}, u32[]{:S(2)}, u32[]{:S(2)}) %all-to-all-start.1) | async-done | bytes 2359328 | tf_op jit(solution)/shard_map/all_to_all | solution.py:596
  116.2 4.9 %shard_map.131 = bf16[2048,768]{1,0:T(8,128)(2,1)} custom-call(s32[1]{0:T(128)} %bitcast.core_ref, s32[16]{0:T(128)S(1)} %bitcast.15, bf16[2048,768]{1,0:T(8,128)(2,1)} %shard_map.128.after_ref.donor_ref, bf16[8,3,64,768]{3,2,1,0:T(8,128)(2,1)S(1)} %all-to-all-done.1.accepted_ref), custom_call_target="tpu_custom_call" | custom-call | flops 3145728 | bytes 9437184 | tf_op jit(solution)/shard_map/pallas_call | solution.py:434
  (1 shorter events, 0.0 us)
Async XLA Ops:
  0.6 10.4 %collective-permute-start.2 = (s32[1,16,128]{2,1,0:T(8,128)}, s32[1,16,128]{2,1,0:T(8,128)S(1)}, u32[]{:S(2)}, u32[]{:S(2)}) collective-permute-start(s32[1,16,128]{2,1,0:T(8,128)} %bitcast.29), channel_id=1, source_target_pairs={{0,8},{2,10},{4,12},{6,14},{8,0},{10,2},{12,4},{14,6},{1,9},{3,11}... | collective-permute-start | bytes 24584 | tf_op jit(solution)/shard_map/ppermute | solution.py:568
  8.5 18.1 %collective-permute-start = (bf16[256,768]{1,0:T(8,128)(2,1)}, bf16[256,768]{1,0:T(8,128)(2,1)S(1)}, u32[]{:S(2)}, u32[]{:S(2)}) collective-permute-start(bf16[256,768]{1,0:T(8,128)(2,1)} %get-tuple-element.30), channel_id=1, source_target_pairs={{0,1},{1,0},{2,3},{3,2},{4,5},{5,4},{6,7},{7,6},{8,9},{9,8},{10,11... | collective-permute-start | bytes 1179656 | tf_op jit(solution)/shard_map/ppermute | solution.py:576
  8.5 18.0 %collective-permute-start.1 = (bf16[256,768]{1,0:T(8,128)(2,1)}, bf16[256,768]{1,0:T(8,128)(2,1)S(1)}, u32[]{:S(2)}, u32[]{:S(2)}) collective-permute-start(bf16[256,768]{1,0:T(8,128)(2,1)} %get-tuple-element.31), channel_id=1, source_target_pairs={{1,2},{3,4},{5,6},{7,8},{9,10},{11,12},{13,14},{2,1},{4,3},{6,5},{... | collective-permute-start | bytes 1179656 | tf_op jit(solution)/shard_map/ppermute | solution.py:575
  11.8 9.8 %collective-permute-start.3 = (s32[2,16,128]{2,1,0:T(8,128)S(1)}, s32[2,16,128]{2,1,0:T(8,128)S(1)}, u32[]{:S(2)}, u32[]{:S(2)}) collective-permute-start(s32[2,16,128]{2,1,0:T(8,128)S(1)} %pad_add_fusion.2), channel_id=1, source_target_pairs={{0,4},{2,6},{4,0},{6,2},{8,12},{10,14},{12,8},{14,10},{1,5},{3,7},... | collective-permute-start | bytes 49160 | tf_op jit(solution)/shard_map/ppermute | solution.py:568
  14.2 7.4 %copy-start.1 = (s32[1,2048]{1,0:T(1,128)S(1)}, s32[1,2048]{1,0:T(1,128)}, u32[]{:S(2)}) copy-start(s32[1,2048]{1,0:T(1,128)} %param.18) | copy-start | bytes 24580
  21.6 4.3 %collective-permute-start.4 = (s32[4,16,128]{2,1,0:T(8,128)S(1)}, s32[4,16,128]{2,1,0:T(8,128)S(1)}, u32[]{:S(2)}, u32[]{:S(2)}) collective-permute-start(s32[4,16,128]{2,1,0:T(8,128)S(1)} %pad_add_fusion.1), channel_id=1, source_target_pairs={{0,2},{2,0},{4,6},{6,4},{8,10},{10,8},{12,14},{14,12},{1,3},{3,1},... | collective-permute-start | bytes 98312 | tf_op jit(solution)/shard_map/ppermute | solution.py:568
  26.5 0.8 copy-start.3
  26.5 0.9 copy-start.4
  40.0 5.5 %collective-permute-start.5 = (bf16[8,3,48,768]{3,2,1,0:T(8,128)(2,1)}, bf16[8,3,48,768]{3,2,1,0:T(8,128)(2,1)S(1)}, u32[]{:S(2)}, u32[]{:S(2)}) collective-permute-start(bf16[8,3,48,768]{3,2,1,0:T(8,128)(2,1)} %get-tuple-element.40), channel_id=1, source_target_pairs={{0,1},{1,0},{2,3},{3,2},{4,5},{5,4},{6,7},{7,6},{8,9},{9,8},{10,11... | collective-permute-start | bytes 5308424 | tf_op jit(solution)/shard_map/ppermute | solution.py:583
  45.1 24.9 %collective-permute-start.6 = (bf16[1024,768]{1,0:T(8,128)(2,1)}, bf16[1024,768]{1,0:T(8,128)(2,1)S(1)}, u32[]{:S(2)}, u32[]{:S(2)}) collective-permute-start(bf16[1024,768]{1,0:T(8,128)(2,1)} %shard_map.125.after_ref.own_ref), channel_id=1, source_target_pairs={{0,1},{1,0},{2,3},{3,2},{4,5},{5,4},{6,7},{7,6},{8,9},{9,8},{10,11... | collective-permute-start | bytes 4718600 | tf_op jit(solution)/shard_map/ppermute | solution.py:588
  49.4 7.4 %copy-start = (s32[1,16]{1,0:T(1,128)S(1)}, s32[1,16]{1,0:T(1,128)}, u32[]{:S(2)}) copy-start(s32[1,16]{1,0:T(1,128)} %param.19) | copy-start | bytes 196
  49.4 31.4 %all-to-all-start = ((bf16[8,3,48,768]{3,2,1,0:T(8,128)(2,1)}), bf16[8,3,48,768]{3,2,1,0:T(8,128)(2,1)S(1)}, u32[]{:S(2)}, u32[]{:S(2)}) async-start(bf16[8,3,48,768]{3,2,1,0:T(8,128)(2,1)} %shard_map.126.after_ref), calls=%async_computation | async-start | bytes 3538944 | tf_op jit(solution)/shard_map/all_to_all | solution.py:586
  69.9 1.2 copy-start.2
  81.2 35.0 %all-to-all-start.1 = ((bf16[8,3,64,768]{3,2,1,0:T(8,128)(2,1)}), bf16[8,3,64,768]{3,2,1,0:T(8,128)(2,1)S(1)}, u32[]{:S(2)}, u32[]{:S(2)}) async-start(bf16[8,3,64,768]{3,2,1,0:T(8,128)(2,1)} %shard_map.129), calls=%async_computation.1 | async-start | bytes 4718592 | tf_op jit(solution)/shard_map/all_to_all | solution.py:596
  87.0 14.7 %collective-permute-start.7 = (bf16[96,144]{1,0:T(8,128)(2,1)S(1)}, bf16[96,144]{1,0:T(8,128)(2,1)S(1)}, u32[]{:S(2)}, u32[]{:S(2)}) collective-permute-start(bf16[96,144]{1,0:T(8,128)(2,1)S(1)} %get-tuple-element.45), channel_id=1, source_target_pairs={{0,32},{32,64},{64,96},{96,128},{128,160},{160,192},{192,224},{224... | collective-permute-start | bytes 82952 | tf_op jit(solution)/shard_map/ppermute | solution.py:534
  88.9 15.5 %collective-permute-start.8 = (bf16[96,144]{1,0:T(8,128)(2,1)S(1)}, bf16[96,144]{1,0:T(8,128)(2,1)S(1)}, u32[]{:S(2)}, u32[]{:S(2)}) collective-permute-start(bf16[96,144]{1,0:T(8,128)(2,1)S(1)} %get-tuple-element.46), channel_id=1, source_target_pairs={{0,64},{32,96},{64,128},{96,160},{128,192},{160,224},{192,0},{224,... | collective-permute-start | bytes 82952 | tf_op jit(solution)/shard_map/ppermute | solution.py:534
  92.2 13.2 %collective-permute-start.9 = (bf16[96,144]{1,0:T(8,128)(2,1)S(1)}, bf16[96,144]{1,0:T(8,128)(2,1)S(1)}, u32[]{:S(2)}, u32[]{:S(2)}) collective-permute-start(bf16[96,144]{1,0:T(8,128)(2,1)S(1)} %get-tuple-element.47), channel_id=1, source_target_pairs={{0,96},{32,128},{64,160},{96,192},{128,224},{160,0},{192,32},{224,... | collective-permute-start | bytes 82952 | tf_op jit(solution)/shard_map/ppermute | solution.py:534
  96.2 9.2 %collective-permute-start.10 = (bf16[96,144]{1,0:T(8,128)(2,1)S(1)}, bf16[96,144]{1,0:T(8,128)(2,1)S(1)}, u32[]{:S(2)}, u32[]{:S(2)}) collective-permute-start(bf16[96,144]{1,0:T(8,128)(2,1)S(1)} %get-tuple-element.48), channel_id=1, source_target_pairs={{0,128},{32,160},{64,192},{96,224},{128,0},{160,32},{192,64},{224,... | collective-permute-start | bytes 82952 | tf_op jit(solution)/shard_map/ppermute | solution.py:534
  96.8 9.7 %collective-permute-start.11 = (bf16[96,144]{1,0:T(8,128)(2,1)S(1)}, bf16[96,144]{1,0:T(8,128)(2,1)S(1)}, u32[]{:S(2)}, u32[]{:S(2)}) collective-permute-start(bf16[96,144]{1,0:T(8,128)(2,1)S(1)} %get-tuple-element.49), channel_id=1, source_target_pairs={{0,160},{32,192},{64,224},{96,0},{128,32},{160,64},{192,96},{224,1... | collective-permute-start | bytes 82952 | tf_op jit(solution)/shard_map/ppermute | solution.py:534
  101.7 6.0 %collective-permute-start.12 = (bf16[96,144]{1,0:T(8,128)(2,1)S(1)}, bf16[96,144]{1,0:T(8,128)(2,1)S(1)}, u32[]{:S(2)}, u32[]{:S(2)}) collective-permute-start(bf16[96,144]{1,0:T(8,128)(2,1)S(1)} %get-tuple-element.50), channel_id=1, source_target_pairs={{0,192},{32,224},{64,0},{96,32},{128,64},{160,96},{192,128},{224,1... | collective-permute-start | bytes 82952 | tf_op jit(solution)/shard_map/ppermute | solution.py:534
  104.4 4.1 %collective-permute-start.13 = (bf16[96,144]{1,0:T(8,128)(2,1)S(1)}, bf16[96,144]{1,0:T(8,128)(2,1)S(1)}, u32[]{:S(2)}, u32[]{:S(2)}) collective-permute-start(bf16[96,144]{1,0:T(8,128)(2,1)S(1)} %get-tuple-element.51), channel_id=1, source_target_pairs={{0,224},{32,0},{64,32},{96,64},{128,96},{160,128},{192,160},{224,1... | collective-permute-start | bytes 82952 | tf_op jit(solution)/shard_map/ppermute | solution.py:534
  108.6 5.5 %collective-permute-start.14 = (bf16[48,144]{1,0:T(8,128)(2,1)S(1)}, bf16[48,144]{1,0:T(8,128)(2,1)S(1)}, u32[]{:S(2)}, u32[]{:S(2)}) collective-permute-start(bf16[48,144]{1,0:T(8,128)(2,1)S(1)} %get-tuple-element.53), channel_id=1, source_target_pairs={{0,16},{16,0},{1,17},{17,1},{2,18},{18,2},{3,19},{19,3},{4,20},{20... | collective-permute-start | bytes 41480 | tf_op jit(solution)/shard_map/ppermute | solution.py:538

commit v4 on v3

--- a/solution.py
+++ b/solution.py
@@ -179,13 +179,22 @@
 
 
 def edge_kernel(core_ref, near_ref, far_ref, n_ref, w_ref, ta_ref, tb_ref, ga_ref, gb_ref, ids_ref, table_ref,
-                inner_ref, turned_ref, hidden_ref, sent_ref, kept_ref, dconv_ref, low_t_ref, high_t_ref, *, rows):
+                inner_ref, turned_ref, hidden_ref, sent_ref, kept_ref, dconv_ref, window_ref, sems, *, rows):
     step = pl.program_id(0)
     chunk = near_ref.shape[0]
     length, width = n_ref.shape
     tiles = width // TILE
     first = core_ref[0] == 0
     part = lambda i: n_ref[i * chunk : (i + 1) * chunk]
+    fetches = [
+        pltpu.make_async_copy(inner_ref, dconv_ref.at[chunk : 3 * chunk], sems.at[0]),
+        pltpu.make_async_copy(turned_ref, window_ref.at[:, :, :, chunk : chunk + length], sems.at[1]),
+    ]
+
+    @pl.when(step == 0)
+    def _():
+        for fetch in fetches:
+            fetch.start()
 
     def conv(tile):
         low = jnp.where(first, far_ref[...], near_ref[...])
@@ -200,10 +209,9 @@
         dconv_ref[:chunk, span] = dconv[0]
         dconv_ref[3 * chunk :, span] = dconv[1]
         if tile == 0:
-            low_t_ref[...] = turned(low, rows)
-            dconv_ref[chunk : 3 * chunk] = inner_ref[...]
+            window_ref[:, :, :, :chunk] = turned(low, rows)
         if tile == 1:
-            high_t_ref[...] = turned(high, rows)
+            window_ref[:, :, :, chunk + length :] = turned(high, rows)
 
     for tile in range(tiles):
         pl.when(step == tile)(functools.partial(conv, tile))
@@ -213,11 +221,9 @@
         @pl.when(step == tiles + tap)
         def _():
             if tap == 0:
-                window = jnp.concatenate([low_t_ref[...], turned_ref[:, :, :, : length - chunk]], axis=3)
-            elif tap == 1:
-                window = turned_ref[...]
-            else:
-                window = jnp.concatenate([turned_ref[:, :, :, chunk:], high_t_ref[...]], axis=3)
+                for fetch in fetches:
+                    fetch.wait()
+            window = window_ref[:, :, :, tap * chunk : tap * chunk + length]
             value = dot(window.reshape(width, length), dconv_ref[...])
             value = value.reshape(width // (2 * rows), 2, rows, width)
             kept_ref[:, 0] = jnp.where(first, value[:, 0], value[:, 1]).astype(BF16)
@@ -234,7 +240,6 @@
     part = lambda k: pl.BlockSpec((1, chunk, TILE), lambda n, c: (k, 0, tile(n)))
     block = pl.BlockSpec((groups, 1, rows, width), lambda n, c: (0, jnp.maximum(n - tiles, 0), 0, 0))
     piece = jax.ShapeDtypeStruct((groups, taps, rows, width), BF16)
-    edge_t = pltpu.VMEM((groups, 2, rows, chunk), BF16)
     return pl.pallas_call(
         functools.partial(edge_kernel, rows=rows),
         grid_spec=pltpu.PrefetchScalarGridSpec(
@@ -248,16 +253,24 @@
                 part(0), part(3), part(0), part(3),
                 pl.BlockSpec(ids.shape, whole),
                 pl.BlockSpec((table.shape[0], TILE), lambda n, c: (0, tile(n))),
-                pl.BlockSpec(inner.shape, whole),
-                pl.BlockSpec(turned_rows.shape, lambda n, c: (0, 0, 0, 0)),
+                pl.BlockSpec(memory_space=pl.ANY),
+                pl.BlockSpec(memory_space=pl.ANY),
             ],
             out_specs=[pl.BlockSpec((2 * chunk, TILE), lambda n, c: (0, tile(n))), block, block],
-            scratch_shapes=[pltpu.VMEM((length, width), BF16), edge_t, edge_t],
+            scratch_shapes=[
+                pltpu.VMEM((length, width), BF16),
+                pltpu.VMEM((groups, 2, rows, length + 2 * chunk), BF16),
+                pltpu.SemaphoreType.DMA((2,)),
+            ],
         ),
-        out_shape=[jax.ShapeDtypeStruct((2 * chunk, width), BF16), piece, piece],
-        compiler_params=params(60),
+        out_shape=[
+            pltpu.HBM((2 * chunk, width), BF16),
+            pltpu.HBM(piece.shape, BF16),
+            piece,
+        ],
+        compiler_params=params(34),
         cost_estimate=cost(9 * length * width * width, 20 * length * width),
-    )(core, near, far, normed, weight, trunk, trunk, grad, grad, ids, table, inner, turned_rows)
+    )(core, near, far, *[in_hbm(v) for v in (normed, weight, trunk, trunk, grad, grad, ids, table, inner, turned_rows)])
 
 
 def table_kernel(inner_ref, outer_ref, weight_ref, after_ref, out_ref):
@@ -281,10 +294,10 @@
             pl.BlockSpec(memory_space=pl.ANY),
         ],
         out_specs=tile(2 * half),
-        out_shape=jax.ShapeDtypeStruct((2 * half, width), BF16),
-        compiler_params=params(60),
+        out_shape=pltpu.HBM((2 * half, width), BF16),
+        compiler_params=params(12),
         cost_estimate=cost(4 * half * width * width, 8 * half * width),
-    )(inner, outer, weight, in_hbm(after))
+    )(in_hbm(inner), in_hbm(outer), in_hbm(weight), after)
 
 
 def table_place(position):
@@ -306,10 +319,10 @@
         grid=(4,),
         in_specs=[block, block, pl.BlockSpec(memory_space=pl.ANY)],
         out_specs=block,
-        out_shape=jax.ShapeDtypeStruct(kept.shape, BF16),
+        out_shape=pltpu.HBM(kept.shape, BF16),
         compiler_params=params(8),
         cost_estimate=cost(kept.size, 6 * kept.size),
-    )(in_hbm(kept), got, in_hbm(after))
+    )(kept, got, in_hbm(after))
 
 
 def selected(index_rows, table_ref):
@@ -329,16 +342,12 @@
     return dot(jnp.concatenate(picks, axis=0), table_ref[...]).astype(BF16)
 
 
-def serve_kernel(chip_ref, hot_ref, index_ref, own_ref, other_ref, after_ref, out_ref):
+def serve_kernel(core_ref, hot_ref, index_ref, own_ref, other_ref, after_ref, out_ref):
     del after_ref
     half = LANES // 2
     per = out_ref.shape[0]
-    chip, core = chip_ref[0], chip_ref[1]
-    sources = []
-    for q in range(per):
-        apart = jnp.bitwise_xor(chip, pl.program_id(0) * per + q)
-        sources.append(apart // 4 + apart % 4 // 2 * 2 + apart % 2 * 4)
-    asked = lambda k: [index_ref[source, pl.ds(2 * chip + k, 1), :] for source in sources]
+    core = core_ref[0]
+    asked = lambda k: [index_ref[pl.program_id(0) * per + q, pl.ds(k, 1), :] for q in range(per)]
     own = selected(asked(core), own_ref)
     other = selected(asked(1 - core), other_ref)
     hot = hot_ref[0] != 0
@@ -358,7 +367,7 @@
             out_ref[q, 2] = other[q * LANES + half : (q + 1) * LANES]
 
 
-def serve(chip, hot, index, own, other, after):
+def serve(core, hot, index, own, other, after):
     groups = index.shape[0]
     width = own.shape[1]
     per = 4
@@ -379,7 +388,7 @@
         out_shape=jax.ShapeDtypeStruct((groups, 3, LANES // 2, width), BF16),
         compiler_params=params(60),
         cost_estimate=cost(4 * groups * LANES * own.shape[0] * width, 8 * own.size),
-    )(chip, hot, index, own, other, in_hbm(after))
+    )(core, hot, index, own, other, in_hbm(after))
 
 
 def donor_kernel(index_ref, table_ref, after_ref, out_ref):
@@ -471,7 +480,7 @@
             out_specs=[pl.BlockSpec(shape, lambda i, z: (0, 0))] * count,
             scratch_shapes=[pltpu.VMEM((width, taps * rows), F32)],
         ),
-        out_shape=[jax.ShapeDtypeStruct(shape, BF16 if k else F32) for k in range(count)],
+        out_shape=[pltpu.HBM(shape, BF16 if k else F32) for k in range(count)],
         compiler_params=params(12),
         cost_estimate=cost(2 * pieces.size, 3 * pieces.size),
     )(z, pieces)
@@ -564,21 +573,14 @@
     split = lambda v: v.reshape(length // DILATION_STEP, DILATION_STEP, width)
     core_id = core[None]
 
-    def widened(slots, bit):
-        other = lax.ppermute(slots, CHIPS, [(i, i ^ bit) for i in range(chips)])
-        return jnp.concatenate([slots, other], axis=0)
-
-    slots = widened(accept_pos.reshape(1, seq_count, -1), 4)
+    slots = lax.all_to_all(accept_pos.reshape(chips, 2, -1), CHIPS, 0, 0, tiled=True)
     normed, near, far = norm_rows(core_id, trunk, ids, base_table, norm_gain)
-    slots = widened(slots, 2)
     borders = [(i, i + 1) for i in range(1, seq_count - 1, 2)]
     far = lax.ppermute(far, SEQ, borders + [(target, source) for source, target in borders])
+    slots, near = lax.optimization_barrier((slots, near))
     near = lax.ppermute(near, "core", swap)
     common = (normed, weight, split(trunk_acts), split(grad_out), ids, base_table)
     hidden_in, dconv_in, turned_rows = conv_inner(*common, rows)
-    slots, dconv_in = lax.optimization_barrier((slots, dconv_in))
-    slots = widened(slots, 1)
-    near, far, slots = lax.optimization_barrier((near, far, slots))
     hidden_out, sent, kept = edges_and_grad(core_id, near, far, *common, dconv_in, turned_rows)
     got = lax.ppermute(sent, "core", swap)
     accept_local = projected(hidden_in, hidden_out, accept_weight, kept)
@@ -590,7 +592,7 @@
     hot = (lax.dynamic_index_in_dim(counts, 2 * chip + 1 - core, 0) > slots.shape[2] // 2).astype(jnp.int32)
     donor_table = projected(hidden_in, hidden_out, donor_weight, chip_half)
     donor_emb = donor_rows(donor_pos.reshape(2 * chips, -1), donor_table, chip_half)
-    served = serve(jnp.stack([chip, core]), hot, slots, accept_local, accept_other, donor_emb)
+    served = serve(core_id, hot, slots, accept_local, accept_other, donor_emb)
     blocks = list(spread(lax.axis_index("z")[None], pieces, lax.axis_size("z")))
     served, blocks[0] = lax.optimization_barrier((served, blocks[0]))
     accepted = lax.all_to_all(served, CHIPS, 0, 0, tiled=True)

time: 123 us -> 117 us (0.951)
  Pallas kernels: 57.9 us -> 54.8 us
  other arithmetic: 2.59 us -> 0.58 us
  local copies, waits for them, and re-layouts: 2.05 us -> 0.05 us
    all_to_all x0 -> x1, starting transfers between devices: none -> 7.47 us  [on_device(): lax.all_to_all(accept_pos.reshape(chips, 2, -1), CHIPS, 0, 0, tiled=True)]
    ppermute x3 -> x0, starting transfers between devices: 6.93 us -> none  [widened(): other = lax.ppermute(slots, CHIPS, [(i, i ^ bit) for i in range(chips)])]
    ppermute x3 -> x0, waiting for transfers between devices: 3.06 us -> none  [widened(): other = lax.ppermute(slots, CHIPS, [(i, i ^ bit) for i in range(chips)])]
    all_to_all x1, waiting for transfers between devices: 2.23 us -> 4.83 us  [on_device(): pieces = lax.all_to_all(chip_half, CHIPS, 0, 0, tiled=True)]
    unnamed x10 -> x22, local copies, waits for them, and re-layouts: 2.05 us -> 0.05 us
    pallas_call x1, Pallas kernels: 3.85 us -> 1.91 us  [join(): pl.pallas_call(join_kernel, grid=(4,), in_specs=[block, block, pl.BlockSp...]
    ppermute x1, starting transfers between devices: 0.01 us -> 1.65 us  [on_device(): near = lax.ppermute(near, 'core', swap)]
    concatenate x3 -> x0, other arithmetic: 1.34 us -> none  [widened(): return jnp.concatenate([slots, other], axis=0)]
  transfers between devices with their start and end apart: 17 -> 15, of which waited for: 7 -> 6; matrix products, arithmetic and copies ran while one was open for 2% -> 1% of each run, Pallas kernels for 33% -> 33%
where the time goes in v4:
time: 117 us; the launch traced here: 115 us
  Pallas kernels  54.8 us (47%)
  starting transfers between devices  43.8 us (37%)
  waiting for transfers between devices  14.1 us (12%)
  between operations  1.43 us (1%)
    ppermute x7, starting transfers between devices, dp_sum(): lax.ppermute(outs[step], 'z', [(i, (i + step) % nz) for i in range(nz)])  18.4 us
    pallas_call x1, Pallas kernels, edges_and_grad(): pl.pallas_call(functools.partial(edge_kernel, rows=rows), grid_spec=pltpu...  11.5 us
    pallas_call x2, Pallas kernels, projected(): pl.pallas_call(table_kernel, grid=(width // TILE,), in_specs=[pl.BlockSpe...  9.35 us
    all_to_all x1, starting transfers between devices, on_device(): lax.all_to_all(accept_pos.reshape(chips, 2, -1), CHIPS, 0, 0, tiled=True)  7.47 us
    pallas_call x1, Pallas kernels, conv_inner(): pl.pallas_call(functools.partial(inner_kernel, rows=rows), grid=(width //...  7.43 us
    all_to_all x1, starting transfers between devices, on_device(): pieces = lax.all_to_all(chip_half, CHIPS, 0, 0, tiled=True)  7.05 us
    pallas_call x1, Pallas kernels, serve(): pl.pallas_call(serve_kernel, grid_spec=pltpu.PrefetchScalarGridSpec(num_s...  6.69 us
    pallas_call x1, Pallas kernels, donor_rows(): pl.pallas_call(donor_kernel, grid=(count // per,), in_specs=[pl.BlockSpec...  6.53 us
  transfers between devices with their start and end apart: 15, of which 6 were waited for; matrix products, arithmetic and copies ran while one was open for 1% of the time, Pallas kernels for 33%

profile of v4, /device:TPU:2, one launch (start us, length us, event | category | flops | bytes accessed | tf_op | source)
XLA Modules:
  0.0 114.7 jit_solution(14485323849623445319)
XLA Ops:
  0.6 7.5 %all-to-all-start = ((s32[8,2,128]{2,1,0:T(2,128)}), s32[8,2,128]{2,1,0:T(2,128)S(1)}, u32[]{:S(2)}, u32[]{:S(2)}) async-start(s32[8,2,128]{2,1,0:T(2,128)} %bitcast.31), calls=%async_computation | async-start | bytes 16384 | tf_op jit(solution)/shard_map/all_to_all | solution.py:576
  8.1 4.6 %shard_map.122 = (bf16[1024,768]{1,0:T(8,128)(2,1)}, bf16[256,768]{1,0:T(8,128)(2,1)}, bf16[256,768]{1,0:T(8,128)(2,1)}) custom-call(s32[1]{0:T(128)} %bitcast.core_ref, bf16[1024,768]{1,0:T(8,128)(2,1)} %bitcast.15, s32[8,128]{1,0:T(8,128)} %bitcast.28, f32[4,768]{1,0:T(4,128)} %table_ref.5, f32[768]{0:T(1024)} %gain_ref.1), custom_call_target="tpu_custom_call" | custom-call | flops 7864320 | bytes 3145728 | tf_op jit(solution)/shard_map/pallas_call | solution.py:82
  12.7 1.9 %collective-permute-start.1 = (bf16[256,768]{1,0:T(8,128)(2,1)}, bf16[256,768]{1,0:T(8,128)(2,1)S(1)}, u32[]{:S(2)}, u32[]{:S(2)}) collective-permute-start(bf16[256,768]{1,0:T(8,128)(2,1)} %get-tuple-element.29), channel_id=1, source_target_pairs={{1,2},{3,4},{5,6},{7,8},{9,10},{11,12},{13,14},{2,1},{4,3},{6,5},{... | collective-permute-start | bytes 1179656 | tf_op jit(solution)/shard_map/ppermute | solution.py:579
  14.6 0.0 all-to-all-done.index_ref
  14.6 0.0 copy-start.3
  14.6 1.7 %collective-permute-start = (bf16[256,768]{1,0:T(8,128)(2,1)}, bf16[256,768]{1,0:T(8,128)(2,1)S(1)}, u32[]{:S(2)}, u32[]{:S(2)}) collective-permute-start(bf16[256,768]{1,0:T(8,128)(2,1)} %get-tuple-element.28), channel_id=1, source_target_pairs={{0,1},{1,0},{2,3},{3,2},{4,5},{5,4},{6,7},{7,6},{8,9},{9,8},{10,11... | collective-permute-start | bytes 1179656 | tf_op jit(solution)/shard_map/ppermute | solution.py:581
  16.3 7.4 %shard_map.123 = (bf16[512,768]{1,0:T(8,128)(2,1)}, bf16[512,768]{1,0:T(8,128)(2,1)}, bf16[8,2,48,1024]{3,2,1,0:T(8,128)(2,1)}) custom-call(bf16[1024,768]{1,0:T(8,128)(2,1)} %get-tuple-element.25.n_ref, bf16[3,768,768]{2,1,0:T(8,128)(2,1)} %bitcast.24, bf16[4,256,768]{2,1,0:T(8,128)(2,1)} %bitcast.16, bf16[4,256,768]{2,1,0:T(8,128)(2,1)} %bitcast.17, ...), custom_call_target="tpu_custom_call" | custom-call | flops 1811939328 | bytes 6291456 | tf_op jit(solution)/shard_map/pallas_call | solution.py:164
  23.7 0.0 copy-done.3
  23.7 0.0 collective-permute-done.1.far_ref
  23.7 0.0 collective-permute-done.near_ref
  23.7 11.5 %shard_map.124 = (bf16[512,768]{1,0:T(8,128)(2,1)}, bf16[8,3,48,768]{3,2,1,0:T(8,128)(2,1)}, bf16[8,3,48,768]{3,2,1,0:T(8,128)(2,1)S(1)}) custom-call(s32[1]{0:T(128)} %bitcast.core_ref, bf16[256,768]{1,0:T(8,128)(2,1)S(1)} %collective-permute-done.near_ref, bf16[256,768]{1,0:T(8,128)(2,1)S(1)} %collective-permute-done.1.far_ref, ...), custom_call_target="tpu_custom_call" | custom-call | flops 5435817984 | bytes 15728640 | tf_op jit(solution)/shard_map/pallas_call | solution.py:243
  35.3 0.1 collective-permute-start.2
  35.4 4.7 %shard_map.125.after_ref.own_ref = bf16[1024,768]{1,0:T(8,128)(2,1)} custom-call(bf16[512,768]{1,0:T(8,128)(2,1)} %get-tuple-element.26.inner_ref, bf16[512,768]{1,0:T(8,128)(2,1)} %get-tuple-element.32.outer_ref, bf16[768,768]{1,0:T(8,128)(2,1)} %weight_ref.2, bf16[8,3,48,768]{3,2,1,0:T(8,128)(2,1)S(1)} %get-tuple-element.33.after_ref.kept_ref), custom_call_target="tpu_custom_call" | custom-call | flops 1207959552 | bytes 3145728 | tf_op jit(solution)/shard_map/pallas_call | solution.py:287
  40.1 0.5 collective-permute-start.3
  40.5 0.0 collective-permute-done.2.got_ref
  40.5 1.9 %shard_map.126.after_ref = bf16[8,3,48,768]{3,2,1,0:T(8,128)(2,1)} custom-call(bf16[8,3,48,768]{3,2,1,0:T(8,128)(2,1)S(1)} %get-tuple-element.33.after_ref.kept_ref, bf16[8,3,48,768]{3,2,1,0:T(8,128)(2,1)S(1)} %collective-permute-done.2.got_ref, bf16[1024,768]{1,0:T(8,128)(2,1)} %shard_map.125.after_ref.own_ref), custom_call_target="tpu_custom_call" | custom-call | flops 884736 | bytes 5308416 | tf_op jit(solution)/shard_map/pallas_call | solution.py:317
  42.5 0.0 copy-start.2
  42.5 0.0 copy-start
  42.5 7.0 %all-to-all-start.1 = ((bf16[8,3,48,768]{3,2,1,0:T(8,128)(2,1)}), bf16[8,3,48,768]{3,2,1,0:T(8,128)(2,1)S(1)}, u32[]{:S(2)}, u32[]{:S(2)}) async-start(bf16[8,3,48,768]{3,2,1,0:T(8,128)(2,1)} %shard_map.126.after_ref), calls=%async_computation.1 | async-start | bytes 3538944 | tf_op jit(solution)/shard_map/all_to_all | solution.py:588
  49.5 0.0 copy-done.2
  49.5 0.6 fusion
  50.7 0.0 copy-done
  50.8 4.7 %shard_map.127.table_ref = bf16[1024,768]{1,0:T(8,128)(2,1)} custom-call(bf16[512,768]{1,0:T(8,128)(2,1)} %get-tuple-element.26.inner_ref, bf16[512,768]{1,0:T(8,128)(2,1)} %get-tuple-element.32.outer_ref, bf16[768,768]{1,0:T(8,128)(2,1)} %weight_ref.3, bf16[8,3,48,768]{3,2,1,0:T(8,128)(2,1)S(1)} %copy-done), custom_call_target="tpu_custom_call" | custom-call | flops 1207959552 | bytes 3145728 | tf_op jit(solution)/shard_map/pallas_call | solution.py:287
  55.4 6.5 %shard_map.128.after_ref.donor_ref = bf16[2048,768]{1,0:T(8,128)(2,1)} custom-call(s32[16,128]{1,0:T(8,128)} %bitcast.32, bf16[1024,768]{1,0:T(8,128)(2,1)} %shard_map.127.table_ref, bf16[8,3,48,768]{3,2,1,0:T(8,128)(2,1)} %shard_map.126.after_ref), custom_call_target="tpu_custom_call" | custom-call | flops 3221225472 | bytes 7864320 | tf_op jit(solution)/shard_map/pallas_call | solution.py:406
  61.9 0.0 collective-permute-done.3.other_ref
  62.0 6.7 %shard_map.129 = bf16[8,3,64,768]{3,2,1,0:T(8,128)(2,1)} custom-call(s32[1]{0:T(128)} %bitcast.core_ref, s32[1]{0:T(128)} %bitcast.9.hot_ref, s32[8,2,128]{2,1,0:T(2,128)} %copy-done.3, bf16[1024,768]{1,0:T(8,128)(2,1)} %shard_map.125.after_ref.own_ref, bf16[1024,768]{1,0:T(8,128)(2,1)} %collective-permute-done.3.other_ref, ...), custom_call_target="tpu_custom_call" | custom-call | flops 3221225472 | bytes 6291456 | tf_op jit(solution)/shard_map/pallas_call | solution.py:375
  68.6 4.8 %all-to-all-done.1.pieces_ref = bf16[8,3,48,768]{3,2,1,0:T(8,128)(2,1)S(1)} async-done(((bf16[8,3,48,768]{3,2,1,0:T(8,128)(2,1)}), bf16[8,3,48,768]{3,2,1,0:T(8,128)(2,1)S(1)}, u32[]{:S(2)}, u32[]{:S(2)}) %all-to-all-start.1) | async-done | bytes 1769504 | tf_op jit(solution)/shard_map/all_to_all | solution.py:588
  73.5 1.1 shard_map.130
  74.6 0.0 copy-start.10
  74.6 0.0 copy-start.9
  74.6 0.0 copy-start.7
  74.6 0.0 copy-start.6
  74.6 0.0 copy-start.5
  74.6 0.0 copy-start.4
  74.6 0.0 copy-start.1
  74.7 6.0 %all-to-all-start.2 = ((bf16[8,3,64,768]{3,2,1,0:T(8,128)(2,1)}), bf16[8,3,64,768]{3,2,1,0:T(8,128)(2,1)S(1)}, u32[]{:S(2)}, u32[]{:S(2)}) async-start(bf16[8,3,64,768]{3,2,1,0:T(8,128)(2,1)} %shard_map.129), calls=%async_computation.2 | async-start | bytes 4718592 | tf_op jit(solution)/shard_map/all_to_all | solution.py:598
  80.6 0.0 copy-done.10
  80.6 1.9 %collective-permute-start.4 = (bf16[96,144]{1,0:T(8,128)(2,1)S(1)}, bf16[96,144]{1,0:T(8,128)(2,1)S(1)}, u32[]{:S(2)}, u32[]{:S(2)}) collective-permute-start(bf16[96,144]{1,0:T(8,128)(2,1)S(1)} %copy-done.10), channel_id=1, source_target_pairs={{0,32},{32,64},{64,96},{96,128},{128,160},{160,192},{192,224},{224... | collective-permute-start | bytes 82952 | tf_op jit(solution)/shard_map/ppermute | solution.py:543
  82.5 0.0 copy-done.9
  82.5 3.3 %collective-permute-start.5 = (bf16[96,144]{1,0:T(8,128)(2,1)S(1)}, bf16[96,144]{1,0:T(8,128)(2,1)S(1)}, u32[]{:S(2)}, u32[]{:S(2)}) collective-permute-start(bf16[96,144]{1,0:T(8,128)(2,1)S(1)} %copy-done.9), channel_id=1, source_target_pairs={{0,64},{32,96},{64,128},{96,160},{128,192},{160,224},{192,0},{224,... | collective-permute-start | bytes 82952 | tf_op jit(solution)/shard_map/ppermute | solution.py:543
  85.8 0.0 copy-done.8
  85.8 4.1 %collective-permute-start.6 = (bf16[96,144]{1,0:T(8,128)(2,1)S(1)}, bf16[96,144]{1,0:T(8,128)(2,1)S(1)}, u32[]{:S(2)}, u32[]{:S(2)}) collective-permute-start(bf16[96,144]{1,0:T(8,128)(2,1)S(1)} %copy-done.8), channel_id=1, source_target_pairs={{0,96},{32,128},{64,160},{96,192},{128,224},{160,0},{192,32},{224,... | collective-permute-start | bytes 82952 | tf_op jit(solution)/shard_map/ppermute | solution.py:543
  89.9 0.0 copy-done.7
  89.9 0.5 collective-permute-start.7
  90.4 0.0 copy-done.6
  90.4 4.9 %collective-permute-start.8 = (bf16[96,144]{1,0:T(8,128)(2,1)S(1)}, bf16[96,144]{1,0:T(8,128)(2,1)S(1)}, u32[]{:S(2)}, u32[]{:S(2)}) collective-permute-start(bf16[96,144]{1,0:T(8,128)(2,1)S(1)} %copy-done.6), channel_id=1, source_target_pairs={{0,160},{32,192},{64,224},{96,0},{128,32},{160,64},{192,96},{224,1... | collective-permute-start | bytes 82952 | tf_op jit(solution)/shard_map/ppermute | solution.py:543
  95.3 0.0 collective-permute-done.4.refs_0_
  95.3 0.0 copy-done.5
  95.4 2.7 %collective-permute-start.9 = (bf16[96,144]{1,0:T(8,128)(2,1)S(1)}, bf16[96,144]{1,0:T(8,128)(2,1)S(1)}, u32[]{:S(2)}, u32[]{:S(2)}) collective-permute-start(bf16[96,144]{1,0:T(8,128)(2,1)S(1)} %copy-done.5), channel_id=1, source_target_pairs={{0,192},{32,224},{64,0},{96,32},{128,64},{160,96},{192,128},{224,1... | collective-permute-start | bytes 82952 | tf_op jit(solution)/shard_map/ppermute | solution.py:543
  98.0 0.0 collective-permute-done.5.refs_1_
  98.0 0.0 copy-done.4
  98.0 1.0 collective-permute-start.10
  99.0 0.0 collective-permute-done.6.refs_2_
  99.0 0.0 collective-permute-done.7.refs_3_
  99.0 1.1 collective-permute-done.8.refs_4_
  100.1 1.3 %collective-permute-done.9.refs_5_ = bf16[96,144]{1,0:T(8,128)(2,1)S(1)} collective-permute-done((bf16[96,144]{1,0:T(8,128)(2,1)S(1)}, bf16[96,144]{1,0:T(8,128)(2,1)S(1)}, u32[]{:S(2)}, u32[]{:S(2)}) %collective-permute-start.9) | collective-permute-done | bytes 27680 | tf_op jit(solution)/shard_map/ppermute | solution.py:543
  101.4 0.7 collective-permute-done.10.refs_6_
  102.1 0.0 copy-done.1
  102.1 0.1 shard_map.132
  102.2 0.8 collective-permute-start.11
  103.0 4.7 %collective-permute-done.11.got_ref = bf16[48,144]{1,0:T(8,128)(2,1)S(1)} collective-permute-done((bf16[48,144]{1,0:T(8,128)(2,1)S(1)}, bf16[48,144]{1,0:T(8,128)(2,1)S(1)}, u32[]{:S(2)}, u32[]{:S(2)}) %collective-permute-start.11) | collective-permute-done | bytes 13856 | tf_op jit(solution)/shard_map/ppermute | solution.py:547
  107.7 0.7 shard_map.133
  108.4 1.4 %all-to-all-done.2.accepted_ref = bf16[8,3,64,768]{3,2,1,0:T(8,128)(2,1)S(1)} async-done(((bf16[8,3,64,768]{3,2,1,0:T(8,128)(2,1)}), bf16[8,3,64,768]{3,2,1,0:T(8,128)(2,1)S(1)}, u32[]{:S(2)}, u32[]{:S(2)}) %all-to-all-start.2) | async-done | bytes 2359328 | tf_op jit(solution)/shard_map/all_to_all | solution.py:598
  109.8 4.9 %shard_map.131 = bf16[2048,768]{1,0:T(8,128)(2,1)} custom-call(s32[1]{0:T(128)} %bitcast.core_ref, s32[16]{0:T(128)S(1)} %bitcast.14, bf16[2048,768]{1,0:T(8,128)(2,1)} %shard_map.128.after_ref.donor_ref, bf16[8,3,64,768]{3,2,1,0:T(8,128)(2,1)S(1)} %all-to-all-done.2.accepted_ref), custom_call_target="tpu_custom_call" | custom-call | flops 3145728 | bytes 9437184 | tf_op jit(solution)/shard_map/pallas_call | solution.py:443
  (1 shorter events, 0.0 us)
Async XLA Ops:
  0.6 14.0 %all-to-all-start = ((s32[8,2,128]{2,1,0:T(2,128)}), s32[8,2,128]{2,1,0:T(2,128)S(1)}, u32[]{:S(2)}, u32[]{:S(2)}) async-start(s32[8,2,128]{2,1,0:T(2,128)} %bitcast.31), calls=%async_computation | async-start | bytes 16384 | tf_op jit(solution)/shard_map/all_to_all | solution.py:576
  12.7 11.0 %collective-permute-start.1 = (bf16[256,768]{1,0:T(8,128)(2,1)}, bf16[256,768]{1,0:T(8,128)(2,1)S(1)}, u32[]{:S(2)}, u32[]{:S(2)}) collective-permute-start(bf16[256,768]{1,0:T(8,128)(2,1)} %get-tuple-element.29), channel_id=1, source_target_pairs={{1,2},{3,4},{5,6},{7,8},{9,10},{11,12},{13,14},{2,1},{4,3},{6,5},{... | collective-permute-start | bytes 1179656 | tf_op jit(solution)/shard_map/ppermute | solution.py:579
  14.6 9.1 %copy-start.3 = (s32[8,2,128]{2,1,0:T(2,128)}, s32[8,2,128]{2,1,0:T(2,128)S(1)}, u32[]{:S(2)}) copy-start(s32[8,2,128]{2,1,0:T(2,128)S(1)} %all-to-all-done.index_ref) | copy-start | bytes 24580
  14.6 9.1 %collective-permute-start = (bf16[256,768]{1,0:T(8,128)(2,1)}, bf16[256,768]{1,0:T(8,128)(2,1)S(1)}, u32[]{:S(2)}, u32[]{:S(2)}) collective-permute-start(bf16[256,768]{1,0:T(8,128)(2,1)} %get-tuple-element.28), channel_id=1, source_target_pairs={{0,1},{1,0},{2,3},{3,2},{4,5},{5,4},{6,7},{7,6},{8,9},{9,8},{10,11... | collective-permute-start | bytes 1179656 | tf_op jit(solution)/shard_map/ppermute | solution.py:581
  35.3 5.3 %collective-permute-start.2 = (bf16[8,3,48,768]{3,2,1,0:T(8,128)(2,1)}, bf16[8,3,48,768]{3,2,1,0:T(8,128)(2,1)S(1)}, u32[]{:S(2)}, u32[]{:S(2)}) collective-permute-start(bf16[8,3,48,768]{3,2,1,0:T(8,128)(2,1)} %get-tuple-element.34), channel_id=1, source_target_pairs={{0,1},{1,0},{2,3},{3,2},{4,5},{5,4},{6,7},{7,6},{8,9},{9,8},{10,11... | collective-permute-start | bytes 5308424 | tf_op jit(solution)/shard_map/ppermute | solution.py:585
  40.1 21.9 %collective-permute-start.3 = (bf16[1024,768]{1,0:T(8,128)(2,1)}, bf16[1024,768]{1,0:T(8,128)(2,1)}, u32[]{:S(2)}, u32[]{:S(2)}) collective-permute-start(bf16[1024,768]{1,0:T(8,128)(2,1)} %shard_map.125.after_ref.own_ref), channel_id=1, source_target_pairs={{0,1},{1,0},{2,3},{3,2},{4,5},{5,4},{6,7},{7,6},{8,9},{9,8},{10,11... | collective-permute-start | bytes 4718600 | tf_op jit(solution)/shard_map/ppermute | solution.py:590
  42.5 7.1 %copy-start.2 = (s32[1,16]{1,0:T(1,128)S(1)}, s32[1,16]{1,0:T(1,128)}, u32[]{:S(2)}) copy-start(s32[1,16]{1,0:T(1,128)} %param.19) | copy-start | bytes 196
  42.5 8.3 %copy-start = (bf16[8,3,48,768]{3,2,1,0:T(8,128)(2,1)S(1)}, bf16[8,3,48,768]{3,2,1,0:T(8,128)(2,1)}, u32[]{:S(2)}) copy-start(bf16[8,3,48,768]{3,2,1,0:T(8,128)(2,1)} %shard_map.126.after_ref) | copy-start | bytes 5308420
  42.5 31.0 %all-to-all-start.1 = ((bf16[8,3,48,768]{3,2,1,0:T(8,128)(2,1)}), bf16[8,3,48,768]{3,2,1,0:T(8,128)(2,1)S(1)}, u32[]{:S(2)}, u32[]{:S(2)}) async-start(bf16[8,3,48,768]{3,2,1,0:T(8,128)(2,1)} %shard_map.126.after_ref), calls=%async_computation.1 | async-start | bytes 3538944 | tf_op jit(solution)/shard_map/all_to_all | solution.py:588
  74.6 6.0 %copy-start.10 = (bf16[96,144]{1,0:T(8,128)(2,1)S(1)}, bf16[96,144]{1,0:T(8,128)(2,1)}, u32[]{:S(2)}) copy-start(bf16[96,144]{1,0:T(8,128)(2,1)} %get-tuple-element.39) | copy-start | bytes 82948
  74.6 7.9 %copy-start.9 = (bf16[96,144]{1,0:T(8,128)(2,1)S(1)}, bf16[96,144]{1,0:T(8,128)(2,1)}, u32[]{:S(2)}) copy-start(bf16[96,144]{1,0:T(8,128)(2,1)} %get-tuple-element.40) | copy-start | bytes 82948
  74.6 11.2 %copy-start.8 = (bf16[96,144]{1,0:T(8,128)(2,1)S(1)}, bf16[96,144]{1,0:T(8,128)(2,1)}, u32[]{:S(2)}) copy-start(bf16[96,144]{1,0:T(8,128)(2,1)} %get-tuple-element.41) | copy-start | bytes 82948
  74.6 15.3 %copy-start.7 = (bf16[96,144]{1,0:T(8,128)(2,1)S(1)}, bf16[96,144]{1,0:T(8,128)(2,1)}, u32[]{:S(2)}) copy-start(bf16[96,144]{1,0:T(8,128)(2,1)} %get-tuple-element.42) | copy-start | bytes 82948
  74.6 15.8 %copy-start.6 = (bf16[96,144]{1,0:T(8,128)(2,1)S(1)}, bf16[96,144]{1,0:T(8,128)(2,1)}, u32[]{:S(2)}) copy-start(bf16[96,144]{1,0:T(8,128)(2,1)} %get-tuple-element.43) | copy-start | bytes 82948
  74.6 20.7 %copy-start.5 = (bf16[96,144]{1,0:T(8,128)(2,1)S(1)}, bf16[96,144]{1,0:T(8,128)(2,1)}, u32[]{:S(2)}) copy-start(bf16[96,144]{1,0:T(8,128)(2,1)} %get-tuple-element.44) | copy-start | bytes 82948
  74.6 23.4 %copy-start.4 = (bf16[96,144]{1,0:T(8,128)(2,1)S(1)}, bf16[96,144]{1,0:T(8,128)(2,1)}, u32[]{:S(2)}) copy-start(bf16[96,144]{1,0:T(8,128)(2,1)} %get-tuple-element.45) | copy-start | bytes 82948
  74.6 27.5 %copy-start.1 = (f32[96,144]{1,0:T(8,128)S(1)}, f32[96,144]{1,0:T(8,128)}, u32[]{:S(2)}) copy-start(f32[96,144]{1,0:T(8,128)} %get-tuple-element.38.own_ref) | copy-start | bytes 165892
  74.7 35.2 %all-to-all-start.2 = ((bf16[8,3,64,768]{3,2,1,0:T(8,128)(2,1)}), bf16[8,3,64,768]{3,2,1,0:T(8,128)(2,1)S(1)}, u32[]{:S(2)}, u32[]{:S(2)}) async-start(bf16[8,3,64,768]{3,2,1,0:T(8,128)(2,1)} %shard_map.129), calls=%async_computation.2 | async-start | bytes 4718592 | tf_op jit(solution)/shard_map/all_to_all | solution.py:598
  80.6 14.7 %collective-permute-start.4 = (bf16[96,144]{1,0:T(8,128)(2,1)S(1)}, bf16[96,144]{1,0:T(8,128)(2,1)S(1)}, u32[]{:S(2)}, u32[]{:S(2)}) collective-permute-start(bf16[96,144]{1,0:T(8,128)(2,1)S(1)} %copy-done.10), channel_id=1, source_target_pairs={{0,32},{32,64},{64,96},{96,128},{128,160},{160,192},{192,224},{224... | collective-permute-start | bytes 82952 | tf_op jit(solution)/shard_map/ppermute | solution.py:543
  82.5 15.5 %collective-permute-start.5 = (bf16[96,144]{1,0:T(8,128)(2,1)S(1)}, bf16[96,144]{1,0:T(8,128)(2,1)S(1)}, u32[]{:S(2)}, u32[]{:S(2)}) collective-permute-start(bf16[96,144]{1,0:T(8,128)(2,1)S(1)} %copy-done.9), channel_id=1, source_target_pairs={{0,64},{32,96},{64,128},{96,160},{128,192},{160,224},{192,0},{224,... | collective-permute-start | bytes 82952 | tf_op jit(solution)/shard_map/ppermute | solution.py:543
  85.8 13.2 %collective-permute-start.6 = (bf16[96,144]{1,0:T(8,128)(2,1)S(1)}, bf16[96,144]{1,0:T(8,128)(2,1)S(1)}, u32[]{:S(2)}, u32[]{:S(2)}) collective-permute-start(bf16[96,144]{1,0:T(8,128)(2,1)S(1)} %copy-done.8), channel_id=1, source_target_pairs={{0,96},{32,128},{64,160},{96,192},{128,224},{160,0},{192,32},{224,... | collective-permute-start | bytes 82952 | tf_op jit(solution)/shard_map/ppermute | solution.py:543
  89.9 9.2 %collective-permute-start.7 = (bf16[96,144]{1,0:T(8,128)(2,1)S(1)}, bf16[96,144]{1,0:T(8,128)(2,1)S(1)}, u32[]{:S(2)}, u32[]{:S(2)}) collective-permute-start(bf16[96,144]{1,0:T(8,128)(2,1)S(1)} %copy-done.7), channel_id=1, source_target_pairs={{0,128},{32,160},{64,192},{96,224},{128,0},{160,32},{192,64},{224,... | collective-permute-start | bytes 82952 | tf_op jit(solution)/shard_map/ppermute | solution.py:543
  90.4 9.7 %collective-permute-start.8 = (bf16[96,144]{1,0:T(8,128)(2,1)S(1)}, bf16[96,144]{1,0:T(8,128)(2,1)S(1)}, u32[]{:S(2)}, u32[]{:S(2)}) collective-permute-start(bf16[96,144]{1,0:T(8,128)(2,1)S(1)} %copy-done.6), channel_id=1, source_target_pairs={{0,160},{32,192},{64,224},{96,0},{128,32},{160,64},{192,96},{224,1... | collective-permute-start | bytes 82952 | tf_op jit(solution)/shard_map/ppermute | solution.py:543
  95.4 6.1 %collective-permute-start.9 = (bf16[96,144]{1,0:T(8,128)(2,1)S(1)}, bf16[96,144]{1,0:T(8,128)(2,1)S(1)}, u32[]{:S(2)}, u32[]{:S(2)}) collective-permute-start(bf16[96,144]{1,0:T(8,128)(2,1)S(1)} %copy-done.5), channel_id=1, source_target_pairs={{0,192},{32,224},{64,0},{96,32},{128,64},{160,96},{192,128},{224,1... | collective-permute-start | bytes 82952 | tf_op jit(solution)/shard_map/ppermute | solution.py:543
  98.0 4.1 %collective-permute-start.10 = (bf16[96,144]{1,0:T(8,128)(2,1)S(1)}, bf16[96,144]{1,0:T(8,128)(2,1)S(1)}, u32[]{:S(2)}, u32[]{:S(2)}) collective-permute-start(bf16[96,144]{1,0:T(8,128)(2,1)S(1)} %copy-done.4), channel_id=1, source_target_pairs={{0,224},{32,0},{64,32},{96,64},{128,96},{160,128},{192,160},{224,1... | collective-permute-start | bytes 82952 | tf_op jit(solution)/shard_map/ppermute | solution.py:543
  102.2 5.5 %collective-permute-start.11 = (bf16[48,144]{1,0:T(8,128)(2,1)S(1)}, bf16[48,144]{1,0:T(8,128)(2,1)S(1)}, u32[]{:S(2)}, u32[]{:S(2)}) collective-permute-start(bf16[48,144]{1,0:T(8,128)(2,1)S(1)} %get-tuple-element.47), channel_id=1, source_target_pairs={{0,16},{16,0},{1,17},{17,1},{2,18},{18,2},{3,19},{19,3},{4,20},{20... | collective-permute-start | bytes 41480 | tf_op jit(solution)/shard_map/ppermute | solution.py:547

commit v5 on v4

--- a/solution.py
+++ b/solution.py
@@ -64,34 +64,37 @@
     mean = jnp.mean(inputs * inputs, axis=-1, keepdims=True)
     normed = (inputs * lax.rsqrt(mean + 1e-06) * gain_ref[...][None, :]).astype(BF16)
     out_ref[...] = normed
+    chunk = near_ref.shape[0]
+    edge = jnp.where(i == 0, normed[:chunk], normed[normed.shape[0] - chunk :])
 
     @pl.when(i == jnp.where(core_ref[0] == 0, last, 0))
     def _():
-        near_ref[...] = normed
+        near_ref[...] = edge
 
     @pl.when(i == jnp.where(core_ref[0] == 0, 0, last))
     def _():
-        far_ref[...] = normed
+        far_ref[...] = edge
 
 
 def norm_rows(core, trunk, ids, table, gain):
     length, width = trunk.shape
     chunk = DILATION_STEP
+    block = length // 2
     whole = lambda i, c: (0, 0)
     edge = jax.ShapeDtypeStruct((chunk, width), BF16)
     return pl.pallas_call(
         norm_kernel,
         grid_spec=pltpu.PrefetchScalarGridSpec(
             num_scalar_prefetch=1,
-            grid=(length // chunk,),
+            grid=(length // block,),
             in_specs=[
-                pl.BlockSpec((chunk, width), lambda i, c: (i, 0)),
+                pl.BlockSpec((block, width), lambda i, c: (i, 0)),
                 pl.BlockSpec(ids.shape, whole),
                 pl.BlockSpec(table.shape, whole),
                 pl.BlockSpec(gain.shape, lambda i, c: (0,)),
             ],
             out_specs=[
-                pl.BlockSpec((chunk, width), lambda i, c: (i, 0)),
+                pl.BlockSpec((block, width), lambda i, c: (i, 0)),
                 pl.BlockSpec((chunk, width), whole),
                 pl.BlockSpec((chunk, width), whole),
             ],
@@ -438,7 +441,7 @@
 def pairs(core, counts, donor, accepted):
     groups = accepted.shape[0]
     width = donor.shape[1]
-    per = 2
+    per = 4
     rows = pl.BlockSpec((2 * per * LANES, width), lambda q, c, n: (q, 0))
     return pl.pallas_call(
         pair_kernel,
@@ -449,7 +452,7 @@
             out_specs=rows,
         ),
         out_shape=jax.ShapeDtypeStruct(donor.shape, BF16),
-        compiler_params=params(12),
+        compiler_params=params(16),
         cost_estimate=cost(2 * donor.size, 6 * donor.size),
     )(core, counts, in_hbm(donor), accepted)
 

time: 117 us -> 115 us (0.983)
  Pallas kernels: 54.8 us -> 52.9 us
  transfers between devices with their start and end apart: 15 -> 15, of which waited for: 6 -> 7; matrix products, arithmetic and copies ran while one was open for 1% -> 1% of each run, Pallas kernels for 33% -> 32%
where the time goes in v5:
time: 115 us; the launch traced here: 113 us
  Pallas kernels  52.9 us (46%)
  starting transfers between devices  43.4 us (38%)
  waiting for transfers between devices  14.6 us (13%)
  between operations  1.41 us (1%)
    ppermute x7, starting transfers between devices, dp_sum(): lax.ppermute(outs[step], 'z', [(i, (i + step) % nz) for i in range(nz)])  18.4 us
    pallas_call x1, Pallas kernels, edges_and_grad(): pl.pallas_call(functools.partial(edge_kernel, rows=rows), grid_spec=pltpu...  11.5 us
    pallas_call x2, Pallas kernels, projected(): pl.pallas_call(table_kernel, grid=(width // TILE,), in_specs=[pl.BlockSpe...  9.36 us
    all_to_all x1, starting transfers between devices, on_device(): lax.all_to_all(accept_pos.reshape(chips, 2, -1), CHIPS, 0, 0, tiled=True)  7.47 us
    pallas_call x1, Pallas kernels, conv_inner(): pl.pallas_call(functools.partial(inner_kernel, rows=rows), grid=(width //...  7.43 us
    all_to_all x1, starting transfers between devices, on_device(): pieces = lax.all_to_all(chip_half, CHIPS, 0, 0, tiled=True)  7.23 us
    pallas_call x1, Pallas kernels, serve(): pl.pallas_call(serve_kernel, grid_spec=pltpu.PrefetchScalarGridSpec(num_s...  6.69 us
    pallas_call x1, Pallas kernels, donor_rows(): pl.pallas_call(donor_kernel, grid=(count // per,), in_specs=[pl.BlockSpec...  6.53 us
  transfers between devices with their start and end apart: 15, of which 7 were waited for; matrix products, arithmetic and copies ran while one was open for 1% of the time, Pallas kernels for 32%

profile of v5, /device:TPU:2, one launch (start us, length us, event | category | flops | bytes accessed | tf_op | source)
XLA Modules:
  0.0 113.0 jit_solution(12184380228654412830)
XLA Ops:
  0.6 7.5 %all-to-all-start = ((s32[8,2,128]{2,1,0:T(2,128)}), s32[8,2,128]{2,1,0:T(2,128)S(1)}, u32[]{:S(2)}, u32[]{:S(2)}) async-start(s32[8,2,128]{2,1,0:T(2,128)} %bitcast.31), calls=%async_computation | async-start | bytes 16384 | tf_op jit(solution)/shard_map/all_to_all | solution.py:579
  8.1 3.7 %shard_map.122 = (bf16[1024,768]{1,0:T(8,128)(2,1)}, bf16[256,768]{1,0:T(8,128)(2,1)}, bf16[256,768]{1,0:T(8,128)(2,1)}) custom-call(s32[1]{0:T(128)} %bitcast.core_ref, bf16[1024,768]{1,0:T(8,128)(2,1)} %bitcast.15, s32[8,128]{1,0:T(8,128)} %bitcast.28, f32[4,768]{1,0:T(4,128)} %table_ref.5, f32[768]{0:T(1024)} %gain_ref.1), custom_call_target="tpu_custom_call" | custom-call | flops 7864320 | bytes 3145728 | tf_op jit(solution)/shard_map/pallas_call | solution.py:85
  11.8 1.9 %collective-permute-start.1 = (bf16[256,768]{1,0:T(8,128)(2,1)}, bf16[256,768]{1,0:T(8,128)(2,1)S(1)}, u32[]{:S(2)}, u32[]{:S(2)}) collective-permute-start(bf16[256,768]{1,0:T(8,128)(2,1)} %get-tuple-element.29), channel_id=1, source_target_pairs={{1,2},{3,4},{5,6},{7,8},{9,10},{11,12},{13,14},{2,1},{4,3},{6,5},{... | collective-permute-start | bytes 1179656 | tf_op jit(solution)/shard_map/ppermute | solution.py:582
  13.8 0.6 all-to-all-done.index_ref
  14.4 0.0 copy-start.3
  14.4 1.1 collective-permute-start
  15.4 7.4 %shard_map.123 = (bf16[512,768]{1,0:T(8,128)(2,1)}, bf16[512,768]{1,0:T(8,128)(2,1)}, bf16[8,2,48,1024]{3,2,1,0:T(8,128)(2,1)}) custom-call(bf16[1024,768]{1,0:T(8,128)(2,1)} %get-tuple-element.25.n_ref, bf16[3,768,768]{2,1,0:T(8,128)(2,1)} %bitcast.24, bf16[4,256,768]{2,1,0:T(8,128)(2,1)} %bitcast.16, bf16[4,256,768]{2,1,0:T(8,128)(2,1)} %bitcast.17, ...), custom_call_target="tpu_custom_call" | custom-call | flops 1811939328 | bytes 6291456 | tf_op jit(solution)/shard_map/pallas_call | solution.py:167
  22.9 0.0 copy-done.3
  22.9 0.0 collective-permute-done.1.far_ref
  22.9 0.0 collective-permute-done.near_ref
  22.9 11.5 %shard_map.124 = (bf16[512,768]{1,0:T(8,128)(2,1)}, bf16[8,3,48,768]{3,2,1,0:T(8,128)(2,1)}, bf16[8,3,48,768]{3,2,1,0:T(8,128)(2,1)S(1)}) custom-call(s32[1]{0:T(128)} %bitcast.core_ref, bf16[256,768]{1,0:T(8,128)(2,1)S(1)} %collective-permute-done.near_ref, bf16[256,768]{1,0:T(8,128)(2,1)S(1)} %collective-permute-done.1.far_ref, ...), custom_call_target="tpu_custom_call" | custom-call | flops 5435817984 | bytes 15728640 | tf_op jit(solution)/shard_map/pallas_call | solution.py:246
  34.4 0.1 collective-permute-start.2
  34.5 4.7 %shard_map.125.after_ref.own_ref = bf16[1024,768]{1,0:T(8,128)(2,1)} custom-call(bf16[512,768]{1,0:T(8,128)(2,1)} %get-tuple-element.26.inner_ref, bf16[512,768]{1,0:T(8,128)(2,1)} %get-tuple-element.32.outer_ref, bf16[768,768]{1,0:T(8,128)(2,1)} %weight_ref.2, bf16[8,3,48,768]{3,2,1,0:T(8,128)(2,1)S(1)} %get-tuple-element.33.after_ref.kept_ref), custom_call_target="tpu_custom_call" | custom-call | flops 1207959552 | bytes 3145728 | tf_op jit(solution)/shard_map/pallas_call | solution.py:290
  39.2 0.5 collective-permute-start.3
  39.7 0.0 collective-permute-done.2.got_ref
  39.7 1.9 %shard_map.126.after_ref = bf16[8,3,48,768]{3,2,1,0:T(8,128)(2,1)} custom-call(bf16[8,3,48,768]{3,2,1,0:T(8,128)(2,1)S(1)} %get-tuple-element.33.after_ref.kept_ref, bf16[8,3,48,768]{3,2,1,0:T(8,128)(2,1)S(1)} %collective-permute-done.2.got_ref, bf16[1024,768]{1,0:T(8,128)(2,1)} %shard_map.125.after_ref.own_ref), custom_call_target="tpu_custom_call" | custom-call | flops 884736 | bytes 5308416 | tf_op jit(solution)/shard_map/pallas_call | solution.py:320
  41.6 0.0 copy-start.2
  41.6 0.0 copy-start
  41.6 7.2 %all-to-all-start.1 = ((bf16[8,3,48,768]{3,2,1,0:T(8,128)(2,1)}), bf16[8,3,48,768]{3,2,1,0:T(8,128)(2,1)S(1)}, u32[]{:S(2)}, u32[]{:S(2)}) async-start(bf16[8,3,48,768]{3,2,1,0:T(8,128)(2,1)} %shard_map.126.after_ref), calls=%async_computation.1 | async-start | bytes 3538944 | tf_op jit(solution)/shard_map/all_to_all | solution.py:591
  48.8 0.0 copy-done.2
  48.8 0.6 fusion
  50.1 0.0 copy-done
  50.1 4.7 %shard_map.127.table_ref = bf16[1024,768]{1,0:T(8,128)(2,1)} custom-call(bf16[512,768]{1,0:T(8,128)(2,1)} %get-tuple-element.26.inner_ref, bf16[512,768]{1,0:T(8,128)(2,1)} %get-tuple-element.32.outer_ref, bf16[768,768]{1,0:T(8,128)(2,1)} %weight_ref.3, bf16[8,3,48,768]{3,2,1,0:T(8,128)(2,1)S(1)} %copy-done), custom_call_target="tpu_custom_call" | custom-call | flops 1207959552 | bytes 3145728 | tf_op jit(solution)/shard_map/pallas_call | solution.py:290
  54.8 6.5 %shard_map.128.after_ref.donor_ref = bf16[2048,768]{1,0:T(8,128)(2,1)} custom-call(s32[16,128]{1,0:T(8,128)} %bitcast.32, bf16[1024,768]{1,0:T(8,128)(2,1)} %shard_map.127.table_ref, bf16[8,3,48,768]{3,2,1,0:T(8,128)(2,1)} %shard_map.126.after_ref), custom_call_target="tpu_custom_call" | custom-call | flops 3221225472 | bytes 7864320 | tf_op jit(solution)/shard_map/pallas_call | solution.py:409
  61.3 0.0 collective-permute-done.3.other_ref
  61.3 6.7 %shard_map.129 = bf16[8,3,64,768]{3,2,1,0:T(8,128)(2,1)} custom-call(s32[1]{0:T(128)} %bitcast.core_ref, s32[1]{0:T(128)} %bitcast.9.hot_ref, s32[8,2,128]{2,1,0:T(2,128)} %copy-done.3, bf16[1024,768]{1,0:T(8,128)(2,1)} %shard_map.125.after_ref.own_ref, bf16[1024,768]{1,0:T(8,128)(2,1)} %collective-permute-done.3.other_ref, ...), custom_call_target="tpu_custom_call" | custom-call | flops 3221225472 | bytes 6291456 | tf_op jit(solution)/shard_map/pallas_call | solution.py:378
  68.0 4.8 %all-to-all-done.1.pieces_ref = bf16[8,3,48,768]{3,2,1,0:T(8,128)(2,1)S(1)} async-done(((bf16[8,3,48,768]{3,2,1,0:T(8,128)(2,1)}), bf16[8,3,48,768]{3,2,1,0:T(8,128)(2,1)S(1)}, u32[]{:S(2)}, u32[]{:S(2)}) %all-to-all-start.1) | async-done | bytes 1769504 | tf_op jit(solution)/shard_map/all_to_all | solution.py:591
  72.8 1.1 shard_map.130
  73.9 0.0 copy-start.10
  73.9 0.0 copy-start.9
  73.9 0.0 copy-start.7
  73.9 0.0 copy-start.6
  74.0 0.0 copy-start.5
  74.0 0.0 copy-start.4
  74.0 0.0 copy-start.1
  74.0 6.0 %all-to-all-start.2 = ((bf16[8,3,64,768]{3,2,1,0:T(8,128)(2,1)}), bf16[8,3,64,768]{3,2,1,0:T(8,128)(2,1)S(1)}, u32[]{:S(2)}, u32[]{:S(2)}) async-start(bf16[8,3,64,768]{3,2,1,0:T(8,128)(2,1)} %shard_map.129), calls=%async_computation.2 | async-start | bytes 4718592 | tf_op jit(solution)/shard_map/all_to_all | solution.py:601
  80.0 0.0 copy-done.10
  80.0 1.9 %collective-permute-start.4 = (bf16[96,144]{1,0:T(8,128)(2,1)S(1)}, bf16[96,144]{1,0:T(8,128)(2,1)S(1)}, u32[]{:S(2)}, u32[]{:S(2)}) collective-permute-start(bf16[96,144]{1,0:T(8,128)(2,1)S(1)} %copy-done.10), channel_id=1, source_target_pairs={{0,32},{32,64},{64,96},{96,128},{128,160},{160,192},{192,224},{224... | collective-permute-start | bytes 82952 | tf_op jit(solution)/shard_map/ppermute | solution.py:546
  81.9 0.0 copy-done.9
  81.9 3.3 %collective-permute-start.5 = (bf16[96,144]{1,0:T(8,128)(2,1)S(1)}, bf16[96,144]{1,0:T(8,128)(2,1)S(1)}, u32[]{:S(2)}, u32[]{:S(2)}) collective-permute-start(bf16[96,144]{1,0:T(8,128)(2,1)S(1)} %copy-done.9), channel_id=1, source_target_pairs={{0,64},{32,96},{64,128},{96,160},{128,192},{160,224},{192,0},{224,... | collective-permute-start | bytes 82952 | tf_op jit(solution)/shard_map/ppermute | solution.py:546
  85.1 0.0 copy-done.8
  85.1 4.0 %collective-permute-start.6 = (bf16[96,144]{1,0:T(8,128)(2,1)S(1)}, bf16[96,144]{1,0:T(8,128)(2,1)S(1)}, u32[]{:S(2)}, u32[]{:S(2)}) collective-permute-start(bf16[96,144]{1,0:T(8,128)(2,1)S(1)} %copy-done.8), channel_id=1, source_target_pairs={{0,96},{32,128},{64,160},{96,192},{128,224},{160,0},{192,32},{224,... | collective-permute-start | bytes 82952 | tf_op jit(solution)/shard_map/ppermute | solution.py:546
  89.2 0.0 copy-done.7
  89.2 0.6 collective-permute-start.7
  89.8 0.0 copy-done.6
  89.8 4.9 %collective-permute-start.8 = (bf16[96,144]{1,0:T(8,128)(2,1)S(1)}, bf16[96,144]{1,0:T(8,128)(2,1)S(1)}, u32[]{:S(2)}, u32[]{:S(2)}) collective-permute-start(bf16[96,144]{1,0:T(8,128)(2,1)S(1)} %copy-done.6), channel_id=1, source_target_pairs={{0,160},{32,192},{64,224},{96,0},{128,32},{160,64},{192,96},{224,1... | collective-permute-start | bytes 82952 | tf_op jit(solution)/shard_map/ppermute | solution.py:546
  94.7 0.0 collective-permute-done.4.refs_0_
  94.7 0.0 copy-done.5
  94.7 2.6 %collective-permute-start.9 = (bf16[96,144]{1,0:T(8,128)(2,1)S(1)}, bf16[96,144]{1,0:T(8,128)(2,1)S(1)}, u32[]{:S(2)}, u32[]{:S(2)}) collective-permute-start(bf16[96,144]{1,0:T(8,128)(2,1)S(1)} %copy-done.5), channel_id=1, source_target_pairs={{0,192},{32,224},{64,0},{96,32},{128,64},{160,96},{192,128},{224,1... | collective-permute-start | bytes 82952 | tf_op jit(solution)/shard_map/ppermute | solution.py:546
  97.4 0.0 collective-permute-done.5.refs_1_
  97.4 0.0 copy-done.4
  97.4 1.0 collective-permute-start.10
  98.4 0.0 collective-permute-done.6.refs_2_
  98.4 0.0 collective-permute-done.7.refs_3_
  98.4 1.1 collective-permute-done.8.refs_4_
  99.5 1.3 %collective-permute-done.9.refs_5_ = bf16[96,144]{1,0:T(8,128)(2,1)S(1)} collective-permute-done((bf16[96,144]{1,0:T(8,128)(2,1)S(1)}, bf16[96,144]{1,0:T(8,128)(2,1)S(1)}, u32[]{:S(2)}, u32[]{:S(2)}) %collective-permute-start.9) | collective-permute-done | bytes 27680 | tf_op jit(solution)/shard_map/ppermute | solution.py:546
  100.8 0.7 collective-permute-done.10.refs_6_
  101.5 0.0 copy-done.1
  101.5 0.1 shard_map.132
  101.5 0.8 collective-permute-start.11
  102.3 4.8 %collective-permute-done.11.got_ref = bf16[48,144]{1,0:T(8,128)(2,1)S(1)} collective-permute-done((bf16[48,144]{1,0:T(8,128)(2,1)S(1)}, bf16[48,144]{1,0:T(8,128)(2,1)S(1)}, u32[]{:S(2)}, u32[]{:S(2)}) %collective-permute-start.11) | collective-permute-done | bytes 13856 | tf_op jit(solution)/shard_map/ppermute | solution.py:550
  107.0 0.7 shard_map.133
  107.8 1.4 %all-to-all-done.2.accepted_ref = bf16[8,3,64,768]{3,2,1,0:T(8,128)(2,1)S(1)} async-done(((bf16[8,3,64,768]{3,2,1,0:T(8,128)(2,1)}), bf16[8,3,64,768]{3,2,1,0:T(8,128)(2,1)S(1)}, u32[]{:S(2)}, u32[]{:S(2)}) %all-to-all-start.2) | async-done | bytes 2359328 | tf_op jit(solution)/shard_map/all_to_all | solution.py:601
  109.1 3.8 %shard_map.131 = bf16[2048,768]{1,0:T(8,128)(2,1)} custom-call(s32[1]{0:T(128)} %bitcast.core_ref, s32[16]{0:T(128)S(1)} %bitcast.14, bf16[2048,768]{1,0:T(8,128)(2,1)} %shard_map.128.after_ref.donor_ref, bf16[8,3,64,768]{3,2,1,0:T(8,128)(2,1)S(1)} %all-to-all-done.2.accepted_ref), custom_call_target="tpu_custom_call" | custom-call | flops 3145728 | bytes 9437184 | tf_op jit(solution)/shard_map/pallas_call | solution.py:446
  (1 shorter events, 0.0 us)
Async XLA Ops:
  0.6 13.7 %all-to-all-start = ((s32[8,2,128]{2,1,0:T(2,128)}), s32[8,2,128]{2,1,0:T(2,128)S(1)}, u32[]{:S(2)}, u32[]{:S(2)}) async-start(s32[8,2,128]{2,1,0:T(2,128)} %bitcast.31), calls=%async_computation | async-start | bytes 16384 | tf_op jit(solution)/shard_map/all_to_all | solution.py:579
  11.8 11.0 %collective-permute-start.1 = (bf16[256,768]{1,0:T(8,128)(2,1)}, bf16[256,768]{1,0:T(8,128)(2,1)S(1)}, u32[]{:S(2)}, u32[]{:S(2)}) collective-permute-start(bf16[256,768]{1,0:T(8,128)(2,1)} %get-tuple-element.29), channel_id=1, source_target_pairs={{1,2},{3,4},{5,6},{7,8},{9,10},{11,12},{13,14},{2,1},{4,3},{6,5},{... | collective-permute-start | bytes 1179656 | tf_op jit(solution)/shard_map/ppermute | solution.py:582
  14.4 8.5 %copy-start.3 = (s32[8,2,128]{2,1,0:T(2,128)}, s32[8,2,128]{2,1,0:T(2,128)S(1)}, u32[]{:S(2)}) copy-start(s32[8,2,128]{2,1,0:T(2,128)S(1)} %all-to-all-done.index_ref) | copy-start | bytes 24580
  14.4 8.5 %collective-permute-start = (bf16[256,768]{1,0:T(8,128)(2,1)}, bf16[256,768]{1,0:T(8,128)(2,1)S(1)}, u32[]{:S(2)}, u32[]{:S(2)}) collective-permute-start(bf16[256,768]{1,0:T(8,128)(2,1)} %get-tuple-element.28), channel_id=1, source_target_pairs={{0,1},{1,0},{2,3},{3,2},{4,5},{5,4},{6,7},{7,6},{8,9},{9,8},{10,11... | collective-permute-start | bytes 1179656 | tf_op jit(solution)/shard_map/ppermute | solution.py:584
  34.4 5.3 %collective-permute-start.2 = (bf16[8,3,48,768]{3,2,1,0:T(8,128)(2,1)}, bf16[8,3,48,768]{3,2,1,0:T(8,128)(2,1)S(1)}, u32[]{:S(2)}, u32[]{:S(2)}) collective-permute-start(bf16[8,3,48,768]{3,2,1,0:T(8,128)(2,1)} %get-tuple-element.34), channel_id=1, source_target_pairs={{0,1},{1,0},{2,3},{3,2},{4,5},{5,4},{6,7},{7,6},{8,9},{9,8},{10,11... | collective-permute-start | bytes 5308424 | tf_op jit(solution)/shard_map/ppermute | solution.py:588
  39.2 22.1 %collective-permute-start.3 = (bf16[1024,768]{1,0:T(8,128)(2,1)}, bf16[1024,768]{1,0:T(8,128)(2,1)}, u32[]{:S(2)}, u32[]{:S(2)}) collective-permute-start(bf16[1024,768]{1,0:T(8,128)(2,1)} %shard_map.125.after_ref.own_ref), channel_id=1, source_target_pairs={{0,1},{1,0},{2,3},{3,2},{4,5},{5,4},{6,7},{7,6},{8,9},{9,8},{10,11... | collective-permute-start | bytes 4718600 | tf_op jit(solution)/shard_map/ppermute | solution.py:593
  41.6 7.2 %copy-start.2 = (s32[1,16]{1,0:T(1,128)S(1)}, s32[1,16]{1,0:T(1,128)}, u32[]{:S(2)}) copy-start(s32[1,16]{1,0:T(1,128)} %param.19) | copy-start | bytes 196
  41.6 8.5 %copy-start = (bf16[8,3,48,768]{3,2,1,0:T(8,128)(2,1)S(1)}, bf16[8,3,48,768]{3,2,1,0:T(8,128)(2,1)}, u32[]{:S(2)}) copy-start(bf16[8,3,48,768]{3,2,1,0:T(8,128)(2,1)} %shard_map.126.after_ref) | copy-start | bytes 5308420
  41.6 31.2 %all-to-all-start.1 = ((bf16[8,3,48,768]{3,2,1,0:T(8,128)(2,1)}), bf16[8,3,48,768]{3,2,1,0:T(8,128)(2,1)S(1)}, u32[]{:S(2)}, u32[]{:S(2)}) async-start(bf16[8,3,48,768]{3,2,1,0:T(8,128)(2,1)} %shard_map.126.after_ref), calls=%async_computation.1 | async-start | bytes 3538944 | tf_op jit(solution)/shard_map/all_to_all | solution.py:591
  73.9 6.0 %copy-start.10 = (bf16[96,144]{1,0:T(8,128)(2,1)S(1)}, bf16[96,144]{1,0:T(8,128)(2,1)}, u32[]{:S(2)}) copy-start(bf16[96,144]{1,0:T(8,128)(2,1)} %get-tuple-element.39) | copy-start | bytes 82948
  73.9 7.9 %copy-start.9 = (bf16[96,144]{1,0:T(8,128)(2,1)S(1)}, bf16[96,144]{1,0:T(8,128)(2,1)}, u32[]{:S(2)}) copy-start(bf16[96,144]{1,0:T(8,128)(2,1)} %get-tuple-element.40) | copy-start | bytes 82948
  73.9 11.2 %copy-start.8 = (bf16[96,144]{1,0:T(8,128)(2,1)S(1)}, bf16[96,144]{1,0:T(8,128)(2,1)}, u32[]{:S(2)}) copy-start(bf16[96,144]{1,0:T(8,128)(2,1)} %get-tuple-element.41) | copy-start | bytes 82948
  73.9 15.3 %copy-start.7 = (bf16[96,144]{1,0:T(8,128)(2,1)S(1)}, bf16[96,144]{1,0:T(8,128)(2,1)}, u32[]{:S(2)}) copy-start(bf16[96,144]{1,0:T(8,128)(2,1)} %get-tuple-element.42) | copy-start | bytes 82948
  73.9 15.8 %copy-start.6 = (bf16[96,144]{1,0:T(8,128)(2,1)S(1)}, bf16[96,144]{1,0:T(8,128)(2,1)}, u32[]{:S(2)}) copy-start(bf16[96,144]{1,0:T(8,128)(2,1)} %get-tuple-element.43) | copy-start | bytes 82948
  74.0 20.7 %copy-start.5 = (bf16[96,144]{1,0:T(8,128)(2,1)S(1)}, bf16[96,144]{1,0:T(8,128)(2,1)}, u32[]{:S(2)}) copy-start(bf16[96,144]{1,0:T(8,128)(2,1)} %get-tuple-element.44) | copy-start | bytes 82948
  74.0 23.4 %copy-start.4 = (bf16[96,144]{1,0:T(8,128)(2,1)S(1)}, bf16[96,144]{1,0:T(8,128)(2,1)}, u32[]{:S(2)}) copy-start(bf16[96,144]{1,0:T(8,128)(2,1)} %get-tuple-element.45) | copy-start | bytes 82948
  74.0 27.5 %copy-start.1 = (f32[96,144]{1,0:T(8,128)S(1)}, f32[96,144]{1,0:T(8,128)}, u32[]{:S(2)}) copy-start(f32[96,144]{1,0:T(8,128)} %get-tuple-element.38.own_ref) | copy-start | bytes 165892
  74.0 35.2 %all-to-all-start.2 = ((bf16[8,3,64,768]{3,2,1,0:T(8,128)(2,1)}), bf16[8,3,64,768]{3,2,1,0:T(8,128)(2,1)S(1)}, u32[]{:S(2)}, u32[]{:S(2)}) async-start(bf16[8,3,64,768]{3,2,1,0:T(8,128)(2,1)} %shard_map.129), calls=%async_computation.2 | async-start | bytes 4718592 | tf_op jit(solution)/shard_map/all_to_all | solution.py:601
  80.0 14.7 %collective-permute-start.4 = (bf16[96,144]{1,0:T(8,128)(2,1)S(1)}, bf16[96,144]{1,0:T(8,128)(2,1)S(1)}, u32[]{:S(2)}, u32[]{:S(2)}) collective-permute-start(bf16[96,144]{1,0:T(8,128)(2,1)S(1)} %copy-done.10), channel_id=1, source_target_pairs={{0,32},{32,64},{64,96},{96,128},{128,160},{160,192},{192,224},{224... | collective-permute-start | bytes 82952 | tf_op jit(solution)/shard_map/ppermute | solution.py:546
  81.9 15.5 %collective-permute-start.5 = (bf16[96,144]{1,0:T(8,128)(2,1)S(1)}, bf16[96,144]{1,0:T(8,128)(2,1)S(1)}, u32[]{:S(2)}, u32[]{:S(2)}) collective-permute-start(bf16[96,144]{1,0:T(8,128)(2,1)S(1)} %copy-done.9), channel_id=1, source_target_pairs={{0,64},{32,96},{64,128},{96,160},{128,192},{160,224},{192,0},{224,... | collective-permute-start | bytes 82952 | tf_op jit(solution)/shard_map/ppermute | solution.py:546
  85.1 13.2 %collective-permute-start.6 = (bf16[96,144]{1,0:T(8,128)(2,1)S(1)}, bf16[96,144]{1,0:T(8,128)(2,1)S(1)}, u32[]{:S(2)}, u32[]{:S(2)}) collective-permute-start(bf16[96,144]{1,0:T(8,128)(2,1)S(1)} %copy-done.8), channel_id=1, source_target_pairs={{0,96},{32,128},{64,160},{96,192},{128,224},{160,0},{192,32},{224,... | collective-permute-start | bytes 82952 | tf_op jit(solution)/shard_map/ppermute | solution.py:546
  89.2 9.2 %collective-permute-start.7 = (bf16[96,144]{1,0:T(8,128)(2,1)S(1)}, bf16[96,144]{1,0:T(8,128)(2,1)S(1)}, u32[]{:S(2)}, u32[]{:S(2)}) collective-permute-start(bf16[96,144]{1,0:T(8,128)(2,1)S(1)} %copy-done.7), channel_id=1, source_target_pairs={{0,128},{32,160},{64,192},{96,224},{128,0},{160,32},{192,64},{224,... | collective-permute-start | bytes 82952 | tf_op jit(solution)/shard_map/ppermute | solution.py:546
  89.8 9.7 %collective-permute-start.8 = (bf16[96,144]{1,0:T(8,128)(2,1)S(1)}, bf16[96,144]{1,0:T(8,128)(2,1)S(1)}, u32[]{:S(2)}, u32[]{:S(2)}) collective-permute-start(bf16[96,144]{1,0:T(8,128)(2,1)S(1)} %copy-done.6), channel_id=1, source_target_pairs={{0,160},{32,192},{64,224},{96,0},{128,32},{160,64},{192,96},{224,1... | collective-permute-start | bytes 82952 | tf_op jit(solution)/shard_map/ppermute | solution.py:546
  94.7 6.1 %collective-permute-start.9 = (bf16[96,144]{1,0:T(8,128)(2,1)S(1)}, bf16[96,144]{1,0:T(8,128)(2,1)S(1)}, u32[]{:S(2)}, u32[]{:S(2)}) collective-permute-start(bf16[96,144]{1,0:T(8,128)(2,1)S(1)} %copy-done.5), channel_id=1, source_target_pairs={{0,192},{32,224},{64,0},{96,32},{128,64},{160,96},{192,128},{224,1... | collective-permute-start | bytes 82952 | tf_op jit(solution)/shard_map/ppermute | solution.py:546
  97.4 4.1 %collective-permute-start.10 = (bf16[96,144]{1,0:T(8,128)(2,1)S(1)}, bf16[96,144]{1,0:T(8,128)(2,1)S(1)}, u32[]{:S(2)}, u32[]{:S(2)}) collective-permute-start(bf16[96,144]{1,0:T(8,128)(2,1)S(1)} %copy-done.4), channel_id=1, source_target_pairs={{0,224},{32,0},{64,32},{96,64},{128,96},{160,128},{192,160},{224,1... | collective-permute-start | bytes 82952 | tf_op jit(solution)/shard_map/ppermute | solution.py:546
  101.5 5.5 %collective-permute-start.11 = (bf16[48,144]{1,0:T(8,128)(2,1)S(1)}, bf16[48,144]{1,0:T(8,128)(2,1)S(1)}, u32[]{:S(2)}, u32[]{:S(2)}) collective-permute-start(bf16[48,144]{1,0:T(8,128)(2,1)S(1)} %get-tuple-element.47), channel_id=1, source_target_pairs={{0,16},{16,0},{1,17},{17,1},{2,18},{18,2},{3,19},{19,3},{4,20},{20... | collective-permute-start | bytes 41480 | tf_op jit(solution)/shard_map/ppermute | solution.py:550

commit v6 on v5

--- a/solution.py
+++ b/solution.py
@@ -316,14 +316,14 @@
 
 def join(kept, got, after):
     groups, taps, rows, width = kept.shape
-    block = pl.BlockSpec((groups // 4, taps, rows, width), lambda i: (i, 0, 0, 0))
+    block = pl.BlockSpec((groups // 2, taps, rows, width), lambda i: (i, 0, 0, 0))
     return pl.pallas_call(
         join_kernel,
-        grid=(4,),
+        grid=(2,),
         in_specs=[block, block, pl.BlockSpec(memory_space=pl.ANY)],
         out_specs=block,
         out_shape=pltpu.HBM(kept.shape, BF16),
-        compiler_params=params(8),
+        compiler_params=params(12),
         cost_estimate=cost(kept.size, 6 * kept.size),
     )(kept, got, in_hbm(after))
 

time: 115 us -> 114 us (level)
  no operation moved by 1% of the time
where the time goes in v6:
time: 114 us; the launch traced here: 112 us
  Pallas kernels  52.4 us (46%)
  starting transfers between devices  43.2 us (38%)
  waiting for transfers between devices  14.6 us (13%)
  between operations  1.41 us (1%)
    ppermute x7, starting transfers between devices, dp_sum(): lax.ppermute(outs[step], 'z', [(i, (i + step) % nz) for i in range(nz)])  18.4 us
    pallas_call x1, Pallas kernels, edges_and_grad(): pl.pallas_call(functools.partial(edge_kernel, rows=rows), grid_spec=pltpu...  11.5 us
    pallas_call x2, Pallas kernels, projected(): pl.pallas_call(table_kernel, grid=(width // TILE,), in_specs=[pl.BlockSpe...  9.36 us
    all_to_all x1, starting transfers between devices, on_device(): lax.all_to_all(accept_pos.reshape(chips, 2, -1), CHIPS, 0, 0, tiled=True)  7.47 us
    pallas_call x1, Pallas kernels, conv_inner(): pl.pallas_call(functools.partial(inner_kernel, rows=rows), grid=(width //...  7.43 us
    all_to_all x1, starting transfers between devices, on_device(): pieces = lax.all_to_all(chip_half, CHIPS, 0, 0, tiled=True)  7.05 us
    pallas_call x1, Pallas kernels, serve(): pl.pallas_call(serve_kernel, grid_spec=pltpu.PrefetchScalarGridSpec(num_s...  6.69 us
    pallas_call x1, Pallas kernels, donor_rows(): pl.pallas_call(donor_kernel, grid=(count // per,), in_specs=[pl.BlockSpec...  6.53 us
  transfers between devices with their start and end apart: 15, of which 7 were waited for; matrix products, arithmetic and copies ran while one was open for 1% of the time, Pallas kernels for 32%

profile of v6, /device:TPU:2, one launch (start us, length us, event | category | flops | bytes accessed | tf_op | source)
XLA Modules:
  0.0 112.3 jit_solution(5049361892884788816)
XLA Ops:
  0.6 7.5 %all-to-all-start = ((s32[8,2,128]{2,1,0:T(2,128)}), s32[8,2,128]{2,1,0:T(2,128)S(1)}, u32[]{:S(2)}, u32[]{:S(2)}) async-start(s32[8,2,128]{2,1,0:T(2,128)} %bitcast.31), calls=%async_computation | async-start | bytes 16384 | tf_op jit(solution)/shard_map/all_to_all | solution.py:579
  8.1 3.7 %shard_map.122 = (bf16[1024,768]{1,0:T(8,128)(2,1)}, bf16[256,768]{1,0:T(8,128)(2,1)}, bf16[256,768]{1,0:T(8,128)(2,1)}) custom-call(s32[1]{0:T(128)} %bitcast.core_ref, bf16[1024,768]{1,0:T(8,128)(2,1)} %bitcast.15, s32[8,128]{1,0:T(8,128)} %bitcast.28, f32[4,768]{1,0:T(4,128)} %table_ref.5, f32[768]{0:T(1024)} %gain_ref.1), custom_call_target="tpu_custom_call" | custom-call | flops 7864320 | bytes 3145728 | tf_op jit(solution)/shard_map/pallas_call | solution.py:85
  11.8 1.9 %collective-permute-start.1 = (bf16[256,768]{1,0:T(8,128)(2,1)}, bf16[256,768]{1,0:T(8,128)(2,1)S(1)}, u32[]{:S(2)}, u32[]{:S(2)}) collective-permute-start(bf16[256,768]{1,0:T(8,128)(2,1)} %get-tuple-element.29), channel_id=1, source_target_pairs={{1,2},{3,4},{5,6},{7,8},{9,10},{11,12},{13,14},{2,1},{4,3},{6,5},{... | collective-permute-start | bytes 1179656 | tf_op jit(solution)/shard_map/ppermute | solution.py:582
  13.8 0.6 all-to-all-done.index_ref
  14.4 0.0 copy-start.3
  14.4 1.1 collective-permute-start
  15.4 7.4 %shard_map.123 = (bf16[512,768]{1,0:T(8,128)(2,1)}, bf16[512,768]{1,0:T(8,128)(2,1)}, bf16[8,2,48,1024]{3,2,1,0:T(8,128)(2,1)}) custom-call(bf16[1024,768]{1,0:T(8,128)(2,1)} %get-tuple-element.25.n_ref, bf16[3,768,768]{2,1,0:T(8,128)(2,1)} %bitcast.24, bf16[4,256,768]{2,1,0:T(8,128)(2,1)} %bitcast.16, bf16[4,256,768]{2,1,0:T(8,128)(2,1)} %bitcast.17, ...), custom_call_target="tpu_custom_call" | custom-call | flops 1811939328 | bytes 6291456 | tf_op jit(solution)/shard_map/pallas_call | solution.py:167
  22.9 0.0 copy-done.3
  22.9 0.0 collective-permute-done.1.far_ref
  22.9 0.0 collective-permute-done.near_ref
  22.9 11.5 %shard_map.124 = (bf16[512,768]{1,0:T(8,128)(2,1)}, bf16[8,3,48,768]{3,2,1,0:T(8,128)(2,1)}, bf16[8,3,48,768]{3,2,1,0:T(8,128)(2,1)S(1)}) custom-call(s32[1]{0:T(128)} %bitcast.core_ref, bf16[256,768]{1,0:T(8,128)(2,1)S(1)} %collective-permute-done.near_ref, bf16[256,768]{1,0:T(8,128)(2,1)S(1)} %collective-permute-done.1.far_ref, ...), custom_call_target="tpu_custom_call" | custom-call | flops 5435817984 | bytes 15728640 | tf_op jit(solution)/shard_map/pallas_call | solution.py:246
  34.4 0.1 collective-permute-start.2
  34.5 4.7 %shard_map.125.after_ref.own_ref = bf16[1024,768]{1,0:T(8,128)(2,1)} custom-call(bf16[512,768]{1,0:T(8,128)(2,1)} %get-tuple-element.26.inner_ref, bf16[512,768]{1,0:T(8,128)(2,1)} %get-tuple-element.32.outer_ref, bf16[768,768]{1,0:T(8,128)(2,1)} %weight_ref.2, bf16[8,3,48,768]{3,2,1,0:T(8,128)(2,1)S(1)} %get-tuple-element.33.after_ref.kept_ref), custom_call_target="tpu_custom_call" | custom-call | flops 1207959552 | bytes 3145728 | tf_op jit(solution)/shard_map/pallas_call | solution.py:290
  39.2 0.5 collective-permute-start.3
  39.7 0.0 collective-permute-done.2.got_ref
  39.7 1.4 %shard_map.126.after_ref = bf16[8,3,48,768]{3,2,1,0:T(8,128)(2,1)} custom-call(bf16[8,3,48,768]{3,2,1,0:T(8,128)(2,1)S(1)} %get-tuple-element.33.after_ref.kept_ref, bf16[8,3,48,768]{3,2,1,0:T(8,128)(2,1)S(1)} %collective-permute-done.2.got_ref, bf16[1024,768]{1,0:T(8,128)(2,1)} %shard_map.125.after_ref.own_ref), custom_call_target="tpu_custom_call" | custom-call | flops 884736 | bytes 5308416 | tf_op jit(solution)/shard_map/pallas_call | solution.py:320
  41.1 0.0 copy-start.2
  41.1 0.0 copy-start
  41.1 7.0 %all-to-all-start.1 = ((bf16[8,3,48,768]{3,2,1,0:T(8,128)(2,1)}), bf16[8,3,48,768]{3,2,1,0:T(8,128)(2,1)S(1)}, u32[]{:S(2)}, u32[]{:S(2)}) async-start(bf16[8,3,48,768]{3,2,1,0:T(8,128)(2,1)} %shard_map.126.after_ref), calls=%async_computation.1 | async-start | bytes 3538944 | tf_op jit(solution)/shard_map/all_to_all | solution.py:591
  48.2 0.0 copy-done.2
  48.2 0.6 fusion
  49.4 0.0 copy-done
  49.4 4.7 %shard_map.127.table_ref = bf16[1024,768]{1,0:T(8,128)(2,1)} custom-call(bf16[512,768]{1,0:T(8,128)(2,1)} %get-tuple-element.26.inner_ref, bf16[512,768]{1,0:T(8,128)(2,1)} %get-tuple-element.32.outer_ref, bf16[768,768]{1,0:T(8,128)(2,1)} %weight_ref.3, bf16[8,3,48,768]{3,2,1,0:T(8,128)(2,1)S(1)} %copy-done), custom_call_target="tpu_custom_call" | custom-call | flops 1207959552 | bytes 3145728 | tf_op jit(solution)/shard_map/pallas_call | solution.py:290
  54.1 6.5 %shard_map.128.after_ref.donor_ref = bf16[2048,768]{1,0:T(8,128)(2,1)} custom-call(s32[16,128]{1,0:T(8,128)} %bitcast.32, bf16[1024,768]{1,0:T(8,128)(2,1)} %shard_map.127.table_ref, bf16[8,3,48,768]{3,2,1,0:T(8,128)(2,1)} %shard_map.126.after_ref), custom_call_target="tpu_custom_call" | custom-call | flops 3221225472 | bytes 7864320 | tf_op jit(solution)/shard_map/pallas_call | solution.py:409
  60.6 0.0 collective-permute-done.3.other_ref
  60.6 6.7 %shard_map.129 = bf16[8,3,64,768]{3,2,1,0:T(8,128)(2,1)} custom-call(s32[1]{0:T(128)} %bitcast.core_ref, s32[1]{0:T(128)} %bitcast.9.hot_ref, s32[8,2,128]{2,1,0:T(2,128)} %copy-done.3, bf16[1024,768]{1,0:T(8,128)(2,1)} %shard_map.125.after_ref.own_ref, bf16[1024,768]{1,0:T(8,128)(2,1)} %collective-permute-done.3.other_ref, ...), custom_call_target="tpu_custom_call" | custom-call | flops 3221225472 | bytes 6291456 | tf_op jit(solution)/shard_map/pallas_call | solution.py:378
  67.3 4.8 %all-to-all-done.1.pieces_ref = bf16[8,3,48,768]{3,2,1,0:T(8,128)(2,1)S(1)} async-done(((bf16[8,3,48,768]{3,2,1,0:T(8,128)(2,1)}), bf16[8,3,48,768]{3,2,1,0:T(8,128)(2,1)S(1)}, u32[]{:S(2)}, u32[]{:S(2)}) %all-to-all-start.1) | async-done | bytes 1769504 | tf_op jit(solution)/shard_map/all_to_all | solution.py:591
  72.1 1.1 %shard_map.130 = (f32[96,144]{1,0:T(8,128)}, bf16[96,144]{1,0:T(8,128)(2,1)}, bf16[96,144]{1,0:T(8,128)(2,1)}, bf16[96,144]{1,0:T(8,128)(2,1)}, bf16[96,144]{1,0...) custom-call(s32[1]{0:T(128)} %bitcast.10.z_ref, ...), custom_call_target="tpu_custom_call" | custom-call | flops 1769472 | bytes 2654208 | tf_op jit(solution)/shard_map/pallas_call | solution.py:477
  73.3 0.0 copy-start.10
  73.3 0.0 copy-start.9
  73.3 0.0 copy-start.7
  73.3 0.0 copy-start.6
  73.3 0.0 copy-start.5
  73.3 0.0 copy-start.4
  73.3 0.0 copy-start.1
  73.3 6.0 %all-to-all-start.2 = ((bf16[8,3,64,768]{3,2,1,0:T(8,128)(2,1)}), bf16[8,3,64,768]{3,2,1,0:T(8,128)(2,1)S(1)}, u32[]{:S(2)}, u32[]{:S(2)}) async-start(bf16[8,3,64,768]{3,2,1,0:T(8,128)(2,1)} %shard_map.129), calls=%async_computation.2 | async-start | bytes 4718592 | tf_op jit(solution)/shard_map/all_to_all | solution.py:601
  79.3 0.0 copy-done.10
  79.3 1.9 %collective-permute-start.4 = (bf16[96,144]{1,0:T(8,128)(2,1)S(1)}, bf16[96,144]{1,0:T(8,128)(2,1)S(1)}, u32[]{:S(2)}, u32[]{:S(2)}) collective-permute-start(bf16[96,144]{1,0:T(8,128)(2,1)S(1)} %copy-done.10), channel_id=1, source_target_pairs={{0,32},{32,64},{64,96},{96,128},{128,160},{160,192},{192,224},{224... | collective-permute-start | bytes 82952 | tf_op jit(solution)/shard_map/ppermute | solution.py:546
  81.2 0.0 copy-done.9
  81.2 3.3 %collective-permute-start.5 = (bf16[96,144]{1,0:T(8,128)(2,1)S(1)}, bf16[96,144]{1,0:T(8,128)(2,1)S(1)}, u32[]{:S(2)}, u32[]{:S(2)}) collective-permute-start(bf16[96,144]{1,0:T(8,128)(2,1)S(1)} %copy-done.9), channel_id=1, source_target_pairs={{0,64},{32,96},{64,128},{96,160},{128,192},{160,224},{192,0},{224,... | collective-permute-start | bytes 82952 | tf_op jit(solution)/shard_map/ppermute | solution.py:546
  84.5 0.0 copy-done.8
  84.5 4.0 %collective-permute-start.6 = (bf16[96,144]{1,0:T(8,128)(2,1)S(1)}, bf16[96,144]{1,0:T(8,128)(2,1)S(1)}, u32[]{:S(2)}, u32[]{:S(2)}) collective-permute-start(bf16[96,144]{1,0:T(8,128)(2,1)S(1)} %copy-done.8), channel_id=1, source_target_pairs={{0,96},{32,128},{64,160},{96,192},{128,224},{160,0},{192,32},{224,... | collective-permute-start | bytes 82952 | tf_op jit(solution)/shard_map/ppermute | solution.py:546
  88.5 0.0 copy-done.7
  88.5 0.6 collective-permute-start.7
  89.1 0.0 copy-done.6
  89.1 4.9 %collective-permute-start.8 = (bf16[96,144]{1,0:T(8,128)(2,1)S(1)}, bf16[96,144]{1,0:T(8,128)(2,1)S(1)}, u32[]{:S(2)}, u32[]{:S(2)}) collective-permute-start(bf16[96,144]{1,0:T(8,128)(2,1)S(1)} %copy-done.6), channel_id=1, source_target_pairs={{0,160},{32,192},{64,224},{96,0},{128,32},{160,64},{192,96},{224,1... | collective-permute-start | bytes 82952 | tf_op jit(solution)/shard_map/ppermute | solution.py:546
  94.0 0.0 collective-permute-done.4.refs_0_
  94.0 0.0 copy-done.5
  94.0 2.6 %collective-permute-start.9 = (bf16[96,144]{1,0:T(8,128)(2,1)S(1)}, bf16[96,144]{1,0:T(8,128)(2,1)S(1)}, u32[]{:S(2)}, u32[]{:S(2)}) collective-permute-start(bf16[96,144]{1,0:T(8,128)(2,1)S(1)} %copy-done.5), channel_id=1, source_target_pairs={{0,192},{32,224},{64,0},{96,32},{128,64},{160,96},{192,128},{224,1... | collective-permute-start | bytes 82952 | tf_op jit(solution)/shard_map/ppermute | solution.py:546
  96.7 0.0 collective-permute-done.5.refs_1_
  96.7 0.0 copy-done.4
  96.7 1.0 collective-permute-start.10
  97.7 0.0 collective-permute-done.6.refs_2_
  97.7 0.0 collective-permute-done.7.refs_3_
  97.7 1.1 collective-permute-done.8.refs_4_
  98.8 1.3 %collective-permute-done.9.refs_5_ = bf16[96,144]{1,0:T(8,128)(2,1)S(1)} collective-permute-done((bf16[96,144]{1,0:T(8,128)(2,1)S(1)}, bf16[96,144]{1,0:T(8,128)(2,1)S(1)}, u32[]{:S(2)}, u32[]{:S(2)}) %collective-permute-start.9) | collective-permute-done | bytes 27680 | tf_op jit(solution)/shard_map/ppermute | solution.py:546
  100.1 0.7 collective-permute-done.10.refs_6_
  100.8 0.0 copy-done.1
  100.8 0.1 shard_map.132
  100.8 0.8 collective-permute-start.11
  101.6 4.8 %collective-permute-done.11.got_ref = bf16[48,144]{1,0:T(8,128)(2,1)S(1)} collective-permute-done((bf16[48,144]{1,0:T(8,128)(2,1)S(1)}, bf16[48,144]{1,0:T(8,128)(2,1)S(1)}, u32[]{:S(2)}, u32[]{:S(2)}) %collective-permute-start.11) | collective-permute-done | bytes 13856 | tf_op jit(solution)/shard_map/ppermute | solution.py:550
  106.4 0.7 shard_map.133
  107.1 1.4 %all-to-all-done.2.accepted_ref = bf16[8,3,64,768]{3,2,1,0:T(8,128)(2,1)S(1)} async-done(((bf16[8,3,64,768]{3,2,1,0:T(8,128)(2,1)}), bf16[8,3,64,768]{3,2,1,0:T(8,128)(2,1)S(1)}, u32[]{:S(2)}, u32[]{:S(2)}) %all-to-all-start.2) | async-done | bytes 2359328 | tf_op jit(solution)/shard_map/all_to_all | solution.py:601
  108.5 3.8 %shard_map.131 = bf16[2048,768]{1,0:T(8,128)(2,1)} custom-call(s32[1]{0:T(128)} %bitcast.core_ref, s32[16]{0:T(128)S(1)} %bitcast.14, bf16[2048,768]{1,0:T(8,128)(2,1)} %shard_map.128.after_ref.donor_ref, bf16[8,3,64,768]{3,2,1,0:T(8,128)(2,1)S(1)} %all-to-all-done.2.accepted_ref), custom_call_target="tpu_custom_call" | custom-call | flops 3145728 | bytes 9437184 | tf_op jit(solution)/shard_map/pallas_call | solution.py:446
  (1 shorter events, 0.0 us)
Async XLA Ops:
  0.6 13.7 %all-to-all-start = ((s32[8,2,128]{2,1,0:T(2,128)}), s32[8,2,128]{2,1,0:T(2,128)S(1)}, u32[]{:S(2)}, u32[]{:S(2)}) async-start(s32[8,2,128]{2,1,0:T(2,128)} %bitcast.31), calls=%async_computation | async-start | bytes 16384 | tf_op jit(solution)/shard_map/all_to_all | solution.py:579
  11.8 11.0 %collective-permute-start.1 = (bf16[256,768]{1,0:T(8,128)(2,1)}, bf16[256,768]{1,0:T(8,128)(2,1)S(1)}, u32[]{:S(2)}, u32[]{:S(2)}) collective-permute-start(bf16[256,768]{1,0:T(8,128)(2,1)} %get-tuple-element.29), channel_id=1, source_target_pairs={{1,2},{3,4},{5,6},{7,8},{9,10},{11,12},{13,14},{2,1},{4,3},{6,5},{... | collective-permute-start | bytes 1179656 | tf_op jit(solution)/shard_map/ppermute | solution.py:582
  14.4 8.5 %copy-start.3 = (s32[8,2,128]{2,1,0:T(2,128)}, s32[8,2,128]{2,1,0:T(2,128)S(1)}, u32[]{:S(2)}) copy-start(s32[8,2,128]{2,1,0:T(2,128)S(1)} %all-to-all-done.index_ref) | copy-start | bytes 24580
  14.4 8.5 %collective-permute-start = (bf16[256,768]{1,0:T(8,128)(2,1)}, bf16[256,768]{1,0:T(8,128)(2,1)S(1)}, u32[]{:S(2)}, u32[]{:S(2)}) collective-permute-start(bf16[256,768]{1,0:T(8,128)(2,1)} %get-tuple-element.28), channel_id=1, source_target_pairs={{0,1},{1,0},{2,3},{3,2},{4,5},{5,4},{6,7},{7,6},{8,9},{9,8},{10,11... | collective-permute-start | bytes 1179656 | tf_op jit(solution)/shard_map/ppermute | solution.py:584
  34.4 5.3 %collective-permute-start.2 = (bf16[8,3,48,768]{3,2,1,0:T(8,128)(2,1)}, bf16[8,3,48,768]{3,2,1,0:T(8,128)(2,1)S(1)}, u32[]{:S(2)}, u32[]{:S(2)}) collective-permute-start(bf16[8,3,48,768]{3,2,1,0:T(8,128)(2,1)} %get-tuple-element.34), channel_id=1, source_target_pairs={{0,1},{1,0},{2,3},{3,2},{4,5},{5,4},{6,7},{7,6},{8,9},{9,8},{10,11... | collective-permute-start | bytes 5308424 | tf_op jit(solution)/shard_map/ppermute | solution.py:588
  39.2 21.4 %collective-permute-start.3 = (bf16[1024,768]{1,0:T(8,128)(2,1)}, bf16[1024,768]{1,0:T(8,128)(2,1)}, u32[]{:S(2)}, u32[]{:S(2)}) collective-permute-start(bf16[1024,768]{1,0:T(8,128)(2,1)} %shard_map.125.after_ref.own_ref), channel_id=1, source_target_pairs={{0,1},{1,0},{2,3},{3,2},{4,5},{5,4},{6,7},{7,6},{8,9},{9,8},{10,11... | collective-permute-start | bytes 4718600 | tf_op jit(solution)/shard_map/ppermute | solution.py:593
  41.1 7.1 %copy-start.2 = (s32[1,16]{1,0:T(1,128)S(1)}, s32[1,16]{1,0:T(1,128)}, u32[]{:S(2)}) copy-start(s32[1,16]{1,0:T(1,128)} %param.19) | copy-start | bytes 196
  41.1 8.3 %copy-start = (bf16[8,3,48,768]{3,2,1,0:T(8,128)(2,1)S(1)}, bf16[8,3,48,768]{3,2,1,0:T(8,128)(2,1)}, u32[]{:S(2)}) copy-start(bf16[8,3,48,768]{3,2,1,0:T(8,128)(2,1)} %shard_map.126.after_ref) | copy-start | bytes 5308420
  41.1 31.0 %all-to-all-start.1 = ((bf16[8,3,48,768]{3,2,1,0:T(8,128)(2,1)}), bf16[8,3,48,768]{3,2,1,0:T(8,128)(2,1)S(1)}, u32[]{:S(2)}, u32[]{:S(2)}) async-start(bf16[8,3,48,768]{3,2,1,0:T(8,128)(2,1)} %shard_map.126.after_ref), calls=%async_computation.1 | async-start | bytes 3538944 | tf_op jit(solution)/shard_map/all_to_all | solution.py:591
  73.3 6.0 %copy-start.10 = (bf16[96,144]{1,0:T(8,128)(2,1)S(1)}, bf16[96,144]{1,0:T(8,128)(2,1)}, u32[]{:S(2)}) copy-start(bf16[96,144]{1,0:T(8,128)(2,1)} %get-tuple-element.39) | copy-start | bytes 82948
  73.3 7.9 %copy-start.9 = (bf16[96,144]{1,0:T(8,128)(2,1)S(1)}, bf16[96,144]{1,0:T(8,128)(2,1)}, u32[]{:S(2)}) copy-start(bf16[96,144]{1,0:T(8,128)(2,1)} %get-tuple-element.40) | copy-start | bytes 82948
  73.3 11.2 %copy-start.8 = (bf16[96,144]{1,0:T(8,128)(2,1)S(1)}, bf16[96,144]{1,0:T(8,128)(2,1)}, u32[]{:S(2)}) copy-start(bf16[96,144]{1,0:T(8,128)(2,1)} %get-tuple-element.41) | copy-start | bytes 82948
  73.3 15.3 %copy-start.7 = (bf16[96,144]{1,0:T(8,128)(2,1)S(1)}, bf16[96,144]{1,0:T(8,128)(2,1)}, u32[]{:S(2)}) copy-start(bf16[96,144]{1,0:T(8,128)(2,1)} %get-tuple-element.42) | copy-start | bytes 82948
  73.3 15.8 %copy-start.6 = (bf16[96,144]{1,0:T(8,128)(2,1)S(1)}, bf16[96,144]{1,0:T(8,128)(2,1)}, u32[]{:S(2)}) copy-start(bf16[96,144]{1,0:T(8,128)(2,1)} %get-tuple-element.43) | copy-start | bytes 82948
  73.3 20.7 %copy-start.5 = (bf16[96,144]{1,0:T(8,128)(2,1)S(1)}, bf16[96,144]{1,0:T(8,128)(2,1)}, u32[]{:S(2)}) copy-start(bf16[96,144]{1,0:T(8,128)(2,1)} %get-tuple-element.44) | copy-start | bytes 82948
  73.3 23.4 %copy-start.4 = (bf16[96,144]{1,0:T(8,128)(2,1)S(1)}, bf16[96,144]{1,0:T(8,128)(2,1)}, u32[]{:S(2)}) copy-start(bf16[96,144]{1,0:T(8,128)(2,1)} %get-tuple-element.45) | copy-start | bytes 82948
  73.3 27.5 %copy-start.1 = (f32[96,144]{1,0:T(8,128)S(1)}, f32[96,144]{1,0:T(8,128)}, u32[]{:S(2)}) copy-start(f32[96,144]{1,0:T(8,128)} %get-tuple-element.38.own_ref) | copy-start | bytes 165892
  73.3 35.2 %all-to-all-start.2 = ((bf16[8,3,64,768]{3,2,1,0:T(8,128)(2,1)}), bf16[8,3,64,768]{3,2,1,0:T(8,128)(2,1)S(1)}, u32[]{:S(2)}, u32[]{:S(2)}) async-start(bf16[8,3,64,768]{3,2,1,0:T(8,128)(2,1)} %shard_map.129), calls=%async_computation.2 | async-start | bytes 4718592 | tf_op jit(solution)/shard_map/all_to_all | solution.py:601
  79.3 14.7 %collective-permute-start.4 = (bf16[96,144]{1,0:T(8,128)(2,1)S(1)}, bf16[96,144]{1,0:T(8,128)(2,1)S(1)}, u32[]{:S(2)}, u32[]{:S(2)}) collective-permute-start(bf16[96,144]{1,0:T(8,128)(2,1)S(1)} %copy-done.10), channel_id=1, source_target_pairs={{0,32},{32,64},{64,96},{96,128},{128,160},{160,192},{192,224},{224... | collective-permute-start | bytes 82952 | tf_op jit(solution)/shard_map/ppermute | solution.py:546
  81.2 15.5 %collective-permute-start.5 = (bf16[96,144]{1,0:T(8,128)(2,1)S(1)}, bf16[96,144]{1,0:T(8,128)(2,1)S(1)}, u32[]{:S(2)}, u32[]{:S(2)}) collective-permute-start(bf16[96,144]{1,0:T(8,128)(2,1)S(1)} %copy-done.9), channel_id=1, source_target_pairs={{0,64},{32,96},{64,128},{96,160},{128,192},{160,224},{192,0},{224,... | collective-permute-start | bytes 82952 | tf_op jit(solution)/shard_map/ppermute | solution.py:546
  84.5 13.2 %collective-permute-start.6 = (bf16[96,144]{1,0:T(8,128)(2,1)S(1)}, bf16[96,144]{1,0:T(8,128)(2,1)S(1)}, u32[]{:S(2)}, u32[]{:S(2)}) collective-permute-start(bf16[96,144]{1,0:T(8,128)(2,1)S(1)} %copy-done.8), channel_id=1, source_target_pairs={{0,96},{32,128},{64,160},{96,192},{128,224},{160,0},{192,32},{224,... | collective-permute-start | bytes 82952 | tf_op jit(solution)/shard_map/ppermute | solution.py:546
  88.5 9.2 %collective-permute-start.7 = (bf16[96,144]{1,0:T(8,128)(2,1)S(1)}, bf16[96,144]{1,0:T(8,128)(2,1)S(1)}, u32[]{:S(2)}, u32[]{:S(2)}) collective-permute-start(bf16[96,144]{1,0:T(8,128)(2,1)S(1)} %copy-done.7), channel_id=1, source_target_pairs={{0,128},{32,160},{64,192},{96,224},{128,0},{160,32},{192,64},{224,... | collective-permute-start | bytes 82952 | tf_op jit(solution)/shard_map/ppermute | solution.py:546
  89.1 9.7 %collective-permute-start.8 = (bf16[96,144]{1,0:T(8,128)(2,1)S(1)}, bf16[96,144]{1,0:T(8,128)(2,1)S(1)}, u32[]{:S(2)}, u32[]{:S(2)}) collective-permute-start(bf16[96,144]{1,0:T(8,128)(2,1)S(1)} %copy-done.6), channel_id=1, source_target_pairs={{0,160},{32,192},{64,224},{96,0},{128,32},{160,64},{192,96},{224,1... | collective-permute-start | bytes 82952 | tf_op jit(solution)/shard_map/ppermute | solution.py:546
  94.0 6.1 %collective-permute-start.9 = (bf16[96,144]{1,0:T(8,128)(2,1)S(1)}, bf16[96,144]{1,0:T(8,128)(2,1)S(1)}, u32[]{:S(2)}, u32[]{:S(2)}) collective-permute-start(bf16[96,144]{1,0:T(8,128)(2,1)S(1)} %copy-done.5), channel_id=1, source_target_pairs={{0,192},{32,224},{64,0},{96,32},{128,64},{160,96},{192,128},{224,1... | collective-permute-start | bytes 82952 | tf_op jit(solution)/shard_map/ppermute | solution.py:546
  96.7 4.1 %collective-permute-start.10 = (bf16[96,144]{1,0:T(8,128)(2,1)S(1)}, bf16[96,144]{1,0:T(8,128)(2,1)S(1)}, u32[]{:S(2)}, u32[]{:S(2)}) collective-permute-start(bf16[96,144]{1,0:T(8,128)(2,1)S(1)} %copy-done.4), channel_id=1, source_target_pairs={{0,224},{32,0},{64,32},{96,64},{128,96},{160,128},{192,160},{224,1... | collective-permute-start | bytes 82952 | tf_op jit(solution)/shard_map/ppermute | solution.py:546
  100.8 5.5 %collective-permute-start.11 = (bf16[48,144]{1,0:T(8,128)(2,1)S(1)}, bf16[48,144]{1,0:T(8,128)(2,1)S(1)}, u32[]{:S(2)}, u32[]{:S(2)}) collective-permute-start(bf16[48,144]{1,0:T(8,128)(2,1)S(1)} %get-tuple-element.47), channel_id=1, source_target_pairs={{0,16},{16,0},{1,17},{17,1},{2,18},{18,2},{3,19},{19,3},{4,20},{20... | collective-permute-start | bytes 41480 | tf_op jit(solution)/shard_map/ppermute | solution.py:550
